TPU v7x, 32 devices: a whole 2x2x4 slice. The times are simulated.
32 devices in a mesh: rep: 8 (over y, x, core), shard: 4 (over z).
Axes of the slice: x: 2, y: 2, z: 4, core: 2. Of those that a mesh axis runs over, the one named last changes fastest.
Arguments:
- tokens: bfloat16 [16, 1024, 768], P('rep', 'shard'), may hold values from -6 to 6
- gain_attn: bfloat16 [768], P('shard'), may hold values from 0.25 to 1.75
- bias_attn: bfloat16 [768], P('shard'), may hold values from -1.5 to 1.5
- w_qkv: bfloat16 [768, 2304], P('shard'), may hold values from -0.21875 to 0.21875
- w_feature: bfloat16 [768, 128], P('shard'), may hold values from -1.5 to 1.5
- w_out: bfloat16 [768, 768], P('shard'), may hold values from -0.875 to 0.875
- gain_mlp: bfloat16 [768], P('shard'), may hold values from 0.25 to 1.75
- bias_mlp: bfloat16 [768], P('shard'), may hold values from -1.5 to 1.5
- w_up: bfloat16 [768, 3072], P('shard'), may hold values from -0.21875 to 0.21875
- w_down: bfloat16 [3072, 768], P('shard'), may hold values from -0.109375 to 0.109375
- cotangent: bfloat16 [16, 1024, 768], P('rep', 'shard'), may hold values from -6 to 6
Outputs:
- block_out: bfloat16 [16, 1024, 768], P('rep', 'shard')
- grad_tokens: bfloat16 [16, 1024, 768], P('rep', 'shard')
- grad_gain_attn: float32 [768], P('shard')
- grad_bias_attn: float32 [768], P('shard')
- grad_w_qkv: float32 [768, 2304], P('shard')
- grad_w_feature: float32 [768, 128], P('shard')
- grad_w_out: float32 [768, 768], P('shard')
- grad_gain_mlp: float32 [768], P('shard')
- grad_bias_mlp: float32 [768], P('shard')
- grad_w_up: float32 [768, 3072], P('shard')
- grad_w_down: float32 [3072, 768], P('shard')
All inputs are finite; a program needn't handle non-finite values.
Results may differ from a plain program's by a relative error of at most 0.019.
Values may be sent and summed in bfloat16 or wider, within the bound.
No kernel may reach another device: no remote copies, remote signals or barrier semaphores. Data moves between devices by JAX's collectives and lax.ppermute only.
A program may use at most 192 MiB of HBM per device.

v0:
```python
import jax
import jax.numpy as jnp
from jax import lax
from jax.experimental import pallas as pl
from jax.experimental.pallas import tpu as pltpu
from jax.sharding import PartitionSpec as P

D = 768
HEADS = 12
HEAD = 64
FEAT = 128
PAIRS = HEADS // 2
GROUP = 4 * HEAD
PIECES = 8
CHUNK = 4 * D // PIECES
QKV_BLOCKS = 3 * D // CHUNK
SLAB = (PAIRS + 1) * FEAT

norm_epsilon = 1e-05
low_type = jnp.bfloat16
wide_type = jnp.float32


def flip(value, bit):
    count = lax.axis_size("rep")
    return lax.ppermute(value, "rep", [(i, i ^ bit) for i in range(count)])


def spin(value, step):
    count = lax.axis_size("shard")
    return lax.ppermute(value, "shard", [(i, (i + step) % count) for i in range(count)])


def slide(value, step):
    count = lax.axis_size("shard")
    pairs = [(i, i + step) for i in range(count) if 0 <= i + step < count]
    return lax.ppermute(value, "shard", pairs)


def wide(value):
    return value.astype(wide_type)


def low(value):
    return value.astype(low_type)


def place_kernel(slots, *refs):
    parts, full = refs[:-1], refs[-1]
    for i, part in enumerate(parts):
        size = part.shape[0]
        full[pl.ds(slots[i] * size, size)] = part[...]


def place_parts(parts, slots):
    shape = (len(parts) * parts[0].shape[0],) + parts[0].shape[1:]
    slots = jnp.stack([jnp.asarray(slot, jnp.int32) for slot in slots])
    return call(place_kernel, 1, whole(shape, parts[0].dtype), scalar_first(len(parts)))(
        slots, *parts
    )


def around_parts(part):
    count, here = lax.axis_size("shard"), lax.axis_index("shard")
    parts = [part[None]] + [spin(part, step)[None] for step in range(1, count)]
    return parts, [(here - step) % count for step in range(count)]


def around(part):
    return place_parts(*around_parts(part))


def scan_first(state, direction):
    received = slide(state, direction)
    return received, low(wide(state) + wide(received))


def scan_rest(received, running, direction):
    found, step = [received], 2
    while step < lax.axis_size("shard"):
        found.append(slide(running, direction * step))
        running = low(wide(running) + wide(found[-1]))
        step *= 2
    return found


def sides_of(own):
    return flip(own, 2), flip(own, 4)


def halves_of(from_x, from_y):
    half = from_x.shape[0] // 2
    return from_x[:half], from_y[half:]


def diagonal_of(halves):
    return jnp.concatenate([flip(halves[0], 4), flip(halves[1], 2)], axis=0)


def share(own):
    parts = [own[None]] + [flip(own, bit)[None] for bit in (2, 4, 6)]
    even = place_parts(parts, [0, 1, 2, 3])
    return even, flip(even, 1)


def sides_kernel(x_part, y_part, to_x, to_y, x_sum, y_sum):
    half = to_x.shape[0]
    x_sum[:half] = low(wide(x_part[:half]) + wide(to_x[...]))
    x_sum[half:] = x_part[half:]
    y_sum[:half] = y_part[:half]
    y_sum[half:] = low(wide(y_part[half:]) + wide(to_y[...]))


def join_parts(parts):
    count, here = lax.axis_size("shard"), lax.axis_index("shard")
    bit = PIECES
    if bit < lax.axis_size("rep"):
        mine = sum(wide(part) for part in parts)
        while bit < lax.axis_size("rep"):
            mine = mine + wide(flip(low(mine), bit))
            bit *= 2
        parts = [mine]
    rows, columns = parts[0].shape
    rows //= count

    def kernel(spot, *refs):
        sources, outs = refs[: len(parts)], refs[len(parts) :]
        for step in range(count):
            block = lax.rem(spot[0] + step, count)
            chosen = pl.ds(pl.multiple_of(block * rows, rows), rows)
            total = wide(sources[0][chosen, :])
            for source in sources[1:]:
                total = total + wide(source[chosen, :])
            outs[step][...] = total if step == 0 else low(total)

    shapes = [whole((rows, columns), wide_type)] + [whole((rows, columns))] * (count - 1)
    return call(kernel, 2, tuple(shapes), scalar_first(len(parts)))(
        here.reshape(1).astype(jnp.int32), *parts
    )


def settle(own, received):
    def kernel(own, *refs):
        total = own[...]
        for ref in refs[:-1]:
            total = total + wide(ref[...])
        refs[-1][...] = low(total)

    return call(kernel, 1, whole(own.shape))(own, *received)


def dot(a, b):
    return jnp.dot(a, b, preferred_element_type=wide_type)


def dot_nt(a, b):
    return lax.dot_general(a, b, (((1,), (1,)), ((), ())), preferred_element_type=wide_type)


def dot_tn(a, b):
    return lax.dot_general(a, b, (((0,), (0,)), ((), ())), preferred_element_type=wide_type)


def normalize(rows):
    centred = rows - jnp.mean(rows, axis=-1, keepdims=True)
    scale = lax.rsqrt(jnp.mean(centred * centred, axis=-1, keepdims=True) + norm_epsilon)
    return centred * scale, scale


def norm_backward(grad, normal, scale, gain):
    e = grad * gain
    return scale * (
        e
        - jnp.mean(e, axis=-1, keepdims=True)
        - normal * jnp.mean(e * normal, axis=-1, keepdims=True)
    )


def lane_index(shape):
    return lax.broadcasted_iota(jnp.int32, shape, len(shape) - 1)


def row_index(shape):
    return lax.broadcasted_iota(jnp.int32, shape, len(shape) - 2)


def left_half(shape):
    return lane_index(shape) < HEAD


def aligned(index, unit):
    return pl.multiple_of(index * unit, unit)


def with_ones(pair):
    left = left_half(pair.shape)
    one = jnp.ones_like(pair)
    return jnp.where(left, pair, one), jnp.where(left, one, pair)


def pack_state(even, odd, p):
    lane = lane_index(even.shape)
    packed = jnp.where(lane < HEAD, even, odd)
    sums = jnp.where(lane == HEAD + 2 * p, even, jnp.where(lane == 2 * p + 1, odd, 0.0))
    return packed, sums


def unpack_state(packed, sums, p):
    shape = packed.shape
    lane, row = lane_index(shape), row_index(shape)
    pick_even = low(jnp.where((row == HEAD + 2 * p) & (lane >= HEAD), 1.0, 0.0))
    pick_odd = low(jnp.where((row == 2 * p + 1) & (lane < HEAD), 1.0, 0.0))
    even = jnp.where(lane < HEAD, packed, dot(sums, pick_even))
    odd = jnp.where(lane < HEAD, dot(sums, pick_odd), packed)
    return low(even), low(odd)


def added(refs, b, rows):
    total = wide(refs[0][b, rows, :])
    for ref in refs[1:]:
        total = total + wide(ref[b, rows, :])
    return total


def states_at(refs, b, p):
    packed = added(refs, b, pl.ds(aligned(p, FEAT), FEAT))
    sums = low(added(refs, b, slice(PAIRS * FEAT, SLAB)))
    return unpack_state(packed, sums, p)


def features(maps, base, columns, f_t, f):
    def group(g, carry):
        u_t = dot_nt(maps[base + g], columns[:, pl.ds(aligned(g, GROUP), GROUP)])
        for a in range(4):
            u = u_t[a * HEAD : (a + 1) * HEAD]
            up = jnp.exp(u - jnp.max(u, axis=0, keepdims=True))
            down = jnp.exp(jnp.min(u, axis=0, keepdims=True) - u)
            plus = up / jnp.sum(up, axis=0, keepdims=True)
            minus = down / jnp.sum(down, axis=0, keepdims=True)
            feature = low(jnp.concatenate([plus, minus], axis=0))
            rows = pl.ds(aligned(g * 4 + a, FEAT), FEAT)
            f_t[rows, :] = feature
            f[:, rows] = feature.T
        return carry

    lax.fori_loop(0, D // GROUP, group, 0)


def wanted(place, k, first, last):
    block = place[0] ^ k
    return block, (block >= first) & (block < last)


def each_piece(place, pieces, first, last, work):
    for k in range(PIECES):
        block, use = wanted(place, k, first, last)

        @pl.when(use)
        def _():
            work(block - first, pieces[k])


def chunk_at(index):
    return pl.ds(aligned(index, CHUNK), CHUNK)


def pair_at(index):
    return pl.ds(aligned(index, FEAT), FEAT)


VALUES = D // FEAT
QUERY_BLOCKS = D // CHUNK


def copy_rows(source, target):
    def step(i, carry):
        rows = pl.ds(aligned(i, 2 * HEAD), 2 * HEAD)
        target[rows, :] = source[rows, :]
        return carry

    lax.fori_loop(0, source.shape[0] // (2 * HEAD), step, 0)


def keys_kernel(place, tokens, vectors, maps, *refs):
    pieces = refs[:PIECES]
    normed, keyed, fk, fk_t, state, w_kv = refs[PIECES:]
    seqs = state.shape[0]
    length = tokens.shape[0] // seqs
    normal, _ = normalize(wide(tokens[...]))
    normed[...] = low(normal * vectors[0:1, :] + vectors[1:2, :])

    def keep(index, weight):
        copy_rows(weight, w_kv.at[index])

    each_piece(place, pieces, QUERY_BLOCKS, QKV_BLOCKS, keep)

    def project(index, carry):
        keyed[:, chunk_at(index)] = low(dot(normed[...], w_kv[index]))
        return carry

    lax.fori_loop(0, QKV_BLOCKS - QUERY_BLOCKS, project, 0)
    features(maps, D // GROUP, keyed, fk_t, fk)
    state_sums(state, length, lambda p, here: with_ones(keyed[here, pair_at(VALUES + p)]), fk_t)


def state_sums(state, length, sides, f_t):
    seqs = state.shape[0]

    def pair(p, sums):
        result = []
        for b in range(seqs):
            here = slice(b * length, (b + 1) * length)
            first, second = sides(p, here)
            even = dot(f_t[pair_at(2 * p), here], first)
            odd = dot(f_t[pair_at(2 * p + 1), here], second)
            packed, new = pack_state(even, odd, p)
            state[b, pair_at(p), :] = low(packed)
            result.append(sums[b] + new)
        return tuple(result)

    empty = tuple(jnp.zeros((FEAT, FEAT), wide_type) for _ in range(seqs))
    sums = lax.fori_loop(0, PAIRS, pair, empty)
    for b in range(seqs):
        state[b, PAIRS * FEAT :, :] = low(sums[b])


def queries_kernel(place, normed, keyed, fk_t, maps, *refs):
    pieces = refs[:PIECES]
    normed_t, queries, fq, fq_t, partial, w_out, w_q = refs[PIECES:]

    def keep(index, weight):
        copy_rows(weight, w_q.at[index])

    def keep_out(index, weight):
        copy_rows(weight, w_out.at[:, chunk_at(index)])

    each_piece(place, pieces, 0, QUERY_BLOCKS, keep)
    each_piece(place, pieces, QKV_BLOCKS, PIECES, keep_out)

    def project(index, carry):
        queries[:, chunk_at(index)] = low(dot(normed[...], w_q[index]))
        return carry

    lax.fori_loop(0, QUERY_BLOCKS, project, 0)
    normed_t[...] = normed[...].T
    features(maps, 0, queries, fq_t, fq)
    seqs, length, _ = partial.shape

    def pair(p, carry):
        for b in range(seqs):
            here = slice(b * length, (b + 1) * length)
            values = with_ones(keyed[here, pair_at(VALUES + p)])
            for side in range(2):
                rows = pair_at(2 * p + side)
                scores = dot(fq[here, rows], fk_t[rows, here])
                scores = jnp.where(row_index(scores.shape) >= lane_index(scores.shape), scores, 0.0)
                partial[b, :, rows] = dot(low(scores), values[side])
        return carry

    lax.fori_loop(0, PAIRS, pair, 0)


def attend_kernel(tokens, vectors, partial, fq, w_out, *refs):
    priors, (attended, inverse, resid, second, second_t) = refs[:-5], refs[-5:]
    seqs = priors[0].shape[0]
    length = tokens.shape[0] // seqs

    def pair(p, carry):
        for b in range(seqs):
            here = slice(b * length, (b + 1) * length)
            states = states_at(priors, b, p)
            found = []
            for side in range(2):
                rows = pair_at(2 * p + side)
                found.append(partial[b, :, rows] + dot(fq[here, rows], states[side]))
            left = left_half(found[0].shape)
            turned = [pltpu.roll(a, HEAD, 1) for a in found]
            over = 1.0 / jnp.where(left, turned[0], turned[1])
            attended[here, pair_at(p)] = low(jnp.where(left, found[0], found[1]) * over)
            inverse[here, pair_at(p)] = over
        return carry

    lax.fori_loop(0, PAIRS, pair, 0)
    resid[...] = wide(tokens[...]) + dot(attended[...], w_out[...])
    normal, _ = normalize(resid[...])
    second[...] = low(normal * vectors[2:3, :] + vectors[3:4, :])
    second_t[...] = second[...].T


def mlp_kernel(second, second_other, cotangent, cotangent_other, resid, attended, *refs):
    pieces = refs[:4]
    out_sum, out_send, back_sum, back_send, hiddens, d_pres, second_other_t, attended_t = refs[4:12]
    out_other, back_other, up, down, ready = refs[12:]
    count = second.shape[0]
    parts = grads_layout(second.shape[1], pieces[0].shape[0])

    def copies(k, source):
        listed = []
        for i, (src, dst) in enumerate(parts):
            if dst[0] == "up":
                target = up.at[k, pl.ds(dst[1], dst[2]), :]
            else:
                target = down.at[k, pl.ds(dst[1], dst[2]), pl.ds(dst[3], CHUNK)]
            listed.append(
                pltpu.make_async_copy(source.at[pl.ds(src, dst[2]), :], target, ready.at[k, i])
            )
        return listed

    for k in range(4):
        for copy in copies(k, pieces[k]):
            copy.start()
    out_sum[...] = resid[...]
    for total in (out_other, back_sum, back_other):
        total[...] = jnp.zeros_like(total)
    second_other_t[...] = second_other[...].T
    attended_t[...] = attended[...].T
    sides = (
        (second, cotangent, out_sum, back_sum),
        (second_other, cotangent_other, out_other, back_other),
    )

    def piece(k, carry):
        for copy in copies(k, pieces[0]):
            copy.wait()
        for side, (source, grad, out_total, back_total) in enumerate(sides):
            here = slice(side * count, (side + 1) * count)
            pre = dot(source[...], up[k])
            square = pre * pre
            bent = jnp.tanh(0.7978845608 * (pre + 0.044715 * square * pre))
            half = 0.5 * (1.0 + bent)
            hidden = low(pre * half)
            slope = half + (0.5 * 0.7978845608) * pre * (1.0 - bent * bent) * (
                1.0 + 3.0 * 0.044715 * square
            )
            hiddens[k, here] = hidden
            out_total[...] += dot(hidden, down[k])
            d_pre = low(dot_nt(grad[...], down[k]) * slope)
            d_pres[k, here] = d_pre
            back_total[...] += dot_nt(d_pre, up[k])
        return carry

    lax.fori_loop(0, 4, piece, 0)
    out_send[...] = low(out_other[...])
    back_send[...] = low(back_other[...])


def store_piece(outs, made, k):
    half = outs[3].shape[0]
    for i in range(3):

        @pl.when(k == i)
        def _():
            outs[i][...] = made[...]

    @pl.when(k == 3)
    def _():
        outs[3][...] = made[:half]
        outs[4][...] = made[half:]


def mlp_grads_kernel(second_t, second_other_t, cotangent, cotangent_other, hiddens, d_pres, *refs):
    outs, made = refs[:5], refs[5]
    count = cotangent.shape[0]
    own, other = slice(0, count), slice(count, 2 * count)

    def piece(k, carry):
        d_up = dot(second_t[...], d_pres[k, own]) + dot(second_other_t[...], d_pres[k, other])
        d_down = dot_tn(hiddens[k, own], cotangent[...])
        d_down = d_down + dot_tn(hiddens[k, other], cotangent_other[...])
        d_up, d_down = low(d_up), low(d_down)
        for src, dst in grads_layout(second_t.shape[0], made.shape[0]):
            rows = slice(dst[1], dst[1] + dst[2])
            if dst[0] == "up":
                made[src : src + dst[2], :] = d_up[rows]
            else:
                made[src : src + dst[2], :] = d_down[rows, dst[3] : dst[3] + CHUNK]
        store_piece(outs, made, k)
        return carry

    lax.fori_loop(0, 4, piece, 0)


def grads_layout(width, block):
    shards = block // CHUNK
    up_rows = width // shards
    down_rows = CHUNK // shards
    parts = []
    for s in range(shards):
        base = s * (up_rows + 2 * down_rows)
        parts.append((base, ("up", s * up_rows, up_rows)))
        for side in range(2):
            parts.append(
                (
                    base + up_rows + side * down_rows,
                    ("down", s * down_rows, down_rows, side * CHUNK),
                )
            )
    return parts


def resid_kernel(back_sum, back_other, resid, cotangent, vectors, w_out, attended, inverse, fq_t, *refs):
    d_resid, d_resid_low, d_vectors, d_num, d_den, state = refs
    seqs = state.shape[0]
    length = resid.shape[0] // seqs
    normal, scale = normalize(resid[...])
    grad = back_sum[...] + wide(back_other[...])
    d_vectors[0:1, :] = jnp.sum(grad * normal, axis=0, keepdims=True)
    d_vectors[1:2, :] = jnp.sum(grad, axis=0, keepdims=True)
    d_resid[...] = wide(cotangent[...]) + norm_backward(grad, normal, scale, vectors[2:3, :])
    d_resid_low[...] = low(d_resid[...])
    d_attended = dot_nt(d_resid_low[...], w_out[...])
    shape = (FEAT, FEAT)
    cross = low(
        jnp.where(left_half(shape) != (row_index(shape) < HEAD), -1.0 / HEAD, 0.0)
    )
    for p in range(PAIRS):
        columns = slice(p * FEAT, (p + 1) * FEAT)
        num = d_attended[:, columns] * inverse[:, columns]
        product = num * wide(attended[:, columns])
        top = low(product)
        rest = low(product - wide(top))
        d_num[:, columns] = low(num)
        d_den[:, columns] = low(dot(top, cross) + dot(rest, cross))

    state_sums(state, length, lambda p, here: joined(d_num, d_den, here, p), fq_t)


def joined(d_num, d_den, here, p):
    columns = pl.ds(aligned(p, FEAT), FEAT)
    num, den = d_num[here, columns], d_den[here, columns]
    left = left_half(num.shape)
    return jnp.where(left, num, den), jnp.where(left, den, num)


def softmax_backward(feature, grad):
    plus, minus = wide(feature[:HEAD]), wide(feature[HEAD:])
    d_plus, d_minus = grad[:HEAD], grad[HEAD:]
    d_plus = plus * (d_plus - jnp.sum(d_plus * plus, axis=0, keepdims=True))
    d_minus = minus * (d_minus - jnp.sum(d_minus * minus, axis=0, keepdims=True))
    return low(d_plus - d_minus)


def local_kernel(queries, keyed, maps, fq_t, fk, fk_t, d_num, d_den, *refs):
    priors, (d_fk_t, d_values, d_queries, d_features, d_uq_t) = refs[:-5], refs[-5:]
    seqs = priors[0].shape[0]
    length = keyed.shape[0] // seqs

    def pair(p, carry):
        for b in range(seqs):
            here = slice(b * length, (b + 1) * length)
            values = with_ones(keyed[here, pair_at(VALUES + p)])
            outer = joined(d_num, d_den, here, p)
            states = states_at(priors, b, p)
            found = []
            for side in range(2):
                rows = pl.ds(aligned(2 * p + side, FEAT), FEAT)
                q_t, k_t = fq_t[rows, here], fk_t[rows, here]
                link = dot_nt(outer[side], values[side])
                row, lane = row_index(link.shape), lane_index(link.shape)
                link = low(jnp.where(row >= lane, link, 0.0))
                d_q = dot_nt(k_t, link) + dot_nt(states[side], outer[side])
                d_uq_t[pl.ds(aligned(2 * p + side, HEAD), HEAD), here] = softmax_backward(q_t, d_q)
                d_fk_t[rows, here] = dot(q_t, link)
                scores = dot(fk[here, rows], q_t)
                scores = low(jnp.where(row <= lane, scores, 0.0))
                found.append(dot(scores, outer[side]))
            left = left_half(found[0].shape)
            d_values[here, pl.ds(aligned(p, FEAT), FEAT)] = jnp.where(left, found[0], found[1])
        return carry

    lax.fori_loop(0, PAIRS, pair, 0)
    feature_backward(d_uq_t, queries, maps, 0, d_queries, d_features, 0)


def feature_backward(d_u_t, source, maps, base, target, d_features, lane):
    def group(g, carry):
        d_u = d_u_t[pl.ds(aligned(g, GROUP), GROUP), :]
        columns = pl.ds(aligned(g, GROUP), GROUP)
        product = dot(d_u, source[:, columns]).T
        for a in range(4):
            block = slice(a * HEAD, (a + 1) * HEAD)
            rows = pl.ds(aligned(g * 4 + a, HEAD), HEAD)
            d_features[rows, lane : lane + HEAD] = product[block, block]
        target[:, columns] = low(dot(d_u.T, maps[base + g]))
        return carry

    lax.fori_loop(0, D // GROUP, group, 0)


def mixed_kernel(
    place, keyed, fk, fk_t, maps, d_fk_t, d_values, d_resid_low, d_queries, d_half, *refs
):
    laters, (d_keyed, d_features, sends, d_uk_t) = refs[:-4], refs[-4:]
    seqs = laters[0].shape[0]
    length = keyed.shape[0] // seqs

    def pair(p, carry):
        for b in range(seqs):
            here = slice(b * length, (b + 1) * length)
            values = with_ones(keyed[here, pair_at(VALUES + p)])
            states = states_at(laters, b, p)
            found = []
            for side in range(2):
                rows = pl.ds(aligned(2 * p + side, FEAT), FEAT)
                d_k = d_fk_t[rows, here] + dot_nt(states[side], values[side])
                d_uk_t[pl.ds(aligned(2 * p + side, HEAD), HEAD), here] = softmax_backward(
                    fk_t[rows, here], d_k
                )
                found.append(dot(fk[here, rows], states[side]))
            left = left_half(found[0].shape)
            total = d_values[here, pl.ds(aligned(p, FEAT), FEAT)] + jnp.where(
                left, found[0], found[1]
            )
            d_keyed[here, pair_at(VALUES + p)] = low(total)
        return carry

    lax.fori_loop(0, PAIRS, pair, 0)
    feature_backward(d_uk_t, keyed, maps, D // GROUP, d_keyed, d_features, HEAD)
    d_features[:, :HEAD] = d_half[:, :HEAD]

    def send(i, carry):
        own_column(place[0] ^ (2 * i + 1), sends.at[i], d_queries, d_keyed, d_resid_low)
        return carry

    lax.fori_loop(0, PIECES // 2, send, 0)


def own_column(block, target, d_queries, d_keyed, d_resid_low):
    @pl.when(block < QUERY_BLOCKS)
    def _():
        target[...] = d_queries[:, chunk_at(block)]

    @pl.when((block >= QUERY_BLOCKS) & (block < QKV_BLOCKS))
    def _():
        target[...] = d_keyed[:, chunk_at(block - QUERY_BLOCKS)]

    @pl.when(block >= QKV_BLOCKS)
    def _():
        target[...] = d_resid_low[:, chunk_at(block - QKV_BLOCKS)]


TINY_ROWS = 48
TINY_TILE = 16


def tiny_size(rows):
    return -(-(rows + 8) // TINY_ROWS) * TINY_ROWS


def in_grads_kernel(
    place, d_queries, d_keyed, d_resid_low, received, tiny, tiny_other, *refs
):
    sources, outs, (held, column, made, ready) = refs[:4], refs[4:9], refs[9:]
    shard_count, size, _ = tiny.shape
    rows = D // shard_count
    copies = [
        pltpu.make_async_copy(source, held.at[i], ready.at[i]) for i, source in enumerate(sources)
    ]
    for copy in copies:
        copy.start()
    for copy in copies:
        copy.wait()

    def piece(i, carry):
        block = place[0] ^ (2 * i)
        kind = 2 * jnp.where(block < QKV_BLOCKS, 0, 1)
        own_column(block, column, d_queries, d_keyed, d_resid_low)
        value = low(dot(held[kind], column[...]) + dot(held[kind + 1], received[i]))
        for s in range(shard_count):
            base = s * (rows + TINY_TILE)
            made[base : base + rows, :] = value[s * rows : (s + 1) * rows]
            for j in range(TINY_ROWS // TINY_TILE):
                target = (slice(base + rows, base + rows + TINY_TILE), slice(j * FEAT, (j + 1) * FEAT))
                made[target] = jnp.zeros((TINY_TILE, FEAT), low_type)

                @pl.when(block < size // TINY_ROWS)
                def _():
                    start = pl.multiple_of(block * TINY_ROWS + j * TINY_TILE, TINY_TILE)
                    spot = pl.ds(start, TINY_TILE)
                    made[target] = low(wide(tiny[s, spot, :]) + wide(tiny_other[s, spot, :]))

        store_piece(outs, made, i)
        return carry

    lax.fori_loop(0, PIECES // 2, piece, 0)


def input_kernel(tokens, vectors, d_queries, d_keyed, d_resid, out_sum, out_other, *refs):
    w_q, w_kv, d_features, d_vectors, block_out, grad_tokens, tiny, total = refs
    total[...] = jnp.zeros_like(total)
    block_out[...] = low(out_sum[...] + wide(out_other[...]))

    def add_from(source, weights):
        def add(index, carry):
            total[...] += dot_nt(source[:, chunk_at(index)], weights[index])
            return carry

        lax.fori_loop(0, weights.shape[0], add, 0)

    add_from(d_queries, w_q)
    add_from(d_keyed, w_kv)
    normal, scale = normalize(wide(tokens[...]))
    grad = total[...]
    grad_tokens[...] = low(d_resid[...] + norm_backward(grad, normal, scale, vectors[0:1, :]))
    gathered = [
        jnp.sum(grad * normal, axis=0, keepdims=True),
        jnp.sum(grad, axis=0, keepdims=True),
        d_vectors[0:1, :],
        d_vectors[1:2, :],
    ]
    shard_count, size, _ = tiny.shape
    rows = D // shard_count
    tiny[...] = jnp.zeros_like(tiny)
    for s in range(shard_count):
        tiny[s, :rows, :] = low(d_features[s * rows : (s + 1) * rows, :])
        lines = []
        for vector in gathered:
            line = vector[:, s * rows : (s + 1) * rows]
            gap = jnp.zeros((1, 2 * FEAT - rows), wide_type)
            line = jnp.concatenate([line, gap], axis=1)
            lines += [line[:, :FEAT], line[:, FEAT:]]
        tiny[s, rows : rows + 8, :] = low(jnp.concatenate(lines, axis=0))


def lay_in_kernel(place, even, odd, qkv, out, tiny):
    rows = qkv.shape[0]
    for k in range(PIECES):
        block = place[0] ^ k
        piece = (even, odd)[k % 2].at[k // 2]

        @pl.when(block < QKV_BLOCKS)
        def _():
            qkv[:, chunk_at(block)] = wide(piece[:rows])

        @pl.when(block >= QKV_BLOCKS)
        def _():
            out[:, chunk_at(block - QKV_BLOCKS)] = wide(piece[:rows])

        @pl.when(block < tiny.shape[0] // TINY_ROWS)
        def _():
            for j in range(TINY_ROWS // TINY_TILE):
                start = pl.multiple_of(block * TINY_ROWS + j * TINY_TILE, TINY_TILE)
                tiny[pl.ds(start, TINY_TILE), :] = wide(
                    piece[rows:, j * FEAT : (j + 1) * FEAT]
                )


def lay_mlp_kernel(place, even, odd, up, down, ordered):
    up_rows, down_rows = ordered.shape[1], down.shape[1]
    for k in range(PIECES):
        block = place[0] ^ k
        piece = (even, odd)[k % 2]
        ordered[block] = piece[k // 2, :up_rows, :]
        for side in range(2):
            start = up_rows + side * down_rows
            down[block, :, side * CHUNK : (side + 1) * CHUNK] = wide(
                piece[k // 2, start : start + down_rows, :]
            )
    for s in range(CHUNK // down_rows):
        columns = slice(s * down_rows, (s + 1) * down_rows)
        row = jnp.concatenate([ordered[r][:, columns] for r in range(PIECES)], axis=1)
        up[:, s * PIECES * down_rows : (s + 1) * PIECES * down_rows] = wide(row)


def whole(shape, dtype=low_type):
    return jax.ShapeDtypeStruct(shape, dtype)


def scalar_first(count):
    return [pl.BlockSpec(memory_space=pltpu.SMEM)] + [
        pl.BlockSpec(memory_space=pltpu.VMEM) for _ in range(count)
    ]


def call(kernel, weight, out_shape, in_specs=None, scratch=(), limit=8, **rest):
    if in_specs is not None:
        rest["in_specs"] = in_specs
    return pl.pallas_call(
        kernel,
        out_shape=out_shape,
        scratch_shapes=list(scratch),
        compiler_params=pltpu.CompilerParams(vmem_limit_bytes=limit << 20),
        cost_estimate=pl.CostEstimate(
            flops=weight * 2000 * 10**6, transcendentals=0, bytes_accessed=weight * 3 * 2000 * 10**3
        ),
        **rest,
    )


def interleave(even, odd):
    return [part for both in zip(even, odd) for part in both]


def shards(
    tokens,
    gain_attn,
    bias_attn,
    w_qkv,
    w_feature,
    w_out,
    gain_mlp,
    bias_mlp,
    w_up,
    w_down,
    cotangent,
):
    shard_count = lax.axis_size("shard")
    place = lax.axis_index("rep") % PIECES
    spot = place.reshape(1).astype(jnp.int32)
    seqs, length, _ = tokens.shape
    count = seqs * length
    rows = w_qkv.shape[0]
    fine = CHUNK // shard_count
    flat = tokens.reshape(count, D)
    flat_cotangent = cotangent.reshape(count, D)
    anywhere = [pl.BlockSpec(memory_space=pl.ANY)] * PIECES

    part_in = lax.dynamic_slice_in_dim(
        jnp.concatenate([w_qkv, w_out], axis=1), place * CHUNK, CHUNK, 1
    )
    vectors = jnp.concatenate([gain_attn, bias_attn, gain_mlp, bias_mlp]).reshape(-1, FEAT)
    small = jnp.concatenate([w_feature, vectors], axis=0)
    small_rows = -(-small.shape[0] // 24) * 8
    small = jnp.pad(small, ((0, 3 * small_rows - small.shape[0]), (0, 0)))
    small = jnp.concatenate(jnp.split(small, 3, axis=0), axis=1)
    part_in = jnp.concatenate([part_in, small], axis=0)
    part_up = lax.dynamic_index_in_dim(
        w_up.reshape(rows, shard_count, PIECES, fine), place, 2, False
    ).reshape(rows, CHUNK)
    part_down = lax.dynamic_slice_in_dim(w_down, place * fine, fine, 0)
    part_mlp = jnp.concatenate([part_up, part_down[:, :CHUNK], part_down[:, CHUNK:]], axis=0)

    here = lax.axis_index("shard")
    in_slots = jnp.stack([(here - step) % shard_count for step in range(shard_count)])
    in_spins = [part_in] + [spin(part_in, step) for step in range(1, shard_count)]

    def place_in_kernel(slots, *refs):
        parts, (full, rest) = refs[:-2], refs[-2:]
        for i, part in enumerate(parts):
            full[slots[i]] = part[:rows]
            rest[slots[i]] = part[rows:]

    in_full, small = call(
        place_in_kernel,
        1,
        (whole((shard_count, rows, CHUNK)), whole((shard_count, small_rows, CHUNK))),
        scalar_first(shard_count),
    )(in_slots.astype(jnp.int32), *in_spins)
    small = jnp.concatenate(jnp.split(small, 3, axis=2), axis=1)
    cotangent_other = flip(flat_cotangent, 1)
    feature_weight = small[:, :rows].reshape(D, FEAT)
    vectors = wide(small[:, rows : rows + 4 * rows // FEAT].reshape(shard_count, 4, rows).transpose(1, 0, 2).reshape(4, D))
    blocks = feature_weight.reshape(D // GROUP, 4, HEAD, 2, HEAD)
    maps = (
        jnp.einsum("gaiwo,ab->wgaobi", blocks, jnp.eye(4, dtype=low_type))
        .reshape(2 * D // GROUP, GROUP, GROUP)
        .astype(low_type)
    )
    in_full = in_full.reshape(-1, CHUNK)
    steps = list(range(1, shard_count))
    soon = {step: spin(part_mlp, step) for step in steps[:1]}
    in_full, part_mlp, soon = lax.optimization_barrier((in_full, part_mlp, soon))
    from_x, from_y = sides_of(in_full)
    in_other = flip(in_full, 1)
    soon.update({step: spin(part_mlp, step) for step in steps[1:2]})
    in_halves, maps, vectors, soon, part_mlp = lax.optimization_barrier(
        (halves_of(from_x, from_y), maps, vectors, soon, part_mlp)
    )
    soon.update({step: spin(part_mlp, step) for step in steps[2:]})
    diagonal, soon = lax.optimization_barrier((diagonal_of(in_halves), soon))
    in_even = [in_full, from_x, from_y, diagonal]
    in_pieces = interleave(in_even, [in_other] + [flip(part, 1) for part in in_even[1:]])
    here = lax.axis_index("shard")
    mlp_parts = [part_mlp[None]] + [soon[step][None] for step in steps]
    mlp_slots = [(here - step) % shard_count for step in range(shard_count)]

    normed, keyed, fk, fk_t, key_state, w_kv = call(
        keys_kernel,
        8,
        (
            whole((count, D)),
            whole((count, 2 * D)),
            whole((count, HEADS * FEAT)),
            whole((HEADS * FEAT, count)),
            whole((seqs, SLAB, FEAT)),
            whole((QKV_BLOCKS - QUERY_BLOCKS, D, CHUNK)),
        ),
        scalar_first(3 + PIECES),
    )(spot, flat, vectors, maps, *in_pieces)
    prior, running = scan_first(key_state, 1)
    mlp_parts, normed = lax.optimization_barrier((mlp_parts, normed))
    mlp_full = place_parts(mlp_parts, mlp_slots).reshape(-1, CHUNK)
    mlp_full, normed = lax.optimization_barrier((mlp_full, normed))
    mlp_x, mlp_y = sides_of(mlp_full)
    normed_t, queries, fq, fq_t, partial, out_weight, w_q = call(
        queries_kernel,
        9,
        (
            whole((D, count)),
            whole((count, D)),
            whole((count, HEADS * FEAT)),
            whole((HEADS * FEAT, count)),
            whole((seqs, length, HEADS * FEAT), wide_type),
            whole((D, D)),
            whole((QUERY_BLOCKS, D, CHUNK)),
        ),
        scalar_first(4 + PIECES),
    )(spot, normed, keyed, fk_t, maps, *in_pieces)
    running, partial = lax.optimization_barrier((running, partial))
    priors = scan_rest(prior, running, 1)
    mlp_halves, partial = lax.optimization_barrier((halves_of(mlp_x, mlp_y), partial))
    mlp_pieces = [mlp_full, mlp_x, mlp_y, diagonal_of(mlp_halves)]
    attended, inverse, resid, second, second_t = call(
        attend_kernel,
        5,
        (
            whole((count, D)),
            whole((count, D), wide_type),
            whole((count, D), wide_type),
            whole((count, D)),
            whole((D, count)),
        ),
    )(flat, vectors, partial, fq, out_weight, *priors)

    second_other = flip(second, 1)
    (
        out_sum,
        out_send,
        back_sum,
        back_send,
        hiddens,
        d_pres,
        second_other_t,
        attended_t,
    ) = call(
        mlp_kernel,
        20,
        (
            whole((count, D), wide_type),
            whole((count, D)),
            whole((count, D), wide_type),
            whole((count, D)),
            whole((4, 2 * count, CHUNK)),
            whole((4, 2 * count, CHUNK)),
            whole((D, count)),
            whole((D, count)),
        ),
        [pl.BlockSpec(memory_space=pltpu.VMEM)] * 6 + anywhere[:4],
        [
            pltpu.VMEM((count, D), wide_type),
            pltpu.VMEM((count, D), wide_type),
            pltpu.VMEM((4, D, CHUNK), low_type),
            pltpu.VMEM((4, CHUNK, D), low_type),
            pltpu.SemaphoreType.DMA((4, 3 * shard_count)),
        ],
        limit=18,
    )(second, second_other, flat_cotangent, cotangent_other, resid, attended, *mlp_pieces)
    back_other = flip(back_send, 1)
    out_other = flip(out_send, 1)
    d_resid, d_resid_low, d_vectors_two, d_num, d_den, query_state = call(
        resid_kernel,
        5,
        (
            whole((count, D), wide_type),
            whole((count, D)),
            whole((2, D), wide_type),
            whole((count, D)),
            whole((count, D)),
            whole((seqs, SLAB, FEAT)),
        ),
    )(back_sum, back_other, resid, flat_cotangent, vectors, out_weight, attended, inverse, fq_t)
    later, running = scan_first(query_state, -1)
    normed_other_t = flip(normed_t, 1)
    attended_other_t = flip(attended_t, 1)
    second_t, query_state, normed_other_t, attended_other_t, out_other = lax.optimization_barrier(
        (second_t, query_state, normed_other_t, attended_other_t, out_other)
    )
    piece = lambda rows: tuple(
        whole((size, CHUNK)) for size in (rows, rows, rows, rows // 2, rows // 2)
    )
    mlp_grads = call(
        mlp_grads_kernel, 7, piece(2 * D), scratch=[pltpu.VMEM((2 * D, CHUNK), low_type)]
    )(second_t, second_other_t, flat_cotangent, cotangent_other, hiddens, d_pres)
    mlp_upper, mlp_lower, running, fk = lax.optimization_barrier(
        (mlp_grads[3], mlp_grads[4], running, fk)
    )
    laters = scan_rest(later, running, -1)
    mlp_to_x, mlp_to_y = flip(mlp_upper, 4), flip(mlp_lower, 2)
    d_fk_t, d_values, d_queries, d_half, _ = call(
        local_kernel,
        10,
        (
            whole((HEADS * FEAT, count), wide_type),
            whole((count, D), wide_type),
            whole((count, D)),
            whole((D, FEAT), wide_type),
            whole((D, count)),
        ),
    )(queries, keyed, maps, fq_t, fk, fk_t, d_num, d_den, *priors)
    add_sides = lambda parts, to_x, to_y: call(
        sides_kernel, 1, (whole(parts[1].shape), whole(parts[1].shape))
    )(parts[1], parts[2], to_x, to_y)
    mlp_sides = add_sides(mlp_grads, mlp_to_x, mlp_to_y)
    mlp_sides, d_half = lax.optimization_barrier((mlp_sides, d_half))
    mlp_joined = [flip(mlp_sides[0], 2), flip(mlp_sides[1], 4)]
    d_keyed, d_features, sends, _ = call(
        mixed_kernel,
        7,
        (
            whole((count, 2 * D)),
            whole((D, FEAT), wide_type),
            whole((PIECES // 2, count, CHUNK)),
            whole((D, count)),
        ),
        scalar_first(9 + len(laters)),
    )(spot, keyed, fk, fk_t, maps, d_fk_t, d_values, d_resid_low, d_queries, d_half, *laters)
    received = flip(sends, 1)
    block_out, grad_tokens, tiny = call(
        input_kernel,
        7,
        (
            whole((count, D)),
            whole((count, D)),
            whole((shard_count, tiny_size(rows), FEAT)),
        ),
        scratch=[pltpu.VMEM((count, D), wide_type)],
    )(
        flat,
        vectors,
        d_queries,
        d_keyed,
        d_resid,
        out_sum,
        out_other,
        w_q,
        w_kv,
        d_features,
        d_vectors_two,
    )
    tiny_other = flip(tiny, 1)
    mlp_blocks = join_parts([mlp_grads[0], *mlp_joined])
    received, tiny_other, mlp_blocks = lax.optimization_barrier((received, tiny_other, mlp_blocks))
    in_grads = call(
        in_grads_kernel,
        7,
        piece(D + shard_count * TINY_TILE),
        scalar_first(6) + anywhere[:4],
        [
            pltpu.VMEM((4, D, count), low_type),
            pltpu.VMEM((count, CHUNK), low_type),
            pltpu.VMEM((D + shard_count * TINY_TILE, CHUNK), low_type),
            pltpu.SemaphoreType.DMA((4,)),
        ],
    )(
        spot,
        d_queries,
        d_keyed,
        d_resid_low,
        received,
        tiny,
        tiny_other,
        normed_t,
        normed_other_t,
        attended_t,
        attended_other_t,
    )
    in_to_x, in_to_y = flip(in_grads[3], 4), flip(in_grads[4], 2)
    mlp_received = [spin(part, step + 1) for step, part in enumerate(mlp_blocks[1:])]
    in_to_x, in_to_y, mlp_received[:1] = lax.optimization_barrier(
        (in_to_x, in_to_y, mlp_received[:1])
    )
    in_sides = add_sides(in_grads, in_to_x, in_to_y)
    in_joined = [flip(in_sides[0], 2), flip(in_sides[1], 4)]
    in_blocks = join_parts([in_grads[0], *in_joined])
    in_blocks, mlp_received = lax.optimization_barrier((in_blocks, mlp_received))
    mlp_sums = share(settle(mlp_blocks[0], mlp_received))
    in_received = [spin(part, step + 1) for step, part in enumerate(in_blocks[1:])]
    in_sums = share(settle(in_blocks[0], in_received))
    grad_up, grad_down = call(
        lay_mlp_kernel,
        3,
        (whole((rows, 4 * D), wide_type), whole((PIECES, fine, D), wide_type)),
        scalar_first(2),
        [pltpu.VMEM((PIECES, rows, CHUNK), low_type)],
    )(spot, *mlp_sums)
    grad_down = grad_down.reshape(-1, D)
    in_sums, grad_up, grad_down = lax.optimization_barrier((in_sums, grad_up, grad_down))
    grad_qkv, grad_out, tiny = call(
        lay_in_kernel,
        2,
        (
            whole((rows, 3 * D), wide_type),
            whole((rows, D), wide_type),
            whole((tiny_size(rows), FEAT), wide_type),
        ),
        scalar_first(2),
    )(spot, *in_sums)
    grad_feature = tiny[:rows]
    d_vectors = tiny[rows : rows + 8].reshape(4, 2 * FEAT)[:, :rows]
    return (
        block_out.reshape(tokens.shape),
        grad_tokens.reshape(tokens.shape),
        d_vectors[0],
        d_vectors[1],
        grad_qkv,
        grad_feature,
        grad_out,
        d_vectors[2],
        d_vectors[3],
        grad_up,
        grad_down,
    )


def solution(mesh):
    placed = (
        P("rep", "shard", None),
        P("shard"),
        P("shard"),
        P("shard", None),
        P("shard", None),
        P("shard", None),
        P("shard"),
        P("shard"),
        P("shard", None),
        P("shard", None),
        P("rep", "shard", None),
    )
    return jax.shard_map(
        shards,
        mesh=mesh,
        in_specs=placed,
        out_specs=(
            P("rep", "shard", None),
            P("rep", "shard", None),
            P("shard"),
            P("shard"),
            P("shard", None),
            P("shard", None),
            P("shard", None),
            P("shard"),
            P("shard"),
            P("shard", None),
            P("shard", None),
        ),
        check_vma=False,
    )
```

profile of v0, /device:TPU:9, one launch (start us, length us, event | category | flops | bytes accessed | tf_op | source)
XLA Modules:
  0.0 286.5 jit_solution(15249793515696532944)
XLA Ops:
  12.7 8.6 %collective-permute-done.1.refs_2_ = bf16[264,384]{1,0:T(8,128)(2,1)S(1)} collective-permute-done((bf16[264,384]{1,0:T(8,128)(2,1)S(1)}, bf16[264,384]{1,0:T(8,128)(2,1)S(1)}, u32[]{:S(2)}, u32[]{:S(2)}) %collective-permute-start.1) | collective-permute-done | bytes 202784 | tf_op jit(solution)/shard_map/ppermute | solution.py:31
  21.3 9.1 %collective-permute-done.2.refs_3_ = bf16[264,384]{1,0:T(8,128)(2,1)S(1)} collective-permute-done((bf16[264,384]{1,0:T(8,128)(2,1)S(1)}, bf16[264,384]{1,0:T(8,128)(2,1)S(1)}, u32[]{:S(2)}, u32[]{:S(2)}) %collective-permute-start.2) | collective-permute-done | bytes 202784 | tf_op jit(solution)/shard_map/ppermute | solution.py:31
  40.2 6.4 %collective-permute-done.4.refs_2_ = bf16[768,384]{1,0:T(8,128)(2,1)S(1)} collective-permute-done((bf16[768,384]{1,0:T(8,128)(2,1)}, bf16[768,384]{1,0:T(8,128)(2,1)S(1)}, u32[]{:S(2)}, u32[]{:S(2)}) %collective-permute-start.4) | collective-permute-done | bytes 589856 | tf_op jit(solution)/shard_map/ppermute | solution.py:26
  51.3 4.0 %collective-permute-done.7 = bf16[384,384]{1,0:T(8,128)(2,1)S(1)} collective-permute-done((bf16[384,384]{1,0:T(8,128)(2,1)S(1)}, bf16[384,384]{1,0:T(8,128)(2,1)S(1)}, u32[]{:S(2)}, u32[]{:S(2)}) %collective-permute-start.7) | collective-permute-done | bytes 294944 | tf_op jit(solution)/shard_map/ppermute | solution.py:26
  60.3 7.5 %shard_map.195 = (bf16[512,768]{1,0:T(8,128)(2,1)S(1)}, bf16[512,1536]{1,0:T(8,128)(2,1)S(1)}, bf16[512,1536]{1,0:T(8,128)(2,1)S(1)}, bf16[1536,512]{1,0:T(8,128...) custom-call(s32[1]{0:T(128)} %bitcast.10.place, bf16[512,768]{1,0:T(8,128)(2,1)S(1)} %bitcast.43, ...), custom_call_target="tpu_custom_call" | custom-call | flops 16000000000 | bytes 48000000 | tf_op jit(solution)/shard_map/pallas_call | solution.py:877
  70.7 3.9 %collective-permute-start.16 = (bf16[2,896,128]{2,1,0:T(8,128)(2,1)S(1)}, bf16[2,896,128]{2,1,0:T(8,128)(2,1)S(1)}, u32[]{:S(2)}, u32[]{:S(2)}) collective-permute-start(bf16[2,896,128]{2,1,0:T(8,128)(2,1)S(1)} %get-tuple-element.167), channel_id=1, source_target_pairs={{0,1},{1,2},{2,3},{4,5},{5,6},{6,7},{8,9},{9,10},{10,11},{12,13},{... | collective-permute-start | bytes 1376264 | tf_op jit(solution)/shard_map/ppermute | solution.py:37
  74.6 7.9 %shard_map.197 = (bf16[768,512]{1,0:T(8,128)(2,1)S(1)}, bf16[512,768]{1,0:T(8,128)(2,1)S(1)}, bf16[512,1536]{1,0:T(8,128)(2,1)S(1)}, bf16[1536,512]{1,0:T(8,128)...) custom-call(s32[1]{0:T(128)} %bitcast.10.place, ...), custom_call_target="tpu_custom_call" | custom-call | flops 17999998976 | bytes 54000000 | tf_op jit(solution)/shard_map/pallas_call | solution.py:895
  84.0 6.9 %collective-permute-start.17 = (bf16[2,896,128]{2,1,0:T(8,128)(2,1)S(1)}, bf16[2,896,128]{2,1,0:T(8,128)(2,1)S(1)}, u32[]{:S(2)}, u32[]{:S(2)}) collective-permute-start(bf16[2,896,128]{2,1,0:T(8,128)(2,1)S(1)} %add_convert_fusion.1), channel_id=1, source_target_pairs={{0,2},{1,3},{4,6},{5,7},{8,10},{9,11},{12,14},{13,15},{16,18},{17,... | collective-permute-start | bytes 1376264 | tf_op jit(solution)/shard_map/ppermute | solution.py:37
  98.1 11.6 %collective-permute-done.17.refs_1_ = bf16[2,896,128]{2,1,0:T(8,128)(2,1)S(1)} collective-permute-done((bf16[2,896,128]{2,1,0:T(8,128)(2,1)S(1)}, bf16[2,896,128]{2,1,0:T(8,128)(2,1)S(1)}, u32[]{:S(2)}, u32[]{:S(2)}) %collective-permute-start.17) | collective-permute-done | bytes 458784 | tf_op jit(solution)/shard_map/ppermute | solution.py:37
  109.7 5.0 %shard_map.198 = (bf16[512,768]{1,0:T(8,128)(2,1)S(1)}, f32[512,768]{1,0:T(8,128)S(1)}, f32[512,768]{1,0:T(8,128)S(1)}, bf16[512,768]{1,0:T(8,128)(2,1)S(1)}, bf16[768,512]{1,0:T(8,128)(2,1)S(1)}) custom-call(bf16[512,768]{1,0:T(8,128)(2,1)S(1)} %bitcast.44, f32[4,768]{1,0:T(4,128)S(1)} %reshape.86.vectors, f32[2,256,1536]{2,1,0:T(8,128)S(1)} %get-tuple-element.170.partial, ...), custom_call_target="tpu_custom_call" | custom-call | flops 10000000000 | bytes 30000000 | tf_op jit(solution)/shard_map/pallas_call | solution.py:913
  117.2 20.0 %shard_map.199 = (f32[512,768]{1,0:T(8,128)S(1)}, bf16[512,768]{1,0:T(8,128)(2,1)S(1)}, f32[512,768]{1,0:T(8,128)S(1)}, bf16[512,768]{1,0:T(8,128)(2,1)S(1)}, bf...) custom-call(bf16[512,768]{1,0:T(8,128)(2,1)S(1)} %get-tuple-element., ...), custom_call_target="tpu_custom_call" | custom-call | flops 40000000000 | bytes 120000000 | tf_op jit(solution)/shard_map/pallas_call | solution.py:935
  145.3 6.9 %shard_map.201 = (bf16[1536,384]{1,0:T(8,128)(2,1)S(1)}, bf16[1536,384]{1,0:T(8,128)(2,1)S(1)}, bf16[1536,384]{1,0:T(8,128)(2,1)S(1)}, bf16[768,384]{1,0:T(8,128)(2,1)S(1)}, bf16[768,384]{1,0:T(8,128)(2,1)S(1)}) custom-call(bf16[768,512]{1,0:T(8,128)(2,1)S(1)} %get-tuple-element.187.second_t, bf16[768,512]{1,0:T(8,128)(2,1)S(1)} %get-tuple-element.188.second_other_t, ...), custom_call_target="tpu_custom_call" | custom-call | flops 14000000000 | bytes 42000000 | tf_op jit(solution)/shard_map/pallas_call | solution.py:981
  152.3 4.8 %collective-permute-done.26.refs_0_ = bf16[2,896,128]{2,1,0:T(8,128)(2,1)S(1)} collective-permute-done((bf16[2,896,128]{2,1,0:T(8,128)(2,1)S(1)}, bf16[2,896,128]{2,1,0:T(8,128)(2,1)S(1)}, u32[]{:S(2)}, u32[]{:S(2)}) %collective-permute-start.26) | collective-permute-done | bytes 458784 | tf_op jit(solution)/shard_map/ppermute | solution.py:37
  159.2 11.1 %shard_map.202 = (f32[1536,512]{1,0:T(8,128)S(1)}, f32[512,768]{1,0:T(8,128)S(1)}, bf16[512,768]{1,0:T(8,128)(2,1)S(1)}, f32[768,128]{1,0:T(8,128)S(1)}, bf16[768,512]{1,0:T(8,128)(2,1)}) custom-call(bf16[512,768]{1,0:T(8,128)(2,1)S(1)} %get-tuple-element.164.queries, bf16[512,1536]{1,0:T(8,128)(2,1)S(1)} %get-tuple-element.162.keyed, ...), custom_call_target="tpu_custom_call" | custom-call | flops 20000000000 | bytes 60000000 | tf_op jit(solution)/shard_map/pallas_call | solution.py:989
  173.2 6.0 %shard_map.204 = (bf16[512,1536]{1,0:T(8,128)(2,1)S(1)}, f32[768,128]{1,0:T(8,128)S(1)}, bf16[4,512,384]{2,1,0:T(8,128)(2,1)S(1)}, bf16[768,512]{1,0:T(8,128)(2,1)}) custom-call(s32[1]{0:T(128)} %bitcast.10.place, bf16[512,1536]{1,0:T(8,128)(2,1)S(1)} %get-tuple-element.162.keyed, bf16[512,1536]{1,0:T(8,128)(2,1)S(1)} %get-tuple-element.194.fk, ...), custom_call_target="tpu_custom_call" | custom-call | flops 14000000000 | bytes 42000000 | tf_op jit(solution)/shard_map/pallas_call | solution.py:1006
  181.7 5.9 %shard_map.205 = (bf16[512,768]{1,0:T(8,128)(2,1)}, bf16[512,768]{1,0:T(8,128)(2,1)}, bf16[4,240,128]{2,1,0:T(8,128)(2,1)S(1)}) custom-call(bf16[512,768]{1,0:T(8,128)(2,1)S(1)} %bitcast.45, f32[4,768]{1,0:T(4,128)S(1)} %reshape.86.vectors, bf16[512,768]{1,0:T(8,128)(2,1)S(1)} %get-tuple-element.197.d_queries, ...), custom_call_target="tpu_custom_call" | custom-call | flops 14000000000 | bytes 42000000 | tf_op jit(solution)/shard_map/pallas_call | solution.py:1018
  187.6 8.7 %collective-permute-done.32.refs_1_ = bf16[1536,384]{1,0:T(8,128)(2,1)S(1)} collective-permute-done((bf16[1536,384]{1,0:T(8,128)(2,1)S(1)}, bf16[1536,384]{1,0:T(8,128)(2,1)S(1)}, u32[]{:S(2)}, u32[]{:S(2)}) %collective-permute-start.32) | collective-permute-done | bytes 1179680 | tf_op jit(solution)/shard_map/ppermute | solution.py:26
  197.8 5.0 %shard_map.207 = (bf16[832,384]{1,0:T(8,128)(2,1)S(1)}, bf16[832,384]{1,0:T(8,128)(2,1)S(1)}, bf16[832,384]{1,0:T(8,128)(2,1)S(1)}, bf16[416,384]{1,0:T(8,128)(2,1)S(1)}, bf16[416,384]{1,0:T(8,128)(2,1)S(1)}) custom-call(s32[1]{0:T(128)} %bitcast.10.place, bf16[512,768]{1,0:T(8,128)(2,1)S(1)} %get-tuple-element.197.d_queries, ...), custom_call_target="tpu_custom_call" | custom-call | flops 14000000000 | bytes 42000000 | tf_op jit(solution)/shard_map/pallas_call | solution.py:1043
  215.5 7.8 %collective-permute-done.37.refs_1_ = bf16[832,384]{1,0:T(8,128)(2,1)S(1)} collective-permute-done((bf16[832,384]{1,0:T(8,128)(2,1)S(1)}, bf16[832,384]{1,0:T(8,128)(2,1)S(1)}, u32[]{:S(2)}, u32[]{:S(2)}) %collective-permute-start.37) | collective-permute-done | bytes 639008 | tf_op jit(solution)/shard_map/ppermute | solution.py:26
  223.5 10.3 %collective-permute-done.39.refs_1_ = bf16[384,384]{1,0:T(8,128)(2,1)S(1)} collective-permute-done((bf16[384,384]{1,0:T(8,128)(2,1)S(1)}, bf16[384,384]{1,0:T(8,128)(2,1)S(1)}, u32[]{:S(2)}, u32[]{:S(2)}) %collective-permute-start.39) | collective-permute-done | bytes 294944 | tf_op jit(solution)/shard_map/ppermute | solution.py:31
  236.6 4.1 %collective-permute-done.48 = bf16[384,384]{1,0:T(8,128)(2,1)S(1)} collective-permute-done((bf16[384,384]{1,0:T(8,128)(2,1)S(1)}, bf16[384,384]{1,0:T(8,128)(2,1)S(1)}, u32[]{:S(2)}, u32[]{:S(2)}) %collective-permute-start.48) | collective-permute-done | bytes 294944 | tf_op jit(solution)/shard_map/ppermute | solution.py:26
  240.8 7.3 %collective-permute-done.50 = bf16[384,384]{1,0:T(8,128)(2,1)S(1)} collective-permute-done((bf16[384,384]{1,0:T(8,128)(2,1)S(1)}, bf16[384,384]{1,0:T(8,128)(2,1)S(1)}, u32[]{:S(2)}, u32[]{:S(2)}) %collective-permute-start.50) | collective-permute-done | bytes 294944 | tf_op jit(solution)/shard_map/ppermute | solution.py:26
  257.1 8.2 %collective-permute-done.42.refs_1_ = bf16[208,384]{1,0:T(8,128)(2,1)S(1)} collective-permute-done((bf16[208,384]{1,0:T(8,128)(2,1)S(1)}, bf16[208,384]{1,0:T(8,128)(2,1)S(1)}, u32[]{:S(2)}, u32[]{:S(2)}) %collective-permute-start.42) | collective-permute-done | bytes 159776 | tf_op jit(solution)/shard_map/ppermute | solution.py:31
  265.2 4.2 %collective-permute-done.43.refs_2_ = bf16[208,384]{1,0:T(8,128)(2,1)S(1)} collective-permute-done((bf16[208,384]{1,0:T(8,128)(2,1)S(1)}, bf16[208,384]{1,0:T(8,128)(2,1)S(1)}, u32[]{:S(2)}, u32[]{:S(2)}) %collective-permute-start.43) | collective-permute-done | bytes 159776 | tf_op jit(solution)/shard_map/ppermute | solution.py:31
  (145 shorter events, 104.1 us)
Async XLA Ops:
  4.6 16.8 %collective-permute-start.1 = (bf16[264,384]{1,0:T(8,128)(2,1)S(1)}, bf16[264,384]{1,0:T(8,128)(2,1)S(1)}, u32[]{:S(2)}, u32[]{:S(2)}) collective-permute-start(bf16[264,384]{1,0:T(8,128)(2,1)S(1)} %maximum_maximum_fusion.refs_0_), channel_id=1, source_target_pairs={{0,2},{1,3},{2,0},{3,1},{4,6},{5,7},{6,4},{7,5},{8,10},{9,11},{10,... | collective-permute-start | bytes 608264 | tf_op jit(solution)/shard_map/ppermute | solution.py:31
  5.7 24.8 %collective-permute-start.2 = (bf16[264,384]{1,0:T(8,128)(2,1)S(1)}, bf16[264,384]{1,0:T(8,128)(2,1)S(1)}, u32[]{:S(2)}, u32[]{:S(2)}) collective-permute-start(bf16[264,384]{1,0:T(8,128)(2,1)S(1)} %maximum_maximum_fusion.refs_0_), channel_id=1, source_target_pairs={{0,3},{1,0},{2,1},{3,2},{4,7},{5,4},{6,5},{7,6},{8,11},{9,8},{10,9... | collective-permute-start | bytes 608264 | tf_op jit(solution)/shard_map/ppermute | solution.py:31
  12.5 19.4 %collective-permute-start.3 = (bf16[384,384]{1,0:T(8,128)(2,1)S(1)}, bf16[384,384]{1,0:T(8,128)(2,1)S(1)}, u32[]{:S(2)}, u32[]{:S(2)}) collective-permute-start(bf16[384,384]{1,0:T(8,128)(2,1)S(1)} %pad_maximum_fusion.2), channel_id=1, source_target_pairs={{0,1},{1,2},{2,3},{3,0},{4,5},{5,6},{6,7},{7,4},{8,9},{9,10},{10,1... | collective-permute-start | bytes 884744 | tf_op jit(solution)/shard_map/ppermute | solution.py:31
  32.0 14.7 %collective-permute-start.4 = (bf16[768,384]{1,0:T(8,128)(2,1)}, bf16[768,384]{1,0:T(8,128)(2,1)S(1)}, u32[]{:S(2)}, u32[]{:S(2)}) collective-permute-start(bf16[768,384]{1,0:T(8,128)(2,1)} %bitcast.6.refs_0_), channel_id=1, source_target_pairs={{0,8},{4,12},{8,0},{12,4},{16,24},{20,28},{24,16},{28,20},{1,9},{5... | collective-permute-start | bytes 1769480 | tf_op jit(solution)/shard_map/ppermute | solution.py:26
  33.2 14.3 %collective-permute-start.5 = (bf16[768,384]{1,0:T(8,128)(2,1)}, bf16[768,384]{1,0:T(8,128)(2,1)S(1)}, u32[]{:S(2)}, u32[]{:S(2)}) collective-permute-start(bf16[768,384]{1,0:T(8,128)(2,1)} %bitcast.6.refs_0_), channel_id=1, source_target_pairs={{0,16},{4,20},{8,24},{12,28},{16,0},{20,4},{24,8},{28,12},{1,17},{... | collective-permute-start | bytes 1769480 | tf_op jit(solution)/shard_map/ppermute | solution.py:26
  68.9 27.3 %collective-permute-start.14 = (bf16[1536,384]{1,0:T(8,128)(2,1)S(1)}, bf16[1536,384]{1,0:T(8,128)(2,1)S(1)}, u32[]{:S(2)}, u32[]{:S(2)}) collective-permute-start(bf16[1536,384]{1,0:T(8,128)(2,1)S(1)} %bitcast.36), channel_id=1, source_target_pairs={{0,8},{4,12},{8,0},{12,4},{16,24},{20,28},{24,16},{28,20},{1,9},{5... | collective-permute-start | bytes 3538952 | tf_op jit(solution)/shard_map/ppermute | solution.py:26
  70.0 26.9 %collective-permute-start.15 = (bf16[1536,384]{1,0:T(8,128)(2,1)S(1)}, bf16[1536,384]{1,0:T(8,128)(2,1)S(1)}, u32[]{:S(2)}, u32[]{:S(2)}) collective-permute-start(bf16[1536,384]{1,0:T(8,128)(2,1)S(1)} %bitcast.37), channel_id=1, source_target_pairs={{0,16},{4,20},{8,24},{12,28},{16,0},{20,4},{24,8},{28,12},{1,17},{... | collective-permute-start | bytes 3538952 | tf_op jit(solution)/shard_map/ppermute | solution.py:26
  70.7 13.2 %collective-permute-start.16 = (bf16[2,896,128]{2,1,0:T(8,128)(2,1)S(1)}, bf16[2,896,128]{2,1,0:T(8,128)(2,1)S(1)}, u32[]{:S(2)}, u32[]{:S(2)}) collective-permute-start(bf16[2,896,128]{2,1,0:T(8,128)(2,1)S(1)} %get-tuple-element.167), channel_id=1, source_target_pairs={{0,1},{1,2},{2,3},{4,5},{5,6},{6,7},{8,9},{9,10},{10,11},{12,13},{... | collective-permute-start | bytes 1376264 | tf_op jit(solution)/shard_map/ppermute | solution.py:37
  84.0 25.7 %collective-permute-start.17 = (bf16[2,896,128]{2,1,0:T(8,128)(2,1)S(1)}, bf16[2,896,128]{2,1,0:T(8,128)(2,1)S(1)}, u32[]{:S(2)}, u32[]{:S(2)}) collective-permute-start(bf16[2,896,128]{2,1,0:T(8,128)(2,1)S(1)} %add_convert_fusion.1), channel_id=1, source_target_pairs={{0,2},{1,3},{4,6},{5,7},{8,10},{9,11},{12,14},{13,15},{16,18},{17,... | collective-permute-start | bytes 1376264 | tf_op jit(solution)/shard_map/ppermute | solution.py:37
  90.9 24.5 %collective-permute-start.19 = (bf16[512,768]{1,0:T(8,128)(2,1)S(1)}, bf16[512,768]{1,0:T(8,128)(2,1)S(1)}, u32[]{:S(2)}, u32[]{:S(2)}) collective-permute-start(bf16[512,768]{1,0:T(8,128)(2,1)S(1)} %bitcast.39), channel_id=1, source_target_pairs={{0,4},{4,0},{8,12},{12,8},{16,20},{20,16},{24,28},{28,24},{1,5},{5... | collective-permute-start | bytes 2359304 | tf_op jit(solution)/shard_map/ppermute | solution.py:26
  97.0 18.3 %collective-permute-start.20 = (bf16[768,384]{1,0:T(8,128)(2,1)S(1)}, bf16[768,384]{1,0:T(8,128)(2,1)S(1)}, u32[]{:S(2)}, u32[]{:S(2)}) collective-permute-start(bf16[768,384]{1,0:T(8,128)(2,1)S(1)} %slice.68), channel_id=1, source_target_pairs={{0,16},{4,20},{8,24},{12,28},{16,0},{20,4},{24,8},{28,12},{1,17},{... | collective-permute-start | bytes 1769480 | tf_op jit(solution)/shard_map/ppermute | solution.py:26
  97.7 17.6 %collective-permute-start.21 = (bf16[768,384]{1,0:T(8,128)(2,1)S(1)}, bf16[768,384]{1,0:T(8,128)(2,1)S(1)}, u32[]{:S(2)}, u32[]{:S(2)}) collective-permute-start(bf16[768,384]{1,0:T(8,128)(2,1)S(1)} %slice.69), channel_id=1, source_target_pairs={{0,8},{4,12},{8,0},{12,4},{16,24},{20,28},{24,16},{28,20},{1,9},{5... | collective-permute-start | bytes 1769480 | tf_op jit(solution)/shard_map/ppermute | solution.py:26
  143.4 13.6 %collective-permute-start.26 = (bf16[2,896,128]{2,1,0:T(8,128)(2,1)S(1)}, bf16[2,896,128]{2,1,0:T(8,128)(2,1)S(1)}, u32[]{:S(2)}, u32[]{:S(2)}) collective-permute-start(bf16[2,896,128]{2,1,0:T(8,128)(2,1)S(1)} %get-tuple-element.183), channel_id=1, source_target_pairs={{1,0},{2,1},{3,2},{5,4},{6,5},{7,6},{9,8},{10,9},{11,10},{13,12},{... | collective-permute-start | bytes 1376264 | tf_op jit(solution)/shard_map/ppermute | solution.py:37
  157.1 13.7 %collective-permute-start.27 = (bf16[768,384]{1,0:T(8,128)(2,1)S(1)}, bf16[768,384]{1,0:T(8,128)(2,1)S(1)}, u32[]{:S(2)}, u32[]{:S(2)}) collective-permute-start(bf16[768,384]{1,0:T(8,128)(2,1)S(1)} %get-tuple-element.203), channel_id=1, source_target_pairs={{0,16},{4,20},{8,24},{12,28},{16,0},{20,4},{24,8},{28,12},{1,17},{... | collective-permute-start | bytes 1769480 | tf_op jit(solution)/shard_map/ppermute | solution.py:26
  157.4 13.4 %collective-permute-start.28 = (bf16[768,384]{1,0:T(8,128)(2,1)S(1)}, bf16[768,384]{1,0:T(8,128)(2,1)S(1)}, u32[]{:S(2)}, u32[]{:S(2)}) collective-permute-start(bf16[768,384]{1,0:T(8,128)(2,1)S(1)} %get-tuple-element.204), channel_id=1, source_target_pairs={{0,8},{4,12},{8,0},{12,4},{16,24},{20,28},{24,16},{28,20},{1,9},{5... | collective-permute-start | bytes 1769480 | tf_op jit(solution)/shard_map/ppermute | solution.py:26
  157.7 15.5 %collective-permute-start.29 = (bf16[2,896,128]{2,1,0:T(8,128)(2,1)S(1)}, bf16[2,896,128]{2,1,0:T(8,128)(2,1)S(1)}, u32[]{:S(2)}, u32[]{:S(2)}) collective-permute-start(bf16[2,896,128]{2,1,0:T(8,128)(2,1)S(1)} %add_convert_fusion), channel_id=1, source_target_pairs={{2,0},{3,1},{6,4},{7,5},{10,8},{11,9},{14,12},{15,13},{18,16},{19,... | collective-permute-start | bytes 1376264 | tf_op jit(solution)/shard_map/ppermute | solution.py:37
  171.2 25.2 %collective-permute-start.32 = (bf16[1536,384]{1,0:T(8,128)(2,1)S(1)}, bf16[1536,384]{1,0:T(8,128)(2,1)S(1)}, u32[]{:S(2)}, u32[]{:S(2)}) collective-permute-start(bf16[1536,384]{1,0:T(8,128)(2,1)S(1)} %get-tuple-element.223), channel_id=1, source_target_pairs={{0,8},{4,12},{8,0},{12,4},{16,24},{20,28},{24,16},{28,20},{1,9},{5... | collective-permute-start | bytes 3538952 | tf_op jit(solution)/shard_map/ppermute | solution.py:26
  172.0 25.3 %collective-permute-start.33 = (bf16[1536,384]{1,0:T(8,128)(2,1)S(1)}, bf16[1536,384]{1,0:T(8,128)(2,1)S(1)}, u32[]{:S(2)}, u32[]{:S(2)}) collective-permute-start(bf16[1536,384]{1,0:T(8,128)(2,1)S(1)} %get-tuple-element.224), channel_id=1, source_target_pairs={{0,16},{4,20},{8,24},{12,28},{16,0},{20,4},{24,8},{28,12},{1,17},{... | collective-permute-start | bytes 3538952 | tf_op jit(solution)/shard_map/ppermute | solution.py:26
  179.3 18.5 %collective-permute-start.30 = (bf16[4,512,384]{2,1,0:T(8,128)(2,1)S(1)}, bf16[4,512,384]{2,1,0:T(8,128)(2,1)S(1)}, u32[]{:S(2)}, u32[]{:S(2)}) collective-permute-start(bf16[4,512,384]{2,1,0:T(8,128)(2,1)S(1)} %get-tuple-element.220), channel_id=1, source_target_pairs={{0,4},{4,0},{8,12},{12,8},{16,20},{20,16},{24,28},{28,24},{1,5},{5... | collective-permute-start | bytes 4718600 | tf_op jit(solution)/shard_map/ppermute | solution.py:26
  212.1 21.7 %collective-permute-start.39 = (bf16[384,384]{1,0:T(8,128)(2,1)S(1)}, bf16[384,384]{1,0:T(8,128)(2,1)S(1)}, u32[]{:S(2)}, u32[]{:S(2)}) collective-permute-start(bf16[384,384]{1,0:T(8,128)(2,1)S(1)} %get-tuple-element.248), channel_id=1, source_target_pairs={{0,2},{1,3},{2,0},{3,1},{4,6},{5,7},{6,4},{7,5},{8,10},{9,11},{10,... | collective-permute-start | bytes 884744 | tf_op jit(solution)/shard_map/ppermute | solution.py:31
  214.8 18.9 %collective-permute-start.40 = (bf16[384,384]{1,0:T(8,128)(2,1)S(1)}, bf16[384,384]{1,0:T(8,128)(2,1)S(1)}, u32[]{:S(2)}, u32[]{:S(2)}) collective-permute-start(bf16[384,384]{1,0:T(8,128)(2,1)S(1)} %get-tuple-element.249), channel_id=1, source_target_pairs={{0,3},{1,0},{2,1},{3,2},{4,7},{5,4},{6,5},{7,6},{8,11},{9,8},{10,9... | collective-permute-start | bytes 884744 | tf_op jit(solution)/shard_map/ppermute | solution.py:31
  248.7 32.0 %collective-permute-start.51 = (bf16[4,384,384]{2,1,0:T(8,128)(2,1)S(1)}, bf16[4,384,384]{2,1,0:T(8,128)(2,1)S(1)}, u32[]{:S(2)}, u32[]{:S(2)}) collective-permute-start(bf16[4,384,384]{2,1,0:T(8,128)(2,1)S(1)} %shard_map.213.even), channel_id=1, source_target_pairs={{0,4},{4,0},{8,12},{12,8},{16,20},{20,16},{24,28},{28,24},{1,5},{5... | collective-permute-start | bytes 3538952 | tf_op jit(solution)/shard_map/ppermute | solution.py:26
  251.4 13.8 %collective-permute-start.42 = (bf16[208,384]{1,0:T(8,128)(2,1)S(1)}, bf16[208,384]{1,0:T(8,128)(2,1)S(1)}, u32[]{:S(2)}, u32[]{:S(2)}) collective-permute-start(bf16[208,384]{1,0:T(8,128)(2,1)S(1)} %get-tuple-element.252), channel_id=1, source_target_pairs={{0,2},{1,3},{2,0},{3,1},{4,6},{5,7},{6,4},{7,5},{8,10},{9,11},{10,... | collective-permute-start | bytes 479240 | tf_op jit(solution)/shard_map/ppermute | solution.py:31
  254.5 14.9 %collective-permute-start.43 = (bf16[208,384]{1,0:T(8,128)(2,1)S(1)}, bf16[208,384]{1,0:T(8,128)(2,1)S(1)}, u32[]{:S(2)}, u32[]{:S(2)}) collective-permute-start(bf16[208,384]{1,0:T(8,128)(2,1)S(1)} %get-tuple-element.253), channel_id=1, source_target_pairs={{0,3},{1,0},{2,1},{3,2},{4,7},{5,4},{6,5},{7,6},{8,11},{9,8},{10,9... | collective-permute-start | bytes 479240 | tf_op jit(solution)/shard_map/ppermute | solution.py:31
  (32 other events, 251.9 us)
where the time goes:
time: 287 us
  waiting for transfers between devices  119 us (41%)
  Pallas kernels  89.1 us (31%)
  starting transfers between devices  62.2 us (22%)
  local copies, waits for them, and re-layouts  10.5 us (4%)
  other arithmetic  5.09 us (2%)
    ppermute x36, waiting for transfers between devices, flip(): return lax.ppermute(value, 'rep', [(i, i ^ bit) for i in range(count)])  55.2 us
    ppermute x12, waiting for transfers between devices, spin(): lax.ppermute(value, 'shard', [(i, (i + step) % count) for i in range(coun...  45.6 us
    ppermute x36, starting transfers between devices, flip(): return lax.ppermute(value, 'rep', [(i, i ^ bit) for i in range(count)])  33.6 us
    pallas_call x1, Pallas kernels, shards(): call(mlp_kernel, 20, (whole((count, D), wide_type), whole((count, D)), wh...  20 us
    ppermute x4, waiting for transfers between devices, slide(): return lax.ppermute(value, 'shard', pairs)  17.7 us
    ppermute x12, starting transfers between devices, spin(): lax.ppermute(value, 'shard', [(i, (i + step) % count) for i in range(coun...  14.3 us
    ppermute x4, starting transfers between devices, slide(): return lax.ppermute(value, 'shard', pairs)  14.2 us
    pallas_call x1, Pallas kernels, shards(): call(local_kernel, 10, (whole((HEADS * FEAT, count), wide_type), whole((c...  11.1 us
  transfers between devices with their start and end apart: 52, of which 29 were waited for; matrix products, arithmetic and copies ran while one was open for 4% of the time, Pallas kernels for 18%

commit v1 on v0

--- a/solution.py
+++ b/solution.py
@@ -97,8 +97,11 @@
     return jnp.concatenate([flip(halves[0], 4), flip(halves[1], 2)], axis=0)
 
 
-def share(own):
-    parts = [own[None]] + [flip(own, bit)[None] for bit in (2, 4, 6)]
+def share_flips(own):
+    return [own[None]] + [flip(own, bit)[None] for bit in (2, 4, 6)]
+
+
+def share_pair(parts):
     even = place_parts(parts, [0, 1, 2, 3])
     return even, flip(even, 1)
 
@@ -226,6 +229,35 @@
     packed = added(refs, b, pl.ds(aligned(p, FEAT), FEAT))
     sums = low(added(refs, b, slice(PAIRS * FEAT, SLAB)))
     return unpack_state(packed, sums, p)
+
+
+def maps_kernel(small, maps, vectors, weight):
+    shard_count, size, _ = small.shape
+    rows = D // shard_count
+    lines = 4 * rows // FEAT
+    for s in range(shard_count):
+        for j in range(3):
+            count = min(size, rows - j * size)
+            if count > 0:
+                weight[s * rows + j * size : s * rows + j * size + count, :] = wide(
+                    small[s, :count, j * FEAT : (j + 1) * FEAT]
+                )
+        flat = []
+        for line in range(rows, rows + lines):
+            j, row = line // size, line % size
+            flat.append(wide(small[s, row : row + 1, j * FEAT : (j + 1) * FEAT]))
+        flat = jnp.concatenate(flat, axis=1)
+        for v in range(4):
+            vectors[v : v + 1, s * rows : (s + 1) * rows] = flat[:, v * rows : (v + 1) * rows]
+    gap = jnp.zeros((HEAD, HEAD), low_type)
+    for head in range(HEADS):
+        turned = low(weight[head * HEAD : (head + 1) * HEAD, :].T)
+        g, a = head // 4, head % 4
+        for which in range(2):
+            block = turned[which * HEAD : (which + 1) * HEAD]
+            maps[which * (D // GROUP) + g, a * HEAD : (a + 1) * HEAD, :] = jnp.concatenate(
+                [block if a == b else gap for b in range(4)], axis=1
+            )
 
 
 def features(maps, base, columns, f_t, f):
@@ -390,7 +422,7 @@
 def mlp_kernel(second, second_other, cotangent, cotangent_other, resid, attended, *refs):
     pieces = refs[:4]
     out_sum, out_send, back_sum, back_send, hiddens, d_pres, second_other_t, attended_t = refs[4:12]
-    out_other, back_other, up, down, ready = refs[12:]
+    up, down, ready = refs[12:]
     count = second.shape[0]
     parts = grads_layout(second.shape[1], pieces[0].shape[0])
 
@@ -398,9 +430,10 @@
         listed = []
         for i, (src, dst) in enumerate(parts):
             if dst[0] == "up":
-                target = up.at[k, pl.ds(dst[1], dst[2]), :]
+                target = up.at[pl.ds(dst[1], dst[2]), chunk_at(k)]
             else:
-                target = down.at[k, pl.ds(dst[1], dst[2]), pl.ds(dst[3], CHUNK)]
+                start = pl.multiple_of(k * CHUNK + dst[1], dst[2])
+                target = down.at[pl.ds(start, dst[2]), pl.ds(dst[3], CHUNK)]
             listed.append(
                 pltpu.make_async_copy(source.at[pl.ds(src, dst[2]), :], target, ready.at[k, i])
             )
@@ -409,39 +442,45 @@
     for k in range(4):
         for copy in copies(k, pieces[k]):
             copy.start()
-    out_sum[...] = resid[...]
-    for total in (out_other, back_sum, back_other):
-        total[...] = jnp.zeros_like(total)
     second_other_t[...] = second_other[...].T
     attended_t[...] = attended[...].T
-    sides = (
-        (second, cotangent, out_sum, back_sum),
-        (second_other, cotangent_other, out_other, back_other),
-    )
 
     def piece(k, carry):
         for copy in copies(k, pieces[0]):
             copy.wait()
-        for side, (source, grad, out_total, back_total) in enumerate(sides):
+        columns = chunk_at(k)
+        for side, (source, grad) in enumerate(
+            ((second, cotangent), (second_other, cotangent_other))
+        ):
             here = slice(side * count, (side + 1) * count)
-            pre = dot(source[...], up[k])
+            pre = dot(source[...], up[:, columns])
             square = pre * pre
-            bent = jnp.tanh(0.7978845608 * (pre + 0.044715 * square * pre))
-            half = 0.5 * (1.0 + bent)
-            hidden = low(pre * half)
-            slope = half + (0.5 * 0.7978845608) * pre * (1.0 - bent * bent) * (
-                1.0 + 3.0 * 0.044715 * square
+            bent = jnp.tanh(pre * (0.7978845608 + (0.7978845608 * 0.044715) * square))
+            half = 0.5 + 0.5 * bent
+            slope = half + (half * (1.0 - bent)) * pre * (
+                0.7978845608 + (3.0 * 0.7978845608 * 0.044715) * square
             )
-            hiddens[k, here] = hidden
-            out_total[...] += dot(hidden, down[k])
-            d_pre = low(dot_nt(grad[...], down[k]) * slope)
-            d_pres[k, here] = d_pre
-            back_total[...] += dot_nt(d_pre, up[k])
+            hiddens[here, columns] = low(pre * half)
+            d_pres[here, columns] = low(dot_nt(grad[...], down[columns, :]) * slope)
         return carry
 
     lax.fori_loop(0, 4, piece, 0)
-    out_send[...] = low(out_other[...])
-    back_send[...] = low(back_other[...])
+    tile = count // 2
+
+    def own(i, carry):
+        here = pl.ds(aligned(i, tile), tile)
+        back_sum[here, :] = dot_nt(d_pres[here, :], up[...])
+        out_sum[here, :] = resid[here, :] + dot(hiddens[here, :], down[...])
+        return carry
+
+    def other(i, carry):
+        here, there = pl.ds(aligned(i, tile), tile), pl.ds(aligned(i + 2, tile), tile)
+        back_send[here, :] = low(dot_nt(d_pres[there, :], up[...]))
+        out_send[here, :] = low(dot(hiddens[there, :], down[...]))
+        return carry
+
+    lax.fori_loop(0, 2, own, 0)
+    lax.fori_loop(0, 2, other, 0)
 
 
 def store_piece(outs, made, k):
@@ -464,9 +503,11 @@
     own, other = slice(0, count), slice(count, 2 * count)
 
     def piece(k, carry):
-        d_up = dot(second_t[...], d_pres[k, own]) + dot(second_other_t[...], d_pres[k, other])
-        d_down = dot_tn(hiddens[k, own], cotangent[...])
-        d_down = d_down + dot_tn(hiddens[k, other], cotangent_other[...])
+        columns = chunk_at(k)
+        d_up = dot(second_t[...], d_pres[own, columns])
+        d_up = d_up + dot(second_other_t[...], d_pres[other, columns])
+        d_down = dot_tn(hiddens[own, columns], cotangent[...])
+        d_down = d_down + dot_tn(hiddens[other, columns], cotangent_other[...])
         d_up, d_down = low(d_up), low(d_down)
         for src, dst in grads_layout(second_t.shape[0], made.shape[0]):
             rows = slice(dst[1], dst[1] + dst[2])
@@ -540,8 +581,13 @@
     return low(d_plus - d_minus)
 
 
-def local_kernel(queries, keyed, maps, fq_t, fk, fk_t, d_num, d_den, *refs):
-    priors, (d_fk_t, d_values, d_queries, d_features, d_uq_t) = refs[:-5], refs[-5:]
+def linked(outer, value):
+    link = dot_nt(outer, value)
+    return low(jnp.where(row_index(link.shape) >= lane_index(link.shape), link, 0.0))
+
+
+def local_queries_kernel(queries, keyed, maps, fq_t, fk_t, d_num, d_den, *refs):
+    priors, (d_queries, d_features, d_uq_t) = refs[:-3], refs[-3:]
     seqs = priors[0].shape[0]
     length = keyed.shape[0] // seqs
 
@@ -551,25 +597,40 @@
             values = with_ones(keyed[here, pair_at(VALUES + p)])
             outer = joined(d_num, d_den, here, p)
             states = states_at(priors, b, p)
+            for side in range(2):
+                rows = pair_at(2 * p + side)
+                link = linked(outer[side], values[side])
+                d_q = dot_nt(fk_t[rows, here], link) + dot_nt(states[side], outer[side])
+                d_uq_t[pl.ds(aligned(2 * p + side, HEAD), HEAD), here] = softmax_backward(
+                    fq_t[rows, here], d_q
+                )
+        return carry
+
+    lax.fori_loop(0, PAIRS, pair, 0)
+    feature_backward(d_uq_t, queries, maps, 0, d_queries, d_features, 0)
+
+
+def local_keys_kernel(keyed, fq_t, fk, d_num, d_den, d_fk_t, d_values, *, seqs):
+    length = keyed.shape[0] // seqs
+
+    def pair(p, carry):
+        for b in range(seqs):
+            here = slice(b * length, (b + 1) * length)
+            values = with_ones(keyed[here, pair_at(VALUES + p)])
+            outer = joined(d_num, d_den, here, p)
             found = []
             for side in range(2):
-                rows = pl.ds(aligned(2 * p + side, FEAT), FEAT)
-                q_t, k_t = fq_t[rows, here], fk_t[rows, here]
-                link = dot_nt(outer[side], values[side])
-                row, lane = row_index(link.shape), lane_index(link.shape)
-                link = low(jnp.where(row >= lane, link, 0.0))
-                d_q = dot_nt(k_t, link) + dot_nt(states[side], outer[side])
-                d_uq_t[pl.ds(aligned(2 * p + side, HEAD), HEAD), here] = softmax_backward(q_t, d_q)
-                d_fk_t[rows, here] = dot(q_t, link)
+                rows = pair_at(2 * p + side)
+                q_t = fq_t[rows, here]
+                d_fk_t[rows, here] = dot(q_t, linked(outer[side], values[side]))
                 scores = dot(fk[here, rows], q_t)
-                scores = low(jnp.where(row <= lane, scores, 0.0))
-                found.append(dot(scores, outer[side]))
+                row, lane = row_index(scores.shape), lane_index(scores.shape)
+                found.append(dot(low(jnp.where(row <= lane, scores, 0.0)), outer[side]))
             left = left_half(found[0].shape)
-            d_values[here, pl.ds(aligned(p, FEAT), FEAT)] = jnp.where(left, found[0], found[1])
+            d_values[here, pair_at(p)] = jnp.where(left, found[0], found[1])
         return carry
 
     lax.fori_loop(0, PAIRS, pair, 0)
-    feature_backward(d_uq_t, queries, maps, 0, d_queries, d_features, 0)
 
 
 def feature_backward(d_u_t, source, maps, base, target, d_features, lane):
@@ -685,20 +746,25 @@
     lax.fori_loop(0, PIECES // 2, piece, 0)
 
 
-def input_kernel(tokens, vectors, d_queries, d_keyed, d_resid, out_sum, out_other, *refs):
-    w_q, w_kv, d_features, d_vectors, block_out, grad_tokens, tiny, total = refs
+def early_kernel(d_queries, w_q, total):
     total[...] = jnp.zeros_like(total)
+    add_products(total, d_queries, w_q)
+
+
+def add_products(total, source, weights):
+    def add(index, carry):
+        total[...] += dot_nt(source[:, chunk_at(index)], weights[index])
+        return carry
+
+    lax.fori_loop(0, weights.shape[0], add, 0)
+
+
+def input_kernel(tokens, vectors, early, d_keyed, d_resid, out_sum, out_other, *refs):
+    w_kv, d_features, d_vectors, block_out, grad_tokens, tiny, total = refs
+    total[...] = early[...]
     block_out[...] = low(out_sum[...] + wide(out_other[...]))
 
-    def add_from(source, weights):
-        def add(index, carry):
-            total[...] += dot_nt(source[:, chunk_at(index)], weights[index])
-            return carry
-
-        lax.fori_loop(0, weights.shape[0], add, 0)
-
-    add_from(d_queries, w_q)
-    add_from(d_keyed, w_kv)
+    add_products(total, d_keyed, w_kv)
     normal, scale = normalize(wide(tokens[...]))
     grad = total[...]
     grad_tokens[...] = low(d_resid[...] + norm_backward(grad, normal, scale, vectors[0:1, :]))
@@ -846,28 +912,26 @@
         (whole((shard_count, rows, CHUNK)), whole((shard_count, small_rows, CHUNK))),
         scalar_first(shard_count),
     )(in_slots.astype(jnp.int32), *in_spins)
-    small = jnp.concatenate(jnp.split(small, 3, axis=2), axis=1)
     cotangent_other = flip(flat_cotangent, 1)
-    feature_weight = small[:, :rows].reshape(D, FEAT)
-    vectors = wide(small[:, rows : rows + 4 * rows // FEAT].reshape(shard_count, 4, rows).transpose(1, 0, 2).reshape(4, D))
-    blocks = feature_weight.reshape(D // GROUP, 4, HEAD, 2, HEAD)
-    maps = (
-        jnp.einsum("gaiwo,ab->wgaobi", blocks, jnp.eye(4, dtype=low_type))
-        .reshape(2 * D // GROUP, GROUP, GROUP)
-        .astype(low_type)
-    )
+    in_full, small = lax.optimization_barrier((in_full, small))
+    maps, vectors = call(
+        maps_kernel,
+        15,
+        (whole((2 * D // GROUP, GROUP, GROUP)), whole((4, D), wide_type)),
+        scratch=[pltpu.VMEM((D, FEAT), wide_type)],
+    )(small)
     in_full = in_full.reshape(-1, CHUNK)
+    part_mlp, in_full = lax.optimization_barrier((part_mlp, in_full))
     steps = list(range(1, shard_count))
-    soon = {step: spin(part_mlp, step) for step in steps[:1]}
-    in_full, part_mlp, soon = lax.optimization_barrier((in_full, part_mlp, soon))
     from_x, from_y = sides_of(in_full)
     in_other = flip(in_full, 1)
-    soon.update({step: spin(part_mlp, step) for step in steps[1:2]})
-    in_halves, maps, vectors, soon, part_mlp = lax.optimization_barrier(
-        (halves_of(from_x, from_y), maps, vectors, soon, part_mlp)
-    )
-    soon.update({step: spin(part_mlp, step) for step in steps[2:]})
-    diagonal, soon = lax.optimization_barrier((diagonal_of(in_halves), soon))
+    soon = {step: spin(part_mlp, step) for step in steps[:1] + steps[2:]}
+    in_halves, maps, vectors, soon = lax.optimization_barrier(
+        (halves_of(from_x, from_y), maps, vectors, soon)
+    )
+    soon.update({step: spin(soon[1], 1) for step in steps[1:2]})
+    diagonal = diagonal_of(in_halves)
+    diagonal, soon = lax.optimization_barrier((diagonal, soon))
     in_even = [in_full, from_x, from_y, diagonal]
     in_pieces = interleave(in_even, [in_other] + [flip(part, 1) for part in in_even[1:]])
     here = lax.axis_index("shard")
@@ -940,17 +1004,15 @@
             whole((count, D)),
             whole((count, D), wide_type),
             whole((count, D)),
-            whole((4, 2 * count, CHUNK)),
-            whole((4, 2 * count, CHUNK)),
+            whole((2 * count, 4 * CHUNK)),
+            whole((2 * count, 4 * CHUNK)),
             whole((D, count)),
             whole((D, count)),
         ),
         [pl.BlockSpec(memory_space=pltpu.VMEM)] * 6 + anywhere[:4],
         [
-            pltpu.VMEM((count, D), wide_type),
-            pltpu.VMEM((count, D), wide_type),
-            pltpu.VMEM((4, D, CHUNK), low_type),
-            pltpu.VMEM((4, CHUNK, D), low_type),
+            pltpu.VMEM((D, 4 * CHUNK), low_type),
+            pltpu.VMEM((4 * CHUNK, D), low_type),
             pltpu.SemaphoreType.DMA((4, 3 * shard_count)),
         ],
         limit=18,
@@ -981,28 +1043,28 @@
     mlp_grads = call(
         mlp_grads_kernel, 7, piece(2 * D), scratch=[pltpu.VMEM((2 * D, CHUNK), low_type)]
     )(second_t, second_other_t, flat_cotangent, cotangent_other, hiddens, d_pres)
-    mlp_upper, mlp_lower, running, fk = lax.optimization_barrier(
-        (mlp_grads[3], mlp_grads[4], running, fk)
-    )
+    mlp_to_x, mlp_to_y = flip(mlp_grads[3], 4), flip(mlp_grads[4], 2)
+    running, fk_t = lax.optimization_barrier((running, fk_t))
     laters = scan_rest(later, running, -1)
-    mlp_to_x, mlp_to_y = flip(mlp_upper, 4), flip(mlp_lower, 2)
-    d_fk_t, d_values, d_queries, d_half, _ = call(
-        local_kernel,
-        10,
-        (
-            whole((HEADS * FEAT, count), wide_type),
-            whole((count, D), wide_type),
-            whole((count, D)),
-            whole((D, FEAT), wide_type),
-            whole((D, count)),
-        ),
-    )(queries, keyed, maps, fq_t, fk, fk_t, d_num, d_den, *priors)
+    d_queries, d_half, _ = call(
+        local_queries_kernel,
+        6,
+        (whole((count, D)), whole((D, FEAT), wide_type), whole((D, count))),
+    )(queries, keyed, maps, fq_t, fk_t, d_num, d_den, *priors)
+    mlp_to_x, mlp_to_y, d_half = lax.optimization_barrier((mlp_to_x, mlp_to_y, d_half))
     add_sides = lambda parts, to_x, to_y: call(
         sides_kernel, 1, (whole(parts[1].shape), whole(parts[1].shape))
     )(parts[1], parts[2], to_x, to_y)
     mlp_sides = add_sides(mlp_grads, mlp_to_x, mlp_to_y)
-    mlp_sides, d_half = lax.optimization_barrier((mlp_sides, d_half))
+    mlp_sides, d_half, fk = lax.optimization_barrier((mlp_sides, d_half, fk))
+    d_fk_t, d_values = call(
+        lambda *refs: local_keys_kernel(*refs, seqs=seqs),
+        5,
+        (whole((HEADS * FEAT, count), wide_type), whole((count, D), wide_type)),
+    )(keyed, fq_t, fk, d_num, d_den)
     mlp_joined = [flip(mlp_sides[0], 2), flip(mlp_sides[1], 4)]
+    early = call(early_kernel, 2, whole((count, D), wide_type))(d_queries, w_q)
+    early, d_half = lax.optimization_barrier((early, d_half))
     d_keyed, d_features, sends, _ = call(
         mixed_kernel,
         7,
@@ -1027,12 +1089,11 @@
     )(
         flat,
         vectors,
-        d_queries,
+        early,
         d_keyed,
         d_resid,
         out_sum,
         out_other,
-        w_q,
         w_kv,
         d_features,
         d_vectors_two,
@@ -1066,16 +1127,15 @@
     )
     in_to_x, in_to_y = flip(in_grads[3], 4), flip(in_grads[4], 2)
     mlp_received = [spin(part, step + 1) for step, part in enumerate(mlp_blocks[1:])]
-    in_to_x, in_to_y, mlp_received[:1] = lax.optimization_barrier(
-        (in_to_x, in_to_y, mlp_received[:1])
-    )
+    in_to_x, in_to_y, mlp_received[:1] = lax.optimization_barrier((in_to_x, in_to_y, mlp_received[:1]))
     in_sides = add_sides(in_grads, in_to_x, in_to_y)
     in_joined = [flip(in_sides[0], 2), flip(in_sides[1], 4)]
+    in_joined, mlp_received = lax.optimization_barrier((in_joined, mlp_received))
     in_blocks = join_parts([in_grads[0], *in_joined])
-    in_blocks, mlp_received = lax.optimization_barrier((in_blocks, mlp_received))
-    mlp_sums = share(settle(mlp_blocks[0], mlp_received))
     in_received = [spin(part, step + 1) for step, part in enumerate(in_blocks[1:])]
-    in_sums = share(settle(in_blocks[0], in_received))
+    in_received, mlp_received = lax.optimization_barrier((in_received, mlp_received))
+    mlp_sums = share_pair(share_flips(settle(mlp_blocks[0], mlp_received)))
+    in_flips = share_flips(settle(in_blocks[0], in_received))
     grad_up, grad_down = call(
         lay_mlp_kernel,
         3,
@@ -1084,7 +1144,8 @@
         [pltpu.VMEM((PIECES, rows, CHUNK), low_type)],
     )(spot, *mlp_sums)
     grad_down = grad_down.reshape(-1, D)
-    in_sums, grad_up, grad_down = lax.optimization_barrier((in_sums, grad_up, grad_down))
+    in_flips, grad_up, grad_down = lax.optimization_barrier((in_flips, grad_up, grad_down))
+    in_sums = share_pair(in_flips)
     grad_qkv, grad_out, tiny = call(
         lay_in_kernel,
         2,

time: 287 us -> 266 us (0.927)
  waiting for transfers between devices: 119 us -> 113 us
  starting transfers between devices: 62.2 us -> 56.4 us
  local copies, waits for them, and re-layouts: 10.5 us -> 6.85 us
  Pallas kernels: 89.1 us -> 85.7 us
    pallas_call x1 -> x4, Pallas kernels: 11.1 us -> 17.3 us  [the longest x1 8.59 us: shards(): call(lambda *refs: local_keys_kernel(*refs, seqs=seqs), 5, (whole((HEADS...]
    ppermute x36, waiting for transfers between devices: 55.2 us -> 49.8 us  [flip(): return lax.ppermute(value, 'rep', [(i, i ^ bit) for i in range(count)])]
    pallas_call x1, Pallas kernels: 20 us -> 15.1 us  [shards(): call(mlp_kernel, 20, (whole((count, D), wide_type), whole((count, D)), wh...]
    ppermute x4, starting transfers between devices: 14.2 us -> 10.1 us  [slide(): return lax.ppermute(value, 'shard', pairs)]
  transfers between devices with their start and end apart: 52 -> 52, of which waited for: 29 -> 29; matrix products, arithmetic and copies ran while one was open for 4% -> 2% of each run, Pallas kernels for 18% -> 20%
where the time goes in v1:
time: 266 us
  waiting for transfers between devices  113 us (42%)
  Pallas kernels  85.7 us (32%)
  starting transfers between devices  56.4 us (21%)
  local copies, waits for them, and re-layouts  6.85 us (3%)
  other arithmetic  3.08 us (1%)
    ppermute x36, waiting for transfers between devices, flip(): return lax.ppermute(value, 'rep', [(i, i ^ bit) for i in range(count)])  49.8 us
    ppermute x12, waiting for transfers between devices, spin(): lax.ppermute(value, 'shard', [(i, (i + step) % count) for i in range(coun...  46.8 us
    ppermute x36, starting transfers between devices, flip(): return lax.ppermute(value, 'rep', [(i, i ^ bit) for i in range(count)])  31.2 us
    ppermute x4, waiting for transfers between devices, slide(): return lax.ppermute(value, 'shard', pairs)  16 us
    ppermute x12, starting transfers between devices, spin(): lax.ppermute(value, 'shard', [(i, (i + step) % count) for i in range(coun...  15.1 us
    pallas_call x1, Pallas kernels, shards(): call(mlp_kernel, 20, (whole((count, D), wide_type), whole((count, D)), wh...  15.1 us
    ppermute x4, starting transfers between devices, slide(): return lax.ppermute(value, 'shard', pairs)  10.1 us
    pallas_call x1, Pallas kernels, shards(): call(lambda *refs: local_keys_kernel(*refs, seqs=seqs), 5, (whole((HEADS...  8.59 us
  transfers between devices with their start and end apart: 52, of which 29 were waited for; matrix products, arithmetic and copies ran while one was open for 2% of the time, Pallas kernels for 20%

profile of v1, /device:TPU:9, one launch (start us, length us, event | category | flops | bytes accessed | tf_op | source)
XLA Modules:
  0.0 265.7 jit_solution(3172498307506416411)
XLA Ops:
  12.6 8.7 %collective-permute-done.1.refs_2_ = bf16[264,384]{1,0:T(8,128)(2,1)S(1)} collective-permute-done((bf16[264,384]{1,0:T(8,128)(2,1)S(1)}, bf16[264,384]{1,0:T(8,128)(2,1)S(1)}, u32[]{:S(2)}, u32[]{:S(2)}) %collective-permute-start.1) | collective-permute-done | bytes 202784 | tf_op jit(solution)/shard_map/ppermute | solution.py:31
  29.0 10.2 %collective-permute-done.3.refs_2_ = bf16[768,384]{1,0:T(8,128)(2,1)S(1)} collective-permute-done((bf16[768,384]{1,0:T(8,128)(2,1)S(1)}, bf16[768,384]{1,0:T(8,128)(2,1)S(1)}, u32[]{:S(2)}, u32[]{:S(2)}) %collective-permute-start.3) | collective-permute-done | bytes 589856 | tf_op jit(solution)/shard_map/ppermute | solution.py:26
  44.0 5.4 %collective-permute-done.7 = bf16[384,384]{1,0:T(8,128)(2,1)S(1)} collective-permute-done((bf16[384,384]{1,0:T(8,128)(2,1)S(1)}, bf16[384,384]{1,0:T(8,128)(2,1)S(1)}, u32[]{:S(2)}, u32[]{:S(2)}) %collective-permute-start.7) | collective-permute-done | bytes 294944 | tf_op jit(solution)/shard_map/ppermute | solution.py:26
  53.2 6.4 %shard_map.196 = (bf16[512,768]{1,0:T(8,128)(2,1)S(1)}, bf16[512,1536]{1,0:T(8,128)(2,1)S(1)}, bf16[512,1536]{1,0:T(8,128)(2,1)S(1)}, bf16[1536,512]{1,0:T(8,128...) custom-call(s32[1]{0:T(128)} %bitcast.7.place, bf16[512,768]{1,0:T(8,128)(2,1)S(1)} %bitcast.39, ...), custom_call_target="tpu_custom_call" | custom-call | flops 16000000000 | bytes 48000000 | tf_op jit(solution)/shard_map/pallas_call | solution.py:941
  64.4 6.8 %shard_map.198 = (bf16[768,512]{1,0:T(8,128)(2,1)S(1)}, bf16[512,768]{1,0:T(8,128)(2,1)S(1)}, bf16[512,1536]{1,0:T(8,128)(2,1)S(1)}, bf16[1536,512]{1,0:T(8,128)...) custom-call(s32[1]{0:T(128)} %bitcast.7.place, ...), custom_call_target="tpu_custom_call" | custom-call | flops 17999998976 | bytes 54000000 | tf_op jit(solution)/shard_map/pallas_call | solution.py:959
  71.2 5.4 %collective-permute-done.16.refs_0_ = bf16[2,896,128]{2,1,0:T(8,128)(2,1)S(1)} collective-permute-done((bf16[2,896,128]{2,1,0:T(8,128)(2,1)S(1)}, bf16[2,896,128]{2,1,0:T(8,128)(2,1)S(1)}, u32[]{:S(2)}, u32[]{:S(2)}) %collective-permute-start.16) | collective-permute-done | bytes 458784 | tf_op jit(solution)/shard_map/ppermute | solution.py:37
  81.7 5.9 %collective-permute-done.14.refs_1_ = bf16[1536,384]{1,0:T(8,128)(2,1)S(1)} collective-permute-done((bf16[1536,384]{1,0:T(8,128)(2,1)S(1)}, bf16[1536,384]{1,0:T(8,128)(2,1)S(1)}, u32[]{:S(2)}, u32[]{:S(2)}) %collective-permute-start.14) | collective-permute-done | bytes 1179680 | tf_op jit(solution)/shard_map/ppermute | solution.py:26
  89.8 8.6 %collective-permute-done.17.refs_1_ = bf16[2,896,128]{2,1,0:T(8,128)(2,1)S(1)} collective-permute-done((bf16[2,896,128]{2,1,0:T(8,128)(2,1)S(1)}, bf16[2,896,128]{2,1,0:T(8,128)(2,1)S(1)}, u32[]{:S(2)}, u32[]{:S(2)}) %collective-permute-start.17) | collective-permute-done | bytes 458784 | tf_op jit(solution)/shard_map/ppermute | solution.py:37
  98.4 5.0 %shard_map.199 = (bf16[512,768]{1,0:T(8,128)(2,1)S(1)}, f32[512,768]{1,0:T(8,128)S(1)}, f32[512,768]{1,0:T(8,128)S(1)}, bf16[512,768]{1,0:T(8,128)(2,1)S(1)}, bf16[768,512]{1,0:T(8,128)(2,1)S(1)}) custom-call(bf16[512,768]{1,0:T(8,128)(2,1)S(1)} %bitcast.40, f32[4,768]{1,0:T(4,128)S(1)} %get-tuple-element.155.vectors, ...), custom_call_target="tpu_custom_call" | custom-call | flops 10000000000 | bytes 30000000 | tf_op jit(solution)/shard_map/pallas_call | solution.py:977
  105.9 15.1 %shard_map.200 = (f32[512,768]{1,0:T(8,128)S(1)}, bf16[512,768]{1,0:T(8,128)(2,1)S(1)}, f32[512,768]{1,0:T(8,128)S(1)}, bf16[512,768]{1,0:T(8,128)(2,1)S(1)}, bf...) custom-call(bf16[512,768]{1,0:T(8,128)(2,1)S(1)} %get-tuple-element., ...), custom_call_target="tpu_custom_call" | custom-call | flops 40000000000 | bytes 120000000 | tf_op jit(solution)/shard_map/pallas_call | solution.py:999
  123.3 3.9 %shard_map.201 = (f32[512,768]{1,0:T(8,128)S(1)}, bf16[512,768]{1,0:T(8,128)(2,1)S(1)}, f32[2,768]{1,0:T(2,128)S(1)}, bf16[512,768]{1,0:T(8,128)(2,1)S(1)}, bf16...) custom-call(f32[512,768]{1,0:T(8,128)S(1)} %get-tuple-element.189.back_sum, ...), custom_call_target="tpu_custom_call" | custom-call | flops 10000000000 | bytes 30000000 | tf_op jit(solution)/shard_map/pallas_call | solution.py:1022
  127.2 4.0 %collective-permute-start.23 = (bf16[2,896,128]{2,1,0:T(8,128)(2,1)S(1)}, bf16[2,896,128]{2,1,0:T(8,128)(2,1)S(1)}, u32[]{:S(2)}, u32[]{:S(2)}) collective-permute-start(bf16[2,896,128]{2,1,0:T(8,128)(2,1)S(1)} %get-tuple-element.192), channel_id=1, source_target_pairs={{1,0},{2,1},{3,2},{5,4},{6,5},{7,6},{9,8},{10,9},{11,10},{13,12},{... | collective-permute-start | bytes 1376264 | tf_op jit(solution)/shard_map/ppermute | solution.py:37
  131.2 6.9 %shard_map.204 = (bf16[1536,384]{1,0:T(8,128)(2,1)S(1)}, bf16[1536,384]{1,0:T(8,128)(2,1)S(1)}, bf16[1536,384]{1,0:T(8,128)(2,1)S(1)}, bf16[768,384]{1,0:T(8,128)(2,1)S(1)}, bf16[768,384]{1,0:T(8,128)(2,1)S(1)}) custom-call(bf16[768,512]{1,0:T(8,128)(2,1)S(1)} %get-tuple-element.202.second_t, bf16[768,512]{1,0:T(8,128)(2,1)S(1)} %get-tuple-element.203.second_other_t, ...), custom_call_target="tpu_custom_call" | custom-call | flops 14000000000 | bytes 42000000 | tf_op jit(solution)/shard_map/pallas_call | solution.py:1043
  142.5 7.1 %shard_map.202 = (bf16[512,768]{1,0:T(8,128)(2,1)S(1)}, f32[768,128]{1,0:T(8,128)S(1)}, bf16[768,512]{1,0:T(8,128)(2,1)}) custom-call(bf16[512,768]{1,0:T(8,128)(2,1)S(1)} %copy-done.3, bf16[512,1536]{1,0:T(8,128)(2,1)S(1)} %get-tuple-element.172.keyed.refs_0_, bf16[6,256,256]{2,1,0:T(8,128)(2,1)S(1)} %get-tuple-element.163.maps, ...), custom_call_target="tpu_custom_call" | custom-call | flops 12000000000 | bytes 36000000 | tf_op jit(solution)/shard_map/pallas_call | solution.py:1049
  154.4 8.6 %shard_map.206 = (f32[1536,512]{1,0:T(8,128)S(1)}, f32[512,768]{1,0:T(8,128)S(1)}) custom-call(bf16[512,1536]{1,0:T(8,128)(2,1)S(1)} %get-tuple-element.172.keyed.refs_0_, bf16[1536,512]{1,0:T(8,128)(2,1)S(1)} %get-tuple-element.175.fq_t.refs_1_, bf16[512,1536]{1,0:T(8,128)(2,1)S(1)} %get-tuple-element.219.refs_2_.fk, ...), custom_call_target="tpu_custom_call" | custom-call | flops 10000000000 | bytes 30000000 | tf_op jit(solution)/shard_map/pallas_call | solution.py:1060
  163.0 6.0 %shard_map.207 = (bf16[512,1536]{1,0:T(8,128)(2,1)S(1)}, f32[768,128]{1,0:T(8,128)S(1)}, bf16[4,512,384]{2,1,0:T(8,128)(2,1)S(1)}, bf16[768,512]{1,0:T(8,128)(2,1)}) custom-call(s32[1]{0:T(128)} %bitcast.7.place, bf16[512,1536]{1,0:T(8,128)(2,1)S(1)} %get-tuple-element.172.keyed.refs_0_, bf16[512,1536]{1,0:T(8,128)(2,1)S(1)} %get-tuple-element.219.refs_2_.fk, ...), custom_call_target="tpu_custom_call" | custom-call | flops 14000000000 | bytes 42000000 | tf_op jit(solution)/shard_map/pallas_call | solution.py:1068
  171.4 4.7 %shard_map.208 = (bf16[512,768]{1,0:T(8,128)(2,1)}, bf16[512,768]{1,0:T(8,128)(2,1)}, bf16[4,240,128]{2,1,0:T(8,128)(2,1)S(1)}) custom-call(bf16[512,768]{1,0:T(8,128)(2,1)S(1)} %bitcast.41, f32[4,768]{1,0:T(4,128)S(1)} %get-tuple-element.155.vectors, f32[512,768]{1,0:T(8,128)S(1)} %shard_map.203.early, bf16[512,1536]{1,0:T(8,128)(2,1)S(1)} %get-tuple-element.225.d_keyed, ...), custom_call_target="tpu_custom_call" | custom-call | flops 14000000000 | bytes 42000000 | tf_op jit(solution)/shard_map/pallas_call | solution.py:1080
  179.2 5.0 %shard_map.210 = (bf16[832,384]{1,0:T(8,128)(2,1)S(1)}, bf16[832,384]{1,0:T(8,128)(2,1)S(1)}, bf16[832,384]{1,0:T(8,128)(2,1)S(1)}, bf16[416,384]{1,0:T(8,128)(2,1)S(1)}, bf16[416,384]{1,0:T(8,128)(2,1)S(1)}) custom-call(s32[1]{0:T(128)} %bitcast.7.place, bf16[512,768]{1,0:T(8,128)(2,1)S(1)} %get-tuple-element.196.d_queries, ...), custom_call_target="tpu_custom_call" | custom-call | flops 14000000000 | bytes 42000000 | tf_op jit(solution)/shard_map/pallas_call | solution.py:1104
  188.3 4.0 %collective-permute-done.36.refs_0_ = bf16[384,384]{1,0:T(8,128)(2,1)S(1)} collective-permute-done((bf16[384,384]{1,0:T(8,128)(2,1)S(1)}, bf16[384,384]{1,0:T(8,128)(2,1)S(1)}, u32[]{:S(2)}, u32[]{:S(2)}) %collective-permute-start.36) | collective-permute-done | bytes 294944 | tf_op jit(solution)/shard_map/ppermute | solution.py:31
  197.2 16.7 %collective-permute-done.39.refs_1_ = bf16[384,384]{1,0:T(8,128)(2,1)S(1)} collective-permute-done((bf16[384,384]{1,0:T(8,128)(2,1)S(1)}, bf16[384,384]{1,0:T(8,128)(2,1)S(1)}, u32[]{:S(2)}, u32[]{:S(2)}) %collective-permute-start.39) | collective-permute-done | bytes 294944 | tf_op jit(solution)/shard_map/ppermute | solution.py:31
  218.8 9.4 %collective-permute-done.42.refs_1_ = bf16[208,384]{1,0:T(8,128)(2,1)S(1)} collective-permute-done((bf16[208,384]{1,0:T(8,128)(2,1)S(1)}, bf16[208,384]{1,0:T(8,128)(2,1)S(1)}, u32[]{:S(2)}, u32[]{:S(2)}) %collective-permute-start.42) | collective-permute-done | bytes 159776 | tf_op jit(solution)/shard_map/ppermute | solution.py:31
  228.2 4.0 %collective-permute-done.43.refs_2_ = bf16[208,384]{1,0:T(8,128)(2,1)S(1)} collective-permute-done((bf16[208,384]{1,0:T(8,128)(2,1)S(1)}, bf16[208,384]{1,0:T(8,128)(2,1)S(1)}, u32[]{:S(2)}, u32[]{:S(2)}) %collective-permute-start.43) | collective-permute-done | bytes 159776 | tf_op jit(solution)/shard_map/ppermute | solution.py:31
  235.0 5.4 %collective-permute-done.47 = bf16[384,384]{1,0:T(8,128)(2,1)S(1)} collective-permute-done((bf16[384,384]{1,0:T(8,128)(2,1)S(1)}, bf16[384,384]{1,0:T(8,128)(2,1)S(1)}, u32[]{:S(2)}, u32[]{:S(2)}) %collective-permute-start.47) | collective-permute-done | bytes 294944 | tf_op jit(solution)/shard_map/ppermute | solution.py:26
  241.2 6.4 %collective-permute-done.49 = bf16[384,384]{1,0:T(8,128)(2,1)S(1)} collective-permute-done((bf16[384,384]{1,0:T(8,128)(2,1)S(1)}, bf16[384,384]{1,0:T(8,128)(2,1)S(1)}, u32[]{:S(2)}, u32[]{:S(2)}) %collective-permute-start.49) | collective-permute-done | bytes 294944 | tf_op jit(solution)/shard_map/ppermute | solution.py:26
  (137 shorter events, 95.0 us)
Async XLA Ops:
  4.6 16.7 %collective-permute-start.1 = (bf16[264,384]{1,0:T(8,128)(2,1)S(1)}, bf16[264,384]{1,0:T(8,128)(2,1)S(1)}, u32[]{:S(2)}, u32[]{:S(2)}) collective-permute-start(bf16[264,384]{1,0:T(8,128)(2,1)S(1)} %maximum_maximum_fusion.refs_0_), channel_id=1, source_target_pairs={{0,2},{1,3},{2,0},{3,1},{4,6},{5,7},{6,4},{7,5},{8,10},{9,11},{10,... | collective-permute-start | bytes 608264 | tf_op jit(solution)/shard_map/ppermute | solution.py:31
  5.7 18.5 %collective-permute-start.2 = (bf16[264,384]{1,0:T(8,128)(2,1)S(1)}, bf16[264,384]{1,0:T(8,128)(2,1)S(1)}, u32[]{:S(2)}, u32[]{:S(2)}) collective-permute-start(bf16[264,384]{1,0:T(8,128)(2,1)S(1)} %maximum_maximum_fusion.refs_0_), channel_id=1, source_target_pairs={{0,3},{1,0},{2,1},{3,2},{4,7},{5,4},{6,5},{7,6},{8,11},{9,8},{10,9... | collective-permute-start | bytes 608264 | tf_op jit(solution)/shard_map/ppermute | solution.py:31
  24.8 14.5 %collective-permute-start.3 = (bf16[768,384]{1,0:T(8,128)(2,1)S(1)}, bf16[768,384]{1,0:T(8,128)(2,1)S(1)}, u32[]{:S(2)}, u32[]{:S(2)}) collective-permute-start(bf16[768,384]{1,0:T(8,128)(2,1)S(1)} %bitcast.42), channel_id=1, source_target_pairs={{0,8},{4,12},{8,0},{12,4},{16,24},{20,28},{24,16},{28,20},{1,9},{5... | collective-permute-start | bytes 1769480 | tf_op jit(solution)/shard_map/ppermute | solution.py:26
  26.0 14.1 %collective-permute-start.4 = (bf16[768,384]{1,0:T(8,128)(2,1)S(1)}, bf16[768,384]{1,0:T(8,128)(2,1)S(1)}, u32[]{:S(2)}, u32[]{:S(2)}) collective-permute-start(bf16[768,384]{1,0:T(8,128)(2,1)S(1)} %bitcast.43), channel_id=1, source_target_pairs={{0,16},{4,20},{8,24},{12,28},{16,0},{20,4},{24,8},{28,12},{1,17},{... | collective-permute-start | bytes 1769480 | tf_op jit(solution)/shard_map/ppermute | solution.py:26
  27.3 14.1 %collective-permute-start.6 = (bf16[384,384]{1,0:T(8,128)(2,1)S(1)}, bf16[384,384]{1,0:T(8,128)(2,1)S(1)}, u32[]{:S(2)}, u32[]{:S(2)}) collective-permute-start(bf16[384,384]{1,0:T(8,128)(2,1)S(1)} %pad_maximum_fusion.2), channel_id=1, source_target_pairs={{0,3},{1,0},{2,1},{3,2},{4,7},{5,4},{6,5},{7,6},{8,11},{9,8},{10,9... | collective-permute-start | bytes 884744 | tf_op jit(solution)/shard_map/ppermute | solution.py:31
  60.3 27.2 %collective-permute-start.14 = (bf16[1536,384]{1,0:T(8,128)(2,1)S(1)}, bf16[1536,384]{1,0:T(8,128)(2,1)S(1)}, u32[]{:S(2)}, u32[]{:S(2)}) collective-permute-start(bf16[1536,384]{1,0:T(8,128)(2,1)S(1)} %bitcast.32), channel_id=1, source_target_pairs={{0,8},{4,12},{8,0},{12,4},{16,24},{20,28},{24,16},{28,20},{1,9},{5... | collective-permute-start | bytes 3538952 | tf_op jit(solution)/shard_map/ppermute | solution.py:26
  61.2 26.9 %collective-permute-start.15 = (bf16[1536,384]{1,0:T(8,128)(2,1)S(1)}, bf16[1536,384]{1,0:T(8,128)(2,1)S(1)}, u32[]{:S(2)}, u32[]{:S(2)}) collective-permute-start(bf16[1536,384]{1,0:T(8,128)(2,1)S(1)} %bitcast.33), channel_id=1, source_target_pairs={{0,16},{4,20},{8,24},{12,28},{16,0},{20,4},{24,8},{28,12},{1,17},{... | collective-permute-start | bytes 3538952 | tf_op jit(solution)/shard_map/ppermute | solution.py:26
  62.5 14.2 %collective-permute-start.16 = (bf16[2,896,128]{2,1,0:T(8,128)(2,1)S(1)}, bf16[2,896,128]{2,1,0:T(8,128)(2,1)S(1)}, u32[]{:S(2)}, u32[]{:S(2)}) collective-permute-start(bf16[2,896,128]{2,1,0:T(8,128)(2,1)S(1)} %get-tuple-element.177), channel_id=1, source_target_pairs={{0,1},{1,2},{2,3},{4,5},{5,6},{6,7},{8,9},{9,10},{10,11},{12,13},{... | collective-permute-start | bytes 1376264 | tf_op jit(solution)/shard_map/ppermute | solution.py:37
  76.8 21.7 %collective-permute-start.17 = (bf16[2,896,128]{2,1,0:T(8,128)(2,1)S(1)}, bf16[2,896,128]{2,1,0:T(8,128)(2,1)S(1)}, u32[]{:S(2)}, u32[]{:S(2)}) collective-permute-start(bf16[2,896,128]{2,1,0:T(8,128)(2,1)S(1)} %add_convert_fusion.1), channel_id=1, source_target_pairs={{0,2},{1,3},{4,6},{5,7},{8,10},{9,11},{12,14},{13,15},{16,18},{17,... | collective-permute-start | bytes 1376264 | tf_op jit(solution)/shard_map/ppermute | solution.py:37
  79.5 24.7 %collective-permute-start.19 = (bf16[512,768]{1,0:T(8,128)(2,1)S(1)}, bf16[512,768]{1,0:T(8,128)(2,1)S(1)}, u32[]{:S(2)}, u32[]{:S(2)}) collective-permute-start(bf16[512,768]{1,0:T(8,128)(2,1)S(1)} %bitcast.35), channel_id=1, source_target_pairs={{0,4},{4,0},{8,12},{12,8},{16,20},{20,16},{24,28},{28,24},{1,5},{5... | collective-permute-start | bytes 2359304 | tf_op jit(solution)/shard_map/ppermute | solution.py:26
  88.1 15.9 %collective-permute-start.20 = (bf16[768,384]{1,0:T(8,128)(2,1)S(1)}, bf16[768,384]{1,0:T(8,128)(2,1)S(1)}, u32[]{:S(2)}, u32[]{:S(2)}) collective-permute-start(bf16[768,384]{1,0:T(8,128)(2,1)S(1)} %slice.59), channel_id=1, source_target_pairs={{0,16},{4,20},{8,24},{12,28},{16,0},{20,4},{24,8},{28,12},{1,17},{... | collective-permute-start | bytes 1769480 | tf_op jit(solution)/shard_map/ppermute | solution.py:26
  89.4 14.6 %collective-permute-start.21 = (bf16[768,384]{1,0:T(8,128)(2,1)S(1)}, bf16[768,384]{1,0:T(8,128)(2,1)S(1)}, u32[]{:S(2)}, u32[]{:S(2)}) collective-permute-start(bf16[768,384]{1,0:T(8,128)(2,1)S(1)} %slice.60), channel_id=1, source_target_pairs={{0,8},{4,12},{8,0},{12,4},{16,24},{20,28},{24,16},{28,20},{1,9},{5... | collective-permute-start | bytes 1769480 | tf_op jit(solution)/shard_map/ppermute | solution.py:26
  138.2 14.3 %collective-permute-start.27 = (bf16[768,384]{1,0:T(8,128)(2,1)S(1)}, bf16[768,384]{1,0:T(8,128)(2,1)S(1)}, u32[]{:S(2)}, u32[]{:S(2)}) collective-permute-start(bf16[768,384]{1,0:T(8,128)(2,1)S(1)} %get-tuple-element.208), channel_id=1, source_target_pairs={{0,16},{4,20},{8,24},{12,28},{16,0},{20,4},{24,8},{28,12},{1,17},{... | collective-permute-start | bytes 1769480 | tf_op jit(solution)/shard_map/ppermute | solution.py:26
  138.4 14.0 %collective-permute-start.28 = (bf16[768,384]{1,0:T(8,128)(2,1)S(1)}, bf16[768,384]{1,0:T(8,128)(2,1)S(1)}, u32[]{:S(2)}, u32[]{:S(2)}) collective-permute-start(bf16[768,384]{1,0:T(8,128)(2,1)S(1)} %get-tuple-element.209), channel_id=1, source_target_pairs={{0,8},{4,12},{8,0},{12,4},{16,24},{20,28},{24,16},{28,20},{1,9},{5... | collective-permute-start | bytes 1769480 | tf_op jit(solution)/shard_map/ppermute | solution.py:26
  141.0 22.0 %collective-permute-start.29 = (bf16[2,896,128]{2,1,0:T(8,128)(2,1)S(1)}, bf16[2,896,128]{2,1,0:T(8,128)(2,1)S(1)}, u32[]{:S(2)}, u32[]{:S(2)}) collective-permute-start(bf16[2,896,128]{2,1,0:T(8,128)(2,1)S(1)} %add_convert_fusion), channel_id=1, source_target_pairs={{2,0},{3,1},{6,4},{7,5},{10,8},{11,9},{14,12},{15,13},{18,16},{19,... | collective-permute-start | bytes 1376264 | tf_op jit(solution)/shard_map/ppermute | solution.py:37
  152.8 25.8 %collective-permute-start.32 = (bf16[1536,384]{1,0:T(8,128)(2,1)S(1)}, bf16[1536,384]{1,0:T(8,128)(2,1)S(1)}, u32[]{:S(2)}, u32[]{:S(2)}) collective-permute-start(bf16[1536,384]{1,0:T(8,128)(2,1)S(1)} %get-tuple-element.237), channel_id=1, source_target_pairs={{0,8},{4,12},{8,0},{12,4},{16,24},{20,28},{24,16},{28,20},{1,9},{5... | collective-permute-start | bytes 3538952 | tf_op jit(solution)/shard_map/ppermute | solution.py:26
  153.3 25.4 %collective-permute-start.33 = (bf16[1536,384]{1,0:T(8,128)(2,1)S(1)}, bf16[1536,384]{1,0:T(8,128)(2,1)S(1)}, u32[]{:S(2)}, u32[]{:S(2)}) collective-permute-start(bf16[1536,384]{1,0:T(8,128)(2,1)S(1)} %get-tuple-element.238), channel_id=1, source_target_pairs={{0,16},{4,20},{8,24},{12,28},{16,0},{20,4},{24,8},{28,12},{1,17},{... | collective-permute-start | bytes 3538952 | tf_op jit(solution)/shard_map/ppermute | solution.py:26
  192.5 21.4 %collective-permute-start.37 = (bf16[832,384]{1,0:T(8,128)(2,1)S(1)}, bf16[832,384]{1,0:T(8,128)(2,1)S(1)}, u32[]{:S(2)}, u32[]{:S(2)}) collective-permute-start(bf16[832,384]{1,0:T(8,128)(2,1)S(1)} %get-tuple-element.255), channel_id=1, source_target_pairs={{0,8},{4,12},{8,0},{12,4},{16,24},{20,28},{24,16},{28,20},{1,9},{5... | collective-permute-start | bytes 1916936 | tf_op jit(solution)/shard_map/ppermute | solution.py:26
  193.0 20.9 %collective-permute-start.38 = (bf16[832,384]{1,0:T(8,128)(2,1)S(1)}, bf16[832,384]{1,0:T(8,128)(2,1)S(1)}, u32[]{:S(2)}, u32[]{:S(2)}) collective-permute-start(bf16[832,384]{1,0:T(8,128)(2,1)S(1)} %get-tuple-element.256), channel_id=1, source_target_pairs={{0,16},{4,20},{8,24},{12,28},{16,0},{20,4},{24,8},{28,12},{1,17},{... | collective-permute-start | bytes 1916936 | tf_op jit(solution)/shard_map/ppermute | solution.py:26
  193.8 20.0 %collective-permute-start.39 = (bf16[384,384]{1,0:T(8,128)(2,1)S(1)}, bf16[384,384]{1,0:T(8,128)(2,1)S(1)}, u32[]{:S(2)}, u32[]{:S(2)}) collective-permute-start(bf16[384,384]{1,0:T(8,128)(2,1)S(1)} %get-tuple-element.258), channel_id=1, source_target_pairs={{0,2},{1,3},{2,0},{3,1},{4,6},{5,7},{6,4},{7,5},{8,10},{9,11},{10,... | collective-permute-start | bytes 884744 | tf_op jit(solution)/shard_map/ppermute | solution.py:31
  195.8 18.1 %collective-permute-start.40 = (bf16[384,384]{1,0:T(8,128)(2,1)S(1)}, bf16[384,384]{1,0:T(8,128)(2,1)S(1)}, u32[]{:S(2)}, u32[]{:S(2)}) collective-permute-start(bf16[384,384]{1,0:T(8,128)(2,1)S(1)} %get-tuple-element.259), channel_id=1, source_target_pairs={{0,3},{1,0},{2,1},{3,2},{4,7},{5,4},{6,5},{7,6},{8,11},{9,8},{10,9... | collective-permute-start | bytes 884744 | tf_op jit(solution)/shard_map/ppermute | solution.py:31
  214.2 13.9 %collective-permute-start.42 = (bf16[208,384]{1,0:T(8,128)(2,1)S(1)}, bf16[208,384]{1,0:T(8,128)(2,1)S(1)}, u32[]{:S(2)}, u32[]{:S(2)}) collective-permute-start(bf16[208,384]{1,0:T(8,128)(2,1)S(1)} %get-tuple-element.264), channel_id=1, source_target_pairs={{0,2},{1,3},{2,0},{3,1},{4,6},{5,7},{6,4},{7,5},{8,10},{9,11},{10,... | collective-permute-start | bytes 479240 | tf_op jit(solution)/shard_map/ppermute | solution.py:31
  217.4 14.8 %collective-permute-start.43 = (bf16[208,384]{1,0:T(8,128)(2,1)S(1)}, bf16[208,384]{1,0:T(8,128)(2,1)S(1)}, u32[]{:S(2)}, u32[]{:S(2)}) collective-permute-start(bf16[208,384]{1,0:T(8,128)(2,1)S(1)} %get-tuple-element.265), channel_id=1, source_target_pairs={{0,3},{1,0},{2,1},{3,2},{4,7},{5,4},{6,5},{7,6},{8,11},{9,8},{10,9... | collective-permute-start | bytes 479240 | tf_op jit(solution)/shard_map/ppermute | solution.py:31
  233.7 13.9 %collective-permute-start.49 = (bf16[384,384]{1,0:T(8,128)(2,1)S(1)}, bf16[384,384]{1,0:T(8,128)(2,1)S(1)}, u32[]{:S(2)}, u32[]{:S(2)}) collective-permute-start(bf16[384,384]{1,0:T(8,128)(2,1)S(1)} %shard_map.214), channel_id=1, source_target_pairs={{0,24},{4,28},{8,16},{12,20},{16,8},{20,12},{24,0},{28,4},{1,25},{... | collective-permute-start | bytes 884744 | tf_op jit(solution)/shard_map/ppermute | solution.py:26
  (32 other events, 266.4 us)

commit v2 on v1

--- a/solution.py
+++ b/solution.py
@@ -142,14 +142,14 @@
     )
 
 
-def settle(own, received):
+def settle(own, received, weight=1):
     def kernel(own, *refs):
         total = own[...]
         for ref in refs[:-1]:
             total = total + wide(ref[...])
         refs[-1][...] = low(total)
 
-    return call(kernel, 1, whole(own.shape))(own, *received)
+    return call(kernel, weight, whole(own.shape))(own, *received)
 
 
 def dot(a, b):
@@ -847,7 +847,7 @@
         scratch_shapes=list(scratch),
         compiler_params=pltpu.CompilerParams(vmem_limit_bytes=limit << 20),
         cost_estimate=pl.CostEstimate(
-            flops=weight * 2000 * 10**6, transcendentals=0, bytes_accessed=weight * 3 * 2000 * 10**3
+            flops=int(weight * 2000 * 10**6), transcendentals=0, bytes_accessed=int(weight * 6 * 10**6)
         ),
         **rest,
     )
@@ -938,6 +938,8 @@
     mlp_parts = [part_mlp[None]] + [soon[step][None] for step in steps]
     mlp_slots = [(here - step) % shard_count for step in range(shard_count)]
 
+    mlp_full = place_parts(mlp_parts, mlp_slots).reshape(-1, CHUNK)
+    mlp_full, vectors = lax.optimization_barrier((mlp_full, vectors))
     normed, keyed, fk, fk_t, key_state, w_kv = call(
         keys_kernel,
         8,
@@ -952,9 +954,6 @@
         scalar_first(3 + PIECES),
     )(spot, flat, vectors, maps, *in_pieces)
     prior, running = scan_first(key_state, 1)
-    mlp_parts, normed = lax.optimization_barrier((mlp_parts, normed))
-    mlp_full = place_parts(mlp_parts, mlp_slots).reshape(-1, CHUNK)
-    mlp_full, normed = lax.optimization_barrier((mlp_full, normed))
     mlp_x, mlp_y = sides_of(mlp_full)
     normed_t, queries, fq, fq_t, partial, out_weight, w_q = call(
         queries_kernel,
@@ -1125,16 +1124,25 @@
         attended_t,
         attended_other_t,
     )
-    in_to_x, in_to_y = flip(in_grads[3], 4), flip(in_grads[4], 2)
     mlp_received = [spin(part, step + 1) for step, part in enumerate(mlp_blocks[1:])]
-    in_to_x, in_to_y, mlp_received[:1] = lax.optimization_barrier((in_to_x, in_to_y, mlp_received[:1]))
+    in_upper, in_lower, mlp_received[:1] = lax.optimization_barrier(
+        (in_grads[3], in_grads[4], mlp_received[:1])
+    )
+    in_to_x, in_to_y = flip(in_upper, 4), flip(in_lower, 2)
+    in_to_x, in_to_y, mlp_received[2:] = lax.optimization_barrier(
+        (in_to_x, in_to_y, mlp_received[2:])
+    )
     in_sides = add_sides(in_grads, in_to_x, in_to_y)
     in_joined = [flip(in_sides[0], 2), flip(in_sides[1], 4)]
     in_joined, mlp_received = lax.optimization_barrier((in_joined, mlp_received))
     in_blocks = join_parts([in_grads[0], *in_joined])
     in_received = [spin(part, step + 1) for step, part in enumerate(in_blocks[1:])]
-    in_received, mlp_received = lax.optimization_barrier((in_received, mlp_received))
-    mlp_sums = share_pair(share_flips(settle(mlp_blocks[0], mlp_received)))
+    in_blocks, mlp_received = lax.optimization_barrier((in_blocks, mlp_received))
+    mlp_total = settle(mlp_blocks[0], mlp_received, 10)
+    mlp_flips = share_flips(mlp_total)
+    in_received, _ = lax.optimization_barrier((in_received, mlp_total))
+    in_received[:1], mlp_flips[:2] = lax.optimization_barrier((in_received[:1], mlp_flips[:2]))
+    mlp_sums = share_pair(mlp_flips)
     in_flips = share_flips(settle(in_blocks[0], in_received))
     grad_up, grad_down = call(
         lay_mlp_kernel,

time: 266 us -> 245 us (0.921)
  waiting for transfers between devices: 113 us -> 91.3 us
    ppermute x36, waiting for transfers between devices: 49.8 us -> 30.1 us  [flip(): return lax.ppermute(value, 'rep', [(i, i ^ bit) for i in range(count)])]
    ppermute x12, waiting for transfers between devices: 46.8 us -> 36.8 us  [spin(): lax.ppermute(value, 'shard', [(i, (i + step) % count) for i in range(coun...]
    ppermute x4, waiting for transfers between devices: 16 us -> 24.5 us  [slide(): return lax.ppermute(value, 'shard', pairs)]
  transfers between devices with their start and end apart: 52 -> 52, of which waited for: 29 -> 20; matrix products, arithmetic and copies ran while one was open for 2% -> 3% of each run, Pallas kernels for 20% -> 27%
where the time goes in v2:
time: 245 us; the launch traced here: 244 us
  waiting for transfers between devices  91.3 us (37%)
  Pallas kernels  85.7 us (35%)
  starting transfers between devices  55.9 us (23%)
  local copies, waits for them, and re-layouts  6.85 us (3%)
  other arithmetic  3.08 us (1%)
    ppermute x12, waiting for transfers between devices, spin(): lax.ppermute(value, 'shard', [(i, (i + step) % count) for i in range(coun...  36.8 us
    ppermute x36, starting transfers between devices, flip(): return lax.ppermute(value, 'rep', [(i, i ^ bit) for i in range(count)])  31.7 us
    ppermute x36, waiting for transfers between devices, flip(): return lax.ppermute(value, 'rep', [(i, i ^ bit) for i in range(count)])  30.1 us
    ppermute x4, waiting for transfers between devices, slide(): return lax.ppermute(value, 'shard', pairs)  24.5 us
    ppermute x12, starting transfers between devices, spin(): lax.ppermute(value, 'shard', [(i, (i + step) % count) for i in range(coun...  16.1 us
    pallas_call x1, Pallas kernels, shards(): call(mlp_kernel, 20, (whole((count, D), wide_type), whole((count, D)), wh...  15.1 us
    pallas_call x1, Pallas kernels, shards(): call(lambda *refs: local_keys_kernel(*refs, seqs=seqs), 5, (whole((HEADS...  8.59 us
    ppermute x4, starting transfers between devices, slide(): return lax.ppermute(value, 'shard', pairs)  8.02 us
  transfers between devices with their start and end apart: 52, of which 20 were waited for; matrix products, arithmetic and copies ran while one was open for 3% of the time, Pallas kernels for 27%

profile of v2, /device:TPU:9, one launch (start us, length us, event | category | flops | bytes accessed | tf_op | source)
XLA Modules:
  0.0 243.9 jit_solution(4834419050867865812)
XLA Ops:
  7.0 2.9 %reshape.64 = bf16[192,4,8,96]{3,2,1,0:T(8,128)(2,1)S(1)} reshape(bf16[192,3072]{1,0:T(8,128)(2,1)} %param.19) | data formatting | bytes 2359296 | tf_op jit(solution)/shard_map/reshape | solution.py:894
  12.6 8.7 %collective-permute-done.1.refs_2_ = bf16[264,384]{1,0:T(8,128)(2,1)S(1)} collective-permute-done((bf16[264,384]{1,0:T(8,128)(2,1)S(1)}, bf16[264,384]{1,0:T(8,128)(2,1)S(1)}, u32[]{:S(2)}, u32[]{:S(2)}) %collective-permute-start.1) | collective-permute-done | bytes 202784 | tf_op jit(solution)/shard_map/ppermute | solution.py:31
  29.0 10.3 %collective-permute-done.3.refs_2_ = bf16[768,384]{1,0:T(8,128)(2,1)S(1)} collective-permute-done((bf16[768,384]{1,0:T(8,128)(2,1)S(1)}, bf16[768,384]{1,0:T(8,128)(2,1)S(1)}, u32[]{:S(2)}, u32[]{:S(2)}) %collective-permute-start.3) | collective-permute-done | bytes 589856 | tf_op jit(solution)/shard_map/ppermute | solution.py:26
  44.0 5.4 %collective-permute-done.7 = bf16[384,384]{1,0:T(8,128)(2,1)S(1)} collective-permute-done((bf16[384,384]{1,0:T(8,128)(2,1)S(1)}, bf16[384,384]{1,0:T(8,128)(2,1)S(1)}, u32[]{:S(2)}, u32[]{:S(2)}) %collective-permute-start.7) | collective-permute-done | bytes 294944 | tf_op jit(solution)/shard_map/ppermute | solution.py:26
  54.4 6.4 %shard_map.197 = (bf16[512,768]{1,0:T(8,128)(2,1)S(1)}, bf16[512,1536]{1,0:T(8,128)(2,1)S(1)}, bf16[512,1536]{1,0:T(8,128)(2,1)S(1)}, bf16[1536,512]{1,0:T(8,128...) custom-call(s32[1]{0:T(128)} %bitcast.12.place, bf16[512,768]{1,0:T(8,128)(2,1)S(1)} %bitcast.39, ...), custom_call_target="tpu_custom_call" | custom-call | flops 16000000000 | bytes 48000000 | tf_op jit(solution)/shard_map/pallas_call | solution.py:943
  62.8 6.8 %shard_map.198 = (bf16[768,512]{1,0:T(8,128)(2,1)S(1)}, bf16[512,768]{1,0:T(8,128)(2,1)S(1)}, bf16[512,1536]{1,0:T(8,128)(2,1)S(1)}, bf16[1536,512]{1,0:T(8,128)...) custom-call(s32[1]{0:T(128)} %bitcast.12.place, ...), custom_call_target="tpu_custom_call" | custom-call | flops 17999998976 | bytes 54000000 | tf_op jit(solution)/shard_map/pallas_call | solution.py:958
  69.6 5.8 %collective-permute-done.16.refs_0_ = bf16[2,896,128]{2,1,0:T(8,128)(2,1)S(1)} collective-permute-done((bf16[2,896,128]{2,1,0:T(8,128)(2,1)S(1)}, bf16[2,896,128]{2,1,0:T(8,128)(2,1)S(1)}, u32[]{:S(2)}, u32[]{:S(2)}) %collective-permute-start.16) | collective-permute-done | bytes 458784 | tf_op jit(solution)/shard_map/ppermute | solution.py:37
  82.2 15.0 %collective-permute-done.17.refs_1_ = bf16[2,896,128]{2,1,0:T(8,128)(2,1)S(1)} collective-permute-done((bf16[2,896,128]{2,1,0:T(8,128)(2,1)S(1)}, bf16[2,896,128]{2,1,0:T(8,128)(2,1)S(1)}, u32[]{:S(2)}, u32[]{:S(2)}) %collective-permute-start.17) | collective-permute-done | bytes 458784 | tf_op jit(solution)/shard_map/ppermute | solution.py:37
  97.3 5.0 %shard_map.199 = (bf16[512,768]{1,0:T(8,128)(2,1)S(1)}, f32[512,768]{1,0:T(8,128)S(1)}, f32[512,768]{1,0:T(8,128)S(1)}, bf16[512,768]{1,0:T(8,128)(2,1)S(1)}, bf16[768,512]{1,0:T(8,128)(2,1)S(1)}) custom-call(bf16[512,768]{1,0:T(8,128)(2,1)S(1)} %bitcast.40, f32[4,768]{1,0:T(4,128)S(1)} %get-tuple-element.165.vectors, ...), custom_call_target="tpu_custom_call" | custom-call | flops 10000000000 | bytes 30000000 | tf_op jit(solution)/shard_map/pallas_call | solution.py:976
  104.7 15.1 %shard_map.200 = (f32[512,768]{1,0:T(8,128)S(1)}, bf16[512,768]{1,0:T(8,128)(2,1)S(1)}, f32[512,768]{1,0:T(8,128)S(1)}, bf16[512,768]{1,0:T(8,128)(2,1)S(1)}, bf...) custom-call(bf16[512,768]{1,0:T(8,128)(2,1)S(1)} %get-tuple-element., ...), custom_call_target="tpu_custom_call" | custom-call | flops 40000000000 | bytes 120000000 | tf_op jit(solution)/shard_map/pallas_call | solution.py:998
  122.2 3.9 %shard_map.201 = (f32[512,768]{1,0:T(8,128)S(1)}, bf16[512,768]{1,0:T(8,128)(2,1)S(1)}, f32[2,768]{1,0:T(2,128)S(1)}, bf16[512,768]{1,0:T(8,128)(2,1)S(1)}, bf16...) custom-call(f32[512,768]{1,0:T(8,128)S(1)} %get-tuple-element.186.back_sum, ...), custom_call_target="tpu_custom_call" | custom-call | flops 10000000000 | bytes 30000000 | tf_op jit(solution)/shard_map/pallas_call | solution.py:1021
  128.0 6.9 %shard_map.204 = (bf16[1536,384]{1,0:T(8,128)(2,1)S(1)}, bf16[1536,384]{1,0:T(8,128)(2,1)S(1)}, bf16[1536,384]{1,0:T(8,128)(2,1)S(1)}, bf16[768,384]{1,0:T(8,128)(2,1)S(1)}, bf16[768,384]{1,0:T(8,128)(2,1)S(1)}) custom-call(bf16[768,512]{1,0:T(8,128)(2,1)S(1)} %get-tuple-element.199.second_t, bf16[768,512]{1,0:T(8,128)(2,1)S(1)} %get-tuple-element.200.second_other_t, ...), custom_call_target="tpu_custom_call" | custom-call | flops 14000000000 | bytes 42000000 | tf_op jit(solution)/shard_map/pallas_call | solution.py:1042
  136.1 3.6 %collective-permute-done.23.refs_0_ = bf16[2,896,128]{2,1,0:T(8,128)(2,1)S(1)} collective-permute-done((bf16[2,896,128]{2,1,0:T(8,128)(2,1)S(1)}, bf16[2,896,128]{2,1,0:T(8,128)(2,1)S(1)}, u32[]{:S(2)}, u32[]{:S(2)}) %collective-permute-start.23) | collective-permute-done | bytes 458784 | tf_op jit(solution)/shard_map/ppermute | solution.py:37
  141.3 7.1 %shard_map.202 = (bf16[512,768]{1,0:T(8,128)(2,1)S(1)}, f32[768,128]{1,0:T(8,128)S(1)}, bf16[768,512]{1,0:T(8,128)(2,1)}) custom-call(bf16[512,768]{1,0:T(8,128)(2,1)S(1)} %copy-done.3, bf16[512,1536]{1,0:T(8,128)(2,1)S(1)} %get-tuple-element.169.keyed.refs_0_, bf16[6,256,256]{2,1,0:T(8,128)(2,1)S(1)} %get-tuple-element.166.maps, ...), custom_call_target="tpu_custom_call" | custom-call | flops 12000000000 | bytes 36000000 | tf_op jit(solution)/shard_map/pallas_call | solution.py:1048
  151.4 8.6 %shard_map.206 = (f32[1536,512]{1,0:T(8,128)S(1)}, f32[512,768]{1,0:T(8,128)S(1)}) custom-call(bf16[512,1536]{1,0:T(8,128)(2,1)S(1)} %get-tuple-element.169.keyed.refs_0_, bf16[1536,512]{1,0:T(8,128)(2,1)S(1)} %get-tuple-element.172.fq_t.refs_1_, bf16[512,1536]{1,0:T(8,128)(2,1)S(1)} %get-tuple-element.216.refs_2_.fk, ...), custom_call_target="tpu_custom_call" | custom-call | flops 10000000000 | bytes 30000000 | tf_op jit(solution)/shard_map/pallas_call | solution.py:1059
  160.0 6.0 %shard_map.207 = (bf16[512,1536]{1,0:T(8,128)(2,1)S(1)}, f32[768,128]{1,0:T(8,128)S(1)}, bf16[4,512,384]{2,1,0:T(8,128)(2,1)S(1)}, bf16[768,512]{1,0:T(8,128)(2,1)}) custom-call(s32[1]{0:T(128)} %bitcast.12.place, bf16[512,1536]{1,0:T(8,128)(2,1)S(1)} %get-tuple-element.169.keyed.refs_0_, bf16[512,1536]{1,0:T(8,128)(2,1)S(1)} %get-tuple-element.216.refs_2_.fk, ...), custom_call_target="tpu_custom_call" | custom-call | flops 14000000000 | bytes 42000000 | tf_op jit(solution)/shard_map/pallas_call | solution.py:1067
  168.1 4.7 %shard_map.208 = (bf16[512,768]{1,0:T(8,128)(2,1)}, bf16[512,768]{1,0:T(8,128)(2,1)}, bf16[4,240,128]{2,1,0:T(8,128)(2,1)S(1)}) custom-call(bf16[512,768]{1,0:T(8,128)(2,1)S(1)} %bitcast.41, f32[4,768]{1,0:T(4,128)S(1)} %get-tuple-element.165.vectors, f32[512,768]{1,0:T(8,128)S(1)} %shard_map.203.early, bf16[512,1536]{1,0:T(8,128)(2,1)S(1)} %get-tuple-element.222.d_keyed, ...), custom_call_target="tpu_custom_call" | custom-call | flops 14000000000 | bytes 42000000 | tf_op jit(solution)/shard_map/pallas_call | solution.py:1079
  172.8 3.7 %collective-permute-done.32.refs_1_ = bf16[1536,384]{1,0:T(8,128)(2,1)S(1)} collective-permute-done((bf16[1536,384]{1,0:T(8,128)(2,1)S(1)}, bf16[1536,384]{1,0:T(8,128)(2,1)S(1)}, u32[]{:S(2)}, u32[]{:S(2)}) %collective-permute-start.32) | collective-permute-done | bytes 1179680 | tf_op jit(solution)/shard_map/ppermute | solution.py:26
  179.2 5.0 %shard_map.210 = (bf16[832,384]{1,0:T(8,128)(2,1)S(1)}, bf16[832,384]{1,0:T(8,128)(2,1)S(1)}, bf16[832,384]{1,0:T(8,128)(2,1)S(1)}, bf16[416,384]{1,0:T(8,128)(2,1)S(1)}, bf16[416,384]{1,0:T(8,128)(2,1)S(1)}) custom-call(s32[1]{0:T(128)} %bitcast.12.place, bf16[512,768]{1,0:T(8,128)(2,1)S(1)} %get-tuple-element.193.d_queries, ...), custom_call_target="tpu_custom_call" | custom-call | flops 14000000000 | bytes 42000000 | tf_op jit(solution)/shard_map/pallas_call | solution.py:1103
  187.1 4.4 %collective-permute-done.37.refs_2_ = bf16[384,384]{1,0:T(8,128)(2,1)S(1)} collective-permute-done((bf16[384,384]{1,0:T(8,128)(2,1)S(1)}, bf16[384,384]{1,0:T(8,128)(2,1)S(1)}, u32[]{:S(2)}, u32[]{:S(2)}) %collective-permute-start.37) | collective-permute-done | bytes 294944 | tf_op jit(solution)/shard_map/ppermute | solution.py:31
  195.9 10.1 %collective-permute-done.40.refs_1_ = bf16[384,384]{1,0:T(8,128)(2,1)S(1)} collective-permute-done((bf16[384,384]{1,0:T(8,128)(2,1)S(1)}, bf16[384,384]{1,0:T(8,128)(2,1)S(1)}, u32[]{:S(2)}, u32[]{:S(2)}) %collective-permute-start.40) | collective-permute-done | bytes 294944 | tf_op jit(solution)/shard_map/ppermute | solution.py:31
  209.8 3.1 %collective-permute-start.42 = (bf16[208,384]{1,0:T(8,128)(2,1)S(1)}, bf16[208,384]{1,0:T(8,128)(2,1)S(1)}, u32[]{:S(2)}, u32[]{:S(2)}) collective-permute-start(bf16[208,384]{1,0:T(8,128)(2,1)S(1)} %get-tuple-element.264), channel_id=1, source_target_pairs={{0,2},{1,3},{2,0},{3,1},{4,6},{5,7},{6,4},{7,5},{8,10},{9,11},{10,... | collective-permute-start | bytes 479240 | tf_op jit(solution)/shard_map/ppermute | solution.py:31
  216.1 7.9 %collective-permute-done.43.refs_2_ = bf16[208,384]{1,0:T(8,128)(2,1)S(1)} collective-permute-done((bf16[208,384]{1,0:T(8,128)(2,1)S(1)}, bf16[208,384]{1,0:T(8,128)(2,1)S(1)}, u32[]{:S(2)}, u32[]{:S(2)}) %collective-permute-start.43) | collective-permute-done | bytes 159776 | tf_op jit(solution)/shard_map/ppermute | solution.py:31
  233.2 4.6 %collective-permute-done.47 = bf16[208,384]{1,0:T(8,128)(2,1)S(1)} collective-permute-done((bf16[208,384]{1,0:T(8,128)(2,1)S(1)}, bf16[208,384]{1,0:T(8,128)(2,1)S(1)}, u32[]{:S(2)}, u32[]{:S(2)}) %collective-permute-start.47) | collective-permute-done | bytes 159776 | tf_op jit(solution)/shard_map/ppermute | solution.py:26
  (137 shorter events, 81.8 us)
Async XLA Ops:
  4.6 16.7 %collective-permute-start.1 = (bf16[264,384]{1,0:T(8,128)(2,1)S(1)}, bf16[264,384]{1,0:T(8,128)(2,1)S(1)}, u32[]{:S(2)}, u32[]{:S(2)}) collective-permute-start(bf16[264,384]{1,0:T(8,128)(2,1)S(1)} %maximum_maximum_fusion.refs_0_), channel_id=1, source_target_pairs={{0,2},{1,3},{2,0},{3,1},{4,6},{5,7},{6,4},{7,5},{8,10},{9,11},{10,... | collective-permute-start | bytes 608264 | tf_op jit(solution)/shard_map/ppermute | solution.py:31
  5.7 18.5 %collective-permute-start.2 = (bf16[264,384]{1,0:T(8,128)(2,1)S(1)}, bf16[264,384]{1,0:T(8,128)(2,1)S(1)}, u32[]{:S(2)}, u32[]{:S(2)}) collective-permute-start(bf16[264,384]{1,0:T(8,128)(2,1)S(1)} %maximum_maximum_fusion.refs_0_), channel_id=1, source_target_pairs={{0,3},{1,0},{2,1},{3,2},{4,7},{5,4},{6,5},{7,6},{8,11},{9,8},{10,9... | collective-permute-start | bytes 608264 | tf_op jit(solution)/shard_map/ppermute | solution.py:31
  24.8 14.5 %collective-permute-start.3 = (bf16[768,384]{1,0:T(8,128)(2,1)S(1)}, bf16[768,384]{1,0:T(8,128)(2,1)S(1)}, u32[]{:S(2)}, u32[]{:S(2)}) collective-permute-start(bf16[768,384]{1,0:T(8,128)(2,1)S(1)} %bitcast.42), channel_id=1, source_target_pairs={{0,8},{4,12},{8,0},{12,4},{16,24},{20,28},{24,16},{28,20},{1,9},{5... | collective-permute-start | bytes 1769480 | tf_op jit(solution)/shard_map/ppermute | solution.py:26
  26.0 14.1 %collective-permute-start.4 = (bf16[768,384]{1,0:T(8,128)(2,1)S(1)}, bf16[768,384]{1,0:T(8,128)(2,1)S(1)}, u32[]{:S(2)}, u32[]{:S(2)}) collective-permute-start(bf16[768,384]{1,0:T(8,128)(2,1)S(1)} %bitcast.43), channel_id=1, source_target_pairs={{0,16},{4,20},{8,24},{12,28},{16,0},{20,4},{24,8},{28,12},{1,17},{... | collective-permute-start | bytes 1769480 | tf_op jit(solution)/shard_map/ppermute | solution.py:26
  27.3 12.9 %collective-permute-start.5 = (bf16[384,384]{1,0:T(8,128)(2,1)S(1)}, bf16[384,384]{1,0:T(8,128)(2,1)S(1)}, u32[]{:S(2)}, u32[]{:S(2)}) collective-permute-start(bf16[384,384]{1,0:T(8,128)(2,1)S(1)} %pad_maximum_fusion.2), channel_id=1, source_target_pairs={{0,1},{1,2},{2,3},{3,0},{4,5},{5,6},{6,7},{7,4},{8,9},{9,10},{10,1... | collective-permute-start | bytes 884744 | tf_op jit(solution)/shard_map/ppermute | solution.py:31
  27.3 14.1 %collective-permute-start.6 = (bf16[384,384]{1,0:T(8,128)(2,1)S(1)}, bf16[384,384]{1,0:T(8,128)(2,1)S(1)}, u32[]{:S(2)}, u32[]{:S(2)}) collective-permute-start(bf16[384,384]{1,0:T(8,128)(2,1)S(1)} %pad_maximum_fusion.2), channel_id=1, source_target_pairs={{0,3},{1,0},{2,1},{3,2},{4,7},{5,4},{6,5},{7,6},{8,11},{9,8},{10,9... | collective-permute-start | bytes 884744 | tf_op jit(solution)/shard_map/ppermute | solution.py:31
  51.9 28.1 %collective-permute-start.14 = (bf16[1536,384]{1,0:T(8,128)(2,1)S(1)}, bf16[1536,384]{1,0:T(8,128)(2,1)S(1)}, u32[]{:S(2)}, u32[]{:S(2)}) collective-permute-start(bf16[1536,384]{1,0:T(8,128)(2,1)S(1)} %bitcast.32), channel_id=1, source_target_pairs={{0,8},{4,12},{8,0},{12,4},{16,24},{20,28},{24,16},{28,20},{1,9},{5... | collective-permute-start | bytes 3538952 | tf_op jit(solution)/shard_map/ppermute | solution.py:26
  53.2 27.3 %collective-permute-start.15 = (bf16[1536,384]{1,0:T(8,128)(2,1)S(1)}, bf16[1536,384]{1,0:T(8,128)(2,1)S(1)}, u32[]{:S(2)}, u32[]{:S(2)}) collective-permute-start(bf16[1536,384]{1,0:T(8,128)(2,1)S(1)} %bitcast.33), channel_id=1, source_target_pairs={{0,16},{4,20},{8,24},{12,28},{16,0},{20,4},{24,8},{28,12},{1,17},{... | collective-permute-start | bytes 3538952 | tf_op jit(solution)/shard_map/ppermute | solution.py:26
  60.8 14.6 %collective-permute-start.16 = (bf16[2,896,128]{2,1,0:T(8,128)(2,1)S(1)}, bf16[2,896,128]{2,1,0:T(8,128)(2,1)S(1)}, u32[]{:S(2)}, u32[]{:S(2)}) collective-permute-start(bf16[2,896,128]{2,1,0:T(8,128)(2,1)S(1)} %get-tuple-element.174), channel_id=1, source_target_pairs={{0,1},{1,2},{2,3},{4,5},{5,6},{6,7},{8,9},{9,10},{10,11},{12,13},{... | collective-permute-start | bytes 1376264 | tf_op jit(solution)/shard_map/ppermute | solution.py:37
  75.6 21.7 %collective-permute-start.17 = (bf16[2,896,128]{2,1,0:T(8,128)(2,1)S(1)}, bf16[2,896,128]{2,1,0:T(8,128)(2,1)S(1)}, u32[]{:S(2)}, u32[]{:S(2)}) collective-permute-start(bf16[2,896,128]{2,1,0:T(8,128)(2,1)S(1)} %add_convert_fusion.1), channel_id=1, source_target_pairs={{0,2},{1,3},{4,6},{5,7},{8,10},{9,11},{12,14},{13,15},{16,18},{17,... | collective-permute-start | bytes 1376264 | tf_op jit(solution)/shard_map/ppermute | solution.py:37
  78.3 24.7 %collective-permute-start.19 = (bf16[512,768]{1,0:T(8,128)(2,1)S(1)}, bf16[512,768]{1,0:T(8,128)(2,1)S(1)}, u32[]{:S(2)}, u32[]{:S(2)}) collective-permute-start(bf16[512,768]{1,0:T(8,128)(2,1)S(1)} %bitcast.35), channel_id=1, source_target_pairs={{0,4},{4,0},{8,12},{12,8},{16,20},{20,16},{24,28},{28,24},{1,5},{5... | collective-permute-start | bytes 2359304 | tf_op jit(solution)/shard_map/ppermute | solution.py:26
  80.5 22.3 %collective-permute-start.20 = (bf16[768,384]{1,0:T(8,128)(2,1)S(1)}, bf16[768,384]{1,0:T(8,128)(2,1)S(1)}, u32[]{:S(2)}, u32[]{:S(2)}) collective-permute-start(bf16[768,384]{1,0:T(8,128)(2,1)S(1)} %slice.59), channel_id=1, source_target_pairs={{0,16},{4,20},{8,24},{12,28},{16,0},{20,4},{24,8},{28,12},{1,17},{... | collective-permute-start | bytes 1769480 | tf_op jit(solution)/shard_map/ppermute | solution.py:26
  81.8 21.0 %collective-permute-start.21 = (bf16[768,384]{1,0:T(8,128)(2,1)S(1)}, bf16[768,384]{1,0:T(8,128)(2,1)S(1)}, u32[]{:S(2)}, u32[]{:S(2)}) collective-permute-start(bf16[768,384]{1,0:T(8,128)(2,1)S(1)} %slice.60), channel_id=1, source_target_pairs={{0,8},{4,12},{8,0},{12,4},{16,24},{20,28},{24,16},{28,20},{1,9},{5... | collective-permute-start | bytes 1769480 | tf_op jit(solution)/shard_map/ppermute | solution.py:26
  126.0 13.6 %collective-permute-start.23 = (bf16[2,896,128]{2,1,0:T(8,128)(2,1)S(1)}, bf16[2,896,128]{2,1,0:T(8,128)(2,1)S(1)}, u32[]{:S(2)}, u32[]{:S(2)}) collective-permute-start(bf16[2,896,128]{2,1,0:T(8,128)(2,1)S(1)} %get-tuple-element.189), channel_id=1, source_target_pairs={{1,0},{2,1},{3,2},{5,4},{6,5},{7,6},{9,8},{10,9},{11,10},{13,12},{... | collective-permute-start | bytes 1376264 | tf_op jit(solution)/shard_map/ppermute | solution.py:37
  134.9 14.8 %collective-permute-start.27 = (bf16[768,384]{1,0:T(8,128)(2,1)S(1)}, bf16[768,384]{1,0:T(8,128)(2,1)S(1)}, u32[]{:S(2)}, u32[]{:S(2)}) collective-permute-start(bf16[768,384]{1,0:T(8,128)(2,1)S(1)} %get-tuple-element.205), channel_id=1, source_target_pairs={{0,16},{4,20},{8,24},{12,28},{16,0},{20,4},{24,8},{28,12},{1,17},{... | collective-permute-start | bytes 1769480 | tf_op jit(solution)/shard_map/ppermute | solution.py:26
  135.2 14.5 %collective-permute-start.28 = (bf16[768,384]{1,0:T(8,128)(2,1)S(1)}, bf16[768,384]{1,0:T(8,128)(2,1)S(1)}, u32[]{:S(2)}, u32[]{:S(2)}) collective-permute-start(bf16[768,384]{1,0:T(8,128)(2,1)S(1)} %get-tuple-element.206), channel_id=1, source_target_pairs={{0,8},{4,12},{8,0},{12,4},{16,24},{20,28},{24,16},{28,20},{1,9},{5... | collective-permute-start | bytes 1769480 | tf_op jit(solution)/shard_map/ppermute | solution.py:26
  139.8 20.2 %collective-permute-start.29 = (bf16[2,896,128]{2,1,0:T(8,128)(2,1)S(1)}, bf16[2,896,128]{2,1,0:T(8,128)(2,1)S(1)}, u32[]{:S(2)}, u32[]{:S(2)}) collective-permute-start(bf16[2,896,128]{2,1,0:T(8,128)(2,1)S(1)} %add_convert_fusion), channel_id=1, source_target_pairs={{2,0},{3,1},{6,4},{7,5},{10,8},{11,9},{14,12},{15,13},{18,16},{19,... | collective-permute-start | bytes 1376264 | tf_op jit(solution)/shard_map/ppermute | solution.py:37
  150.1 26.3 %collective-permute-start.32 = (bf16[1536,384]{1,0:T(8,128)(2,1)S(1)}, bf16[1536,384]{1,0:T(8,128)(2,1)S(1)}, u32[]{:S(2)}, u32[]{:S(2)}) collective-permute-start(bf16[1536,384]{1,0:T(8,128)(2,1)S(1)} %get-tuple-element.234), channel_id=1, source_target_pairs={{0,8},{4,12},{8,0},{12,4},{16,24},{20,28},{24,16},{28,20},{1,9},{5... | collective-permute-start | bytes 3538952 | tf_op jit(solution)/shard_map/ppermute | solution.py:26
  150.7 25.7 %collective-permute-start.33 = (bf16[1536,384]{1,0:T(8,128)(2,1)S(1)}, bf16[1536,384]{1,0:T(8,128)(2,1)S(1)}, u32[]{:S(2)}, u32[]{:S(2)}) collective-permute-start(bf16[1536,384]{1,0:T(8,128)(2,1)S(1)} %get-tuple-element.235), channel_id=1, source_target_pairs={{0,16},{4,20},{8,24},{12,28},{16,0},{20,4},{24,8},{28,12},{1,17},{... | collective-permute-start | bytes 3538952 | tf_op jit(solution)/shard_map/ppermute | solution.py:26
  191.6 14.3 %collective-permute-start.38 = (bf16[832,384]{1,0:T(8,128)(2,1)S(1)}, bf16[832,384]{1,0:T(8,128)(2,1)S(1)}, u32[]{:S(2)}, u32[]{:S(2)}) collective-permute-start(bf16[832,384]{1,0:T(8,128)(2,1)S(1)} %get-tuple-element.255), channel_id=1, source_target_pairs={{0,8},{4,12},{8,0},{12,4},{16,24},{20,28},{24,16},{28,20},{1,9},{5... | collective-permute-start | bytes 1916936 | tf_op jit(solution)/shard_map/ppermute | solution.py:26
  192.7 13.3 %collective-permute-start.39 = (bf16[832,384]{1,0:T(8,128)(2,1)S(1)}, bf16[832,384]{1,0:T(8,128)(2,1)S(1)}, u32[]{:S(2)}, u32[]{:S(2)}) collective-permute-start(bf16[832,384]{1,0:T(8,128)(2,1)S(1)} %get-tuple-element.256), channel_id=1, source_target_pairs={{0,16},{4,20},{8,24},{12,28},{16,0},{20,4},{24,8},{28,12},{1,17},{... | collective-permute-start | bytes 1916936 | tf_op jit(solution)/shard_map/ppermute | solution.py:26
  206.4 17.6 %collective-permute-start.44 = (bf16[384,384]{1,0:T(8,128)(2,1)S(1)}, bf16[384,384]{1,0:T(8,128)(2,1)S(1)}, u32[]{:S(2)}, u32[]{:S(2)}) collective-permute-start(bf16[384,384]{1,0:T(8,128)(2,1)S(1)} %shard_map.213), channel_id=1, source_target_pairs={{0,8},{4,12},{8,0},{12,4},{16,24},{20,28},{24,16},{28,20},{1,9},{5... | collective-permute-start | bytes 884744 | tf_op jit(solution)/shard_map/ppermute | solution.py:26
  207.5 16.5 %collective-permute-start.48 = (bf16[384,384]{1,0:T(8,128)(2,1)S(1)}, bf16[384,384]{1,0:T(8,128)(2,1)S(1)}, u32[]{:S(2)}, u32[]{:S(2)}) collective-permute-start(bf16[384,384]{1,0:T(8,128)(2,1)S(1)} %shard_map.213), channel_id=1, source_target_pairs={{0,16},{4,20},{8,24},{12,28},{16,0},{20,4},{24,8},{28,12},{1,17},{... | collective-permute-start | bytes 884744 | tf_op jit(solution)/shard_map/ppermute | solution.py:26
  208.7 15.3 %collective-permute-start.49 = (bf16[384,384]{1,0:T(8,128)(2,1)S(1)}, bf16[384,384]{1,0:T(8,128)(2,1)S(1)}, u32[]{:S(2)}, u32[]{:S(2)}) collective-permute-start(bf16[384,384]{1,0:T(8,128)(2,1)S(1)} %shard_map.213), channel_id=1, source_target_pairs={{0,24},{4,28},{8,16},{12,20},{16,8},{20,12},{24,0},{28,4},{1,25},{... | collective-permute-start | bytes 884744 | tf_op jit(solution)/shard_map/ppermute | solution.py:26
  (32 other events, 242.8 us)

commit v3 on v2

--- a/solution.py
+++ b/solution.py
@@ -14,7 +14,8 @@
 PIECES = 8
 CHUNK = 4 * D // PIECES
 QKV_BLOCKS = 3 * D // CHUNK
-SLAB = (PAIRS + 1) * FEAT
+EDGE = 16
+SLAB = PAIRS * FEAT + 2 * EDGE
 
 norm_epsilon = 1e-05
 low_type = jnp.bfloat16
@@ -225,10 +226,17 @@
     return total
 
 
-def states_at(refs, b, p):
-    packed = added(refs, b, pl.ds(aligned(p, FEAT), FEAT))
-    sums = low(added(refs, b, slice(PAIRS * FEAT, SLAB)))
-    return unpack_state(packed, sums, p)
+def sums_of(refs):
+    found = []
+    gap = jnp.zeros((HEAD - EDGE, FEAT), wide_type)
+    for b in range(refs[0].shape[0]):
+        edges = added(refs, b, slice(PAIRS * FEAT, SLAB))
+        found.append(low(jnp.concatenate([edges[:EDGE], gap, edges[EDGE:], gap], axis=0).T))
+    return found
+
+
+def states_at(refs, b, p, sums):
+    return unpack_state(added(refs, b, pair_at(p)), sums[b], p)
 
 
 def maps_kernel(small, maps, vectors, weight):
@@ -353,7 +361,9 @@
     empty = tuple(jnp.zeros((FEAT, FEAT), wide_type) for _ in range(seqs))
     sums = lax.fori_loop(0, PAIRS, pair, empty)
     for b in range(seqs):
-        state[b, PAIRS * FEAT :, :] = low(sums[b])
+        turned = low(sums[b].T)
+        state[b, PAIRS * FEAT : PAIRS * FEAT + EDGE, :] = turned[:EDGE]
+        state[b, PAIRS * FEAT + EDGE :, :] = turned[HEAD : HEAD + EDGE]
 
 
 def queries_kernel(place, normed, keyed, fk_t, maps, *refs):
@@ -397,10 +407,12 @@
     seqs = priors[0].shape[0]
     length = tokens.shape[0] // seqs
 
+    sums = sums_of(priors)
+
     def pair(p, carry):
         for b in range(seqs):
             here = slice(b * length, (b + 1) * length)
-            states = states_at(priors, b, p)
+            states = states_at(priors, b, p, sums)
             found = []
             for side in range(2):
                 rows = pair_at(2 * p + side)
@@ -591,12 +603,14 @@
     seqs = priors[0].shape[0]
     length = keyed.shape[0] // seqs
 
+    sums = sums_of(priors)
+
     def pair(p, carry):
         for b in range(seqs):
             here = slice(b * length, (b + 1) * length)
             values = with_ones(keyed[here, pair_at(VALUES + p)])
             outer = joined(d_num, d_den, here, p)
-            states = states_at(priors, b, p)
+            states = states_at(priors, b, p, sums)
             for side in range(2):
                 rows = pair_at(2 * p + side)
                 link = linked(outer[side], values[side])
@@ -655,11 +669,13 @@
     seqs = laters[0].shape[0]
     length = keyed.shape[0] // seqs
 
+    sums = sums_of(laters)
+
     def pair(p, carry):
         for b in range(seqs):
             here = slice(b * length, (b + 1) * length)
             values = with_ones(keyed[here, pair_at(VALUES + p)])
-            states = states_at(laters, b, p)
+            states = states_at(laters, b, p, sums)
             found = []
             for side in range(2):
                 rows = pl.ds(aligned(2 * p + side, FEAT), FEAT)
@@ -788,7 +804,7 @@
         tiny[s, rows : rows + 8, :] = low(jnp.concatenate(lines, axis=0))
 
 
-def lay_in_kernel(place, even, odd, qkv, out, tiny):
+def lay_in_kernel(place, even, odd, qkv, out, feature, rest):
     rows = qkv.shape[0]
     for k in range(PIECES):
         block = place[0] ^ k
@@ -802,13 +818,18 @@
         def _():
             out[:, chunk_at(block - QKV_BLOCKS)] = wide(piece[:rows])
 
-        @pl.when(block < tiny.shape[0] // TINY_ROWS)
-        def _():
-            for j in range(TINY_ROWS // TINY_TILE):
+        for j in range(TINY_ROWS // TINY_TILE):
+
+            @pl.when(block < rows // TINY_ROWS)
+            def _():
                 start = pl.multiple_of(block * TINY_ROWS + j * TINY_TILE, TINY_TILE)
-                tiny[pl.ds(start, TINY_TILE), :] = wide(
+                feature[pl.ds(start, TINY_TILE), :] = wide(
                     piece[rows:, j * FEAT : (j + 1) * FEAT]
                 )
+
+        @pl.when(block == rows // TINY_ROWS)
+        def _():
+            rest[...] = wide(piece[rows : rows + 8, :FEAT])
 
 
 def lay_mlp_kernel(place, even, odd, up, down, ordered):
@@ -1154,18 +1175,18 @@
     grad_down = grad_down.reshape(-1, D)
     in_flips, grad_up, grad_down = lax.optimization_barrier((in_flips, grad_up, grad_down))
     in_sums = share_pair(in_flips)
-    grad_qkv, grad_out, tiny = call(
+    grad_qkv, grad_out, grad_feature, d_vectors = call(
         lay_in_kernel,
         2,
         (
             whole((rows, 3 * D), wide_type),
             whole((rows, D), wide_type),
-            whole((tiny_size(rows), FEAT), wide_type),
+            whole((rows, FEAT), wide_type),
+            whole((8, FEAT), wide_type),
         ),
         scalar_first(2),
     )(spot, *in_sums)
-    grad_feature = tiny[:rows]
-    d_vectors = tiny[rows : rows + 8].reshape(4, 2 * FEAT)[:, :rows]
+    d_vectors = d_vectors.reshape(4, 2 * FEAT)[:, :rows]
     return (
         block_out.reshape(tokens.shape),
         grad_tokens.reshape(tokens.shape),

time: 245 us -> 241 us (0.984)
    ppermute x4, waiting for transfers between devices: 24.5 us -> 19.2 us  [slide(): return lax.ppermute(value, 'shard', pairs)]
    ppermute x12, waiting for transfers between devices: 36.8 us -> 39.9 us  [spin(): lax.ppermute(value, 'shard', [(i, (i + step) % count) for i in range(coun...]
  transfers between devices with their start and end apart: 52 -> 52, of which waited for: 20 -> 23; matrix products, arithmetic and copies ran while one was open for 3% -> 3% of each run, Pallas kernels for 27% -> 28%
where the time goes in v3:
time: 241 us; the launch traced here: 240 us
  waiting for transfers between devices  89.5 us (37%)
  Pallas kernels  86.1 us (36%)
  starting transfers between devices  54.2 us (22%)
  local copies, waits for them, and re-layouts  6.19 us (3%)
  other arithmetic  3.05 us (1%)
    ppermute x12, waiting for transfers between devices, spin(): lax.ppermute(value, 'shard', [(i, (i + step) % count) for i in range(coun...  39.9 us
    ppermute x36, waiting for transfers between devices, flip(): return lax.ppermute(value, 'rep', [(i, i ^ bit) for i in range(count)])  30.4 us
    ppermute x36, starting transfers between devices, flip(): return lax.ppermute(value, 'rep', [(i, i ^ bit) for i in range(count)])  29.7 us
    ppermute x4, waiting for transfers between devices, slide(): return lax.ppermute(value, 'shard', pairs)  19.2 us
    ppermute x12, starting transfers between devices, spin(): lax.ppermute(value, 'shard', [(i, (i + step) % count) for i in range(coun...  16.4 us
    pallas_call x1, Pallas kernels, shards(): call(mlp_kernel, 20, (whole((count, D), wide_type), whole((count, D)), wh...  15.1 us
    pallas_call x1, Pallas kernels, shards(): call(lambda *refs: local_keys_kernel(*refs, seqs=seqs), 5, (whole((HEADS...  8.59 us
    ppermute x4, starting transfers between devices, slide(): return lax.ppermute(value, 'shard', pairs)  8.03 us
  transfers between devices with their start and end apart: 52, of which 23 were waited for; matrix products, arithmetic and copies ran while one was open for 3% of the time, Pallas kernels for 28%

profile of v3, /device:TPU:9, one launch (start us, length us, event | category | flops | bytes accessed | tf_op | source)
XLA Modules:
  0.0 240.1 jit_solution(970452674041297380)
XLA Ops:
  12.6 8.7 %collective-permute-done.1.refs_2_ = bf16[264,384]{1,0:T(8,128)(2,1)S(1)} collective-permute-done((bf16[264,384]{1,0:T(8,128)(2,1)S(1)}, bf16[264,384]{1,0:T(8,128)(2,1)S(1)}, u32[]{:S(2)}, u32[]{:S(2)}) %collective-permute-start.1) | collective-permute-done | bytes 202784 | tf_op jit(solution)/shard_map/ppermute | solution.py:32
  29.0 10.3 %collective-permute-done.3.refs_2_ = bf16[768,384]{1,0:T(8,128)(2,1)S(1)} collective-permute-done((bf16[768,384]{1,0:T(8,128)(2,1)S(1)}, bf16[768,384]{1,0:T(8,128)(2,1)S(1)}, u32[]{:S(2)}, u32[]{:S(2)}) %collective-permute-start.3) | collective-permute-done | bytes 589856 | tf_op jit(solution)/shard_map/ppermute | solution.py:27
  44.0 5.4 %collective-permute-done.7 = bf16[384,384]{1,0:T(8,128)(2,1)S(1)} collective-permute-done((bf16[384,384]{1,0:T(8,128)(2,1)S(1)}, bf16[384,384]{1,0:T(8,128)(2,1)S(1)}, u32[]{:S(2)}, u32[]{:S(2)}) %collective-permute-start.7) | collective-permute-done | bytes 294944 | tf_op jit(solution)/shard_map/ppermute | solution.py:27
  54.4 6.5 %shard_map.197 = (bf16[512,768]{1,0:T(8,128)(2,1)S(1)}, bf16[512,1536]{1,0:T(8,128)(2,1)S(1)}, bf16[512,1536]{1,0:T(8,128)(2,1)S(1)}, bf16[1536,512]{1,0:T(8,128...) custom-call(s32[1]{0:T(128)} %bitcast.12.place, bf16[512,768]{1,0:T(8,128)(2,1)S(1)} %bitcast.39, ...), custom_call_target="tpu_custom_call" | custom-call | flops 16000000000 | bytes 48000000 | tf_op jit(solution)/shard_map/pallas_call | solution.py:964
  62.9 6.8 %shard_map.198 = (bf16[768,512]{1,0:T(8,128)(2,1)S(1)}, bf16[512,768]{1,0:T(8,128)(2,1)S(1)}, bf16[512,1536]{1,0:T(8,128)(2,1)S(1)}, bf16[1536,512]{1,0:T(8,128)...) custom-call(s32[1]{0:T(128)} %bitcast.12.place, ...), custom_call_target="tpu_custom_call" | custom-call | flops 17999998976 | bytes 54000000 | tf_op jit(solution)/shard_map/pallas_call | solution.py:979
  69.7 4.8 %collective-permute-done.16.refs_0_ = bf16[2,800,128]{2,1,0:T(8,128)(2,1)S(1)} collective-permute-done((bf16[2,800,128]{2,1,0:T(8,128)(2,1)S(1)}, bf16[2,800,128]{2,1,0:T(8,128)(2,1)S(1)}, u32[]{:S(2)}, u32[]{:S(2)}) %collective-permute-start.16) | collective-permute-done | bytes 409632 | tf_op jit(solution)/shard_map/ppermute | solution.py:38
  82.2 11.9 %collective-permute-done.17.refs_1_ = bf16[2,800,128]{2,1,0:T(8,128)(2,1)S(1)} collective-permute-done((bf16[2,800,128]{2,1,0:T(8,128)(2,1)S(1)}, bf16[2,800,128]{2,1,0:T(8,128)(2,1)S(1)}, u32[]{:S(2)}, u32[]{:S(2)}) %collective-permute-start.17) | collective-permute-done | bytes 409632 | tf_op jit(solution)/shard_map/ppermute | solution.py:38
  94.2 5.1 %shard_map.199 = (bf16[512,768]{1,0:T(8,128)(2,1)S(1)}, f32[512,768]{1,0:T(8,128)S(1)}, f32[512,768]{1,0:T(8,128)S(1)}, bf16[512,768]{1,0:T(8,128)(2,1)S(1)}, bf16[768,512]{1,0:T(8,128)(2,1)S(1)}) custom-call(bf16[512,768]{1,0:T(8,128)(2,1)S(1)} %bitcast.40, f32[4,768]{1,0:T(4,128)S(1)} %get-tuple-element.166.vectors, ...), custom_call_target="tpu_custom_call" | custom-call | flops 10000000000 | bytes 30000000 | tf_op jit(solution)/shard_map/pallas_call | solution.py:997
  101.7 15.1 %shard_map.200 = (f32[512,768]{1,0:T(8,128)S(1)}, bf16[512,768]{1,0:T(8,128)(2,1)S(1)}, f32[512,768]{1,0:T(8,128)S(1)}, bf16[512,768]{1,0:T(8,128)(2,1)S(1)}, bf...) custom-call(bf16[512,768]{1,0:T(8,128)(2,1)S(1)} %get-tuple-element., ...), custom_call_target="tpu_custom_call" | custom-call | flops 40000000000 | bytes 120000000 | tf_op jit(solution)/shard_map/pallas_call | solution.py:1019
  119.2 3.9 %shard_map.201 = (f32[512,768]{1,0:T(8,128)S(1)}, bf16[512,768]{1,0:T(8,128)(2,1)S(1)}, f32[2,768]{1,0:T(2,128)S(1)}, bf16[512,768]{1,0:T(8,128)(2,1)S(1)}, bf16...) custom-call(f32[512,768]{1,0:T(8,128)S(1)} %get-tuple-element.187.back_sum, ...), custom_call_target="tpu_custom_call" | custom-call | flops 10000000000 | bytes 30000000 | tf_op jit(solution)/shard_map/pallas_call | solution.py:1042
  125.1 6.9 %shard_map.204 = (bf16[1536,384]{1,0:T(8,128)(2,1)S(1)}, bf16[1536,384]{1,0:T(8,128)(2,1)S(1)}, bf16[1536,384]{1,0:T(8,128)(2,1)S(1)}, bf16[768,384]{1,0:T(8,128)(2,1)S(1)}, bf16[768,384]{1,0:T(8,128)(2,1)S(1)}) custom-call(bf16[768,512]{1,0:T(8,128)(2,1)S(1)} %get-tuple-element.200.second_t, bf16[768,512]{1,0:T(8,128)(2,1)S(1)} %get-tuple-element.201.second_other_t, ...), custom_call_target="tpu_custom_call" | custom-call | flops 14000000000 | bytes 42000000 | tf_op jit(solution)/shard_map/pallas_call | solution.py:1063
  137.3 7.2 %shard_map.202 = (bf16[512,768]{1,0:T(8,128)(2,1)S(1)}, f32[768,128]{1,0:T(8,128)S(1)}, bf16[768,512]{1,0:T(8,128)(2,1)}) custom-call(bf16[512,768]{1,0:T(8,128)(2,1)S(1)} %copy-done.3, bf16[512,1536]{1,0:T(8,128)(2,1)S(1)} %get-tuple-element.170.keyed.refs_0_, bf16[6,256,256]{2,1,0:T(8,128)(2,1)S(1)} %get-tuple-element.167.maps, ...), custom_call_target="tpu_custom_call" | custom-call | flops 12000000000 | bytes 36000000 | tf_op jit(solution)/shard_map/pallas_call | solution.py:1069
  148.4 8.6 %shard_map.206 = (f32[1536,512]{1,0:T(8,128)S(1)}, f32[512,768]{1,0:T(8,128)S(1)}) custom-call(bf16[512,1536]{1,0:T(8,128)(2,1)S(1)} %get-tuple-element.170.keyed.refs_0_, bf16[1536,512]{1,0:T(8,128)(2,1)S(1)} %get-tuple-element.173.fq_t.refs_1_, bf16[512,1536]{1,0:T(8,128)(2,1)S(1)} %get-tuple-element.217.refs_2_.fk, ...), custom_call_target="tpu_custom_call" | custom-call | flops 10000000000 | bytes 30000000 | tf_op jit(solution)/shard_map/pallas_call | solution.py:1080
  157.0 6.1 %shard_map.207 = (bf16[512,1536]{1,0:T(8,128)(2,1)S(1)}, f32[768,128]{1,0:T(8,128)S(1)}, bf16[4,512,384]{2,1,0:T(8,128)(2,1)S(1)}, bf16[768,512]{1,0:T(8,128)(2,1)}) custom-call(s32[1]{0:T(128)} %bitcast.12.place, bf16[512,1536]{1,0:T(8,128)(2,1)S(1)} %get-tuple-element.170.keyed.refs_0_, bf16[512,1536]{1,0:T(8,128)(2,1)S(1)} %get-tuple-element.217.refs_2_.fk, ...), custom_call_target="tpu_custom_call" | custom-call | flops 14000000000 | bytes 42000000 | tf_op jit(solution)/shard_map/pallas_call | solution.py:1088
  165.2 4.7 %shard_map.208 = (bf16[512,768]{1,0:T(8,128)(2,1)}, bf16[512,768]{1,0:T(8,128)(2,1)}, bf16[4,240,128]{2,1,0:T(8,128)(2,1)S(1)}) custom-call(bf16[512,768]{1,0:T(8,128)(2,1)S(1)} %bitcast.41, f32[4,768]{1,0:T(4,128)S(1)} %get-tuple-element.166.vectors, f32[512,768]{1,0:T(8,128)S(1)} %shard_map.203.early, bf16[512,1536]{1,0:T(8,128)(2,1)S(1)} %get-tuple-element.223.d_keyed, ...), custom_call_target="tpu_custom_call" | custom-call | flops 14000000000 | bytes 42000000 | tf_op jit(solution)/shard_map/pallas_call | solution.py:1100
  169.9 3.1 %collective-permute-done.32.refs_1_ = bf16[1536,384]{1,0:T(8,128)(2,1)S(1)} collective-permute-done((bf16[1536,384]{1,0:T(8,128)(2,1)S(1)}, bf16[1536,384]{1,0:T(8,128)(2,1)S(1)}, u32[]{:S(2)}, u32[]{:S(2)}) %collective-permute-start.32) | collective-permute-done | bytes 1179680 | tf_op jit(solution)/shard_map/ppermute | solution.py:27
  175.0 5.0 %shard_map.210 = (bf16[832,384]{1,0:T(8,128)(2,1)S(1)}, bf16[832,384]{1,0:T(8,128)(2,1)S(1)}, bf16[832,384]{1,0:T(8,128)(2,1)S(1)}, bf16[416,384]{1,0:T(8,128)(2,1)S(1)}, bf16[416,384]{1,0:T(8,128)(2,1)S(1)}) custom-call(s32[1]{0:T(128)} %bitcast.12.place, bf16[512,768]{1,0:T(8,128)(2,1)S(1)} %get-tuple-element.194.d_queries, ...), custom_call_target="tpu_custom_call" | custom-call | flops 14000000000 | bytes 42000000 | tf_op jit(solution)/shard_map/pallas_call | solution.py:1124
  184.1 4.0 %collective-permute-done.37.refs_2_ = bf16[384,384]{1,0:T(8,128)(2,1)S(1)} collective-permute-done((bf16[384,384]{1,0:T(8,128)(2,1)S(1)}, bf16[384,384]{1,0:T(8,128)(2,1)S(1)}, u32[]{:S(2)}, u32[]{:S(2)}) %collective-permute-start.37) | collective-permute-done | bytes 294944 | tf_op jit(solution)/shard_map/ppermute | solution.py:32
  189.5 3.1 %collective-permute-start.40 = (bf16[384,384]{1,0:T(8,128)(2,1)S(1)}, bf16[384,384]{1,0:T(8,128)(2,1)S(1)}, u32[]{:S(2)}, u32[]{:S(2)}) collective-permute-start(bf16[384,384]{1,0:T(8,128)(2,1)S(1)} %get-tuple-element.259), channel_id=1, source_target_pairs={{0,2},{1,3},{2,0},{3,1},{4,6},{5,7},{6,4},{7,5},{8,10},{9,11},{10,... | collective-permute-start | bytes 884744 | tf_op jit(solution)/shard_map/ppermute | solution.py:32
  192.7 11.9 %collective-permute-done.40.refs_1_ = bf16[384,384]{1,0:T(8,128)(2,1)S(1)} collective-permute-done((bf16[384,384]{1,0:T(8,128)(2,1)S(1)}, bf16[384,384]{1,0:T(8,128)(2,1)S(1)}, u32[]{:S(2)}, u32[]{:S(2)}) %collective-permute-start.40) | collective-permute-done | bytes 294944 | tf_op jit(solution)/shard_map/ppermute | solution.py:32
  207.7 3.1 %collective-permute-start.42 = (bf16[208,384]{1,0:T(8,128)(2,1)S(1)}, bf16[208,384]{1,0:T(8,128)(2,1)S(1)}, u32[]{:S(2)}, u32[]{:S(2)}) collective-permute-start(bf16[208,384]{1,0:T(8,128)(2,1)S(1)} %get-tuple-element.265), channel_id=1, source_target_pairs={{0,2},{1,3},{2,0},{3,1},{4,6},{5,7},{6,4},{7,5},{8,10},{9,11},{10,... | collective-permute-start | bytes 479240 | tf_op jit(solution)/shard_map/ppermute | solution.py:32
  212.3 4.5 %collective-permute-done.42.refs_1_ = bf16[208,384]{1,0:T(8,128)(2,1)S(1)} collective-permute-done((bf16[208,384]{1,0:T(8,128)(2,1)S(1)}, bf16[208,384]{1,0:T(8,128)(2,1)S(1)}, u32[]{:S(2)}, u32[]{:S(2)}) %collective-permute-start.42) | collective-permute-done | bytes 159776 | tf_op jit(solution)/shard_map/ppermute | solution.py:32
  216.8 6.7 %collective-permute-done.43.refs_2_ = bf16[208,384]{1,0:T(8,128)(2,1)S(1)} collective-permute-done((bf16[208,384]{1,0:T(8,128)(2,1)S(1)}, bf16[208,384]{1,0:T(8,128)(2,1)S(1)}, u32[]{:S(2)}, u32[]{:S(2)}) %collective-permute-start.43) | collective-permute-done | bytes 159776 | tf_op jit(solution)/shard_map/ppermute | solution.py:32
  231.1 3.2 %collective-permute-done.47 = bf16[208,384]{1,0:T(8,128)(2,1)S(1)} collective-permute-done((bf16[208,384]{1,0:T(8,128)(2,1)S(1)}, bf16[208,384]{1,0:T(8,128)(2,1)S(1)}, u32[]{:S(2)}, u32[]{:S(2)}) %collective-permute-start.47) | collective-permute-done | bytes 159776 | tf_op jit(solution)/shard_map/ppermute | solution.py:27
  (135 shorter events, 82.3 us)
Async XLA Ops:
  4.6 16.7 %collective-permute-start.1 = (bf16[264,384]{1,0:T(8,128)(2,1)S(1)}, bf16[264,384]{1,0:T(8,128)(2,1)S(1)}, u32[]{:S(2)}, u32[]{:S(2)}) collective-permute-start(bf16[264,384]{1,0:T(8,128)(2,1)S(1)} %maximum_maximum_fusion.refs_0_), channel_id=1, source_target_pairs={{0,2},{1,3},{2,0},{3,1},{4,6},{5,7},{6,4},{7,5},{8,10},{9,11},{10,... | collective-permute-start | bytes 608264 | tf_op jit(solution)/shard_map/ppermute | solution.py:32
  5.7 18.5 %collective-permute-start.2 = (bf16[264,384]{1,0:T(8,128)(2,1)S(1)}, bf16[264,384]{1,0:T(8,128)(2,1)S(1)}, u32[]{:S(2)}, u32[]{:S(2)}) collective-permute-start(bf16[264,384]{1,0:T(8,128)(2,1)S(1)} %maximum_maximum_fusion.refs_0_), channel_id=1, source_target_pairs={{0,3},{1,0},{2,1},{3,2},{4,7},{5,4},{6,5},{7,6},{8,11},{9,8},{10,9... | collective-permute-start | bytes 608264 | tf_op jit(solution)/shard_map/ppermute | solution.py:32
  24.8 14.5 %collective-permute-start.3 = (bf16[768,384]{1,0:T(8,128)(2,1)S(1)}, bf16[768,384]{1,0:T(8,128)(2,1)S(1)}, u32[]{:S(2)}, u32[]{:S(2)}) collective-permute-start(bf16[768,384]{1,0:T(8,128)(2,1)S(1)} %bitcast.42), channel_id=1, source_target_pairs={{0,8},{4,12},{8,0},{12,4},{16,24},{20,28},{24,16},{28,20},{1,9},{5... | collective-permute-start | bytes 1769480 | tf_op jit(solution)/shard_map/ppermute | solution.py:27
  26.0 14.1 %collective-permute-start.4 = (bf16[768,384]{1,0:T(8,128)(2,1)S(1)}, bf16[768,384]{1,0:T(8,128)(2,1)S(1)}, u32[]{:S(2)}, u32[]{:S(2)}) collective-permute-start(bf16[768,384]{1,0:T(8,128)(2,1)S(1)} %bitcast.43), channel_id=1, source_target_pairs={{0,16},{4,20},{8,24},{12,28},{16,0},{20,4},{24,8},{28,12},{1,17},{... | collective-permute-start | bytes 1769480 | tf_op jit(solution)/shard_map/ppermute | solution.py:27
  27.3 12.9 %collective-permute-start.5 = (bf16[384,384]{1,0:T(8,128)(2,1)S(1)}, bf16[384,384]{1,0:T(8,128)(2,1)S(1)}, u32[]{:S(2)}, u32[]{:S(2)}) collective-permute-start(bf16[384,384]{1,0:T(8,128)(2,1)S(1)} %pad_maximum_fusion.2), channel_id=1, source_target_pairs={{0,1},{1,2},{2,3},{3,0},{4,5},{5,6},{6,7},{7,4},{8,9},{9,10},{10,1... | collective-permute-start | bytes 884744 | tf_op jit(solution)/shard_map/ppermute | solution.py:32
  27.3 14.1 %collective-permute-start.6 = (bf16[384,384]{1,0:T(8,128)(2,1)S(1)}, bf16[384,384]{1,0:T(8,128)(2,1)S(1)}, u32[]{:S(2)}, u32[]{:S(2)}) collective-permute-start(bf16[384,384]{1,0:T(8,128)(2,1)S(1)} %pad_maximum_fusion.2), channel_id=1, source_target_pairs={{0,3},{1,0},{2,1},{3,2},{4,7},{5,4},{6,5},{7,6},{8,11},{9,8},{10,9... | collective-permute-start | bytes 884744 | tf_op jit(solution)/shard_map/ppermute | solution.py:32
  51.9 27.5 %collective-permute-start.14 = (bf16[1536,384]{1,0:T(8,128)(2,1)S(1)}, bf16[1536,384]{1,0:T(8,128)(2,1)S(1)}, u32[]{:S(2)}, u32[]{:S(2)}) collective-permute-start(bf16[1536,384]{1,0:T(8,128)(2,1)S(1)} %bitcast.32), channel_id=1, source_target_pairs={{0,8},{4,12},{8,0},{12,4},{16,24},{20,28},{24,16},{28,20},{1,9},{5... | collective-permute-start | bytes 3538952 | tf_op jit(solution)/shard_map/ppermute | solution.py:27
  53.2 27.3 %collective-permute-start.15 = (bf16[1536,384]{1,0:T(8,128)(2,1)S(1)}, bf16[1536,384]{1,0:T(8,128)(2,1)S(1)}, u32[]{:S(2)}, u32[]{:S(2)}) collective-permute-start(bf16[1536,384]{1,0:T(8,128)(2,1)S(1)} %bitcast.33), channel_id=1, source_target_pairs={{0,16},{4,20},{8,24},{12,28},{16,0},{20,4},{24,8},{28,12},{1,17},{... | collective-permute-start | bytes 3538952 | tf_op jit(solution)/shard_map/ppermute | solution.py:27
  60.9 13.6 %collective-permute-start.16 = (bf16[2,800,128]{2,1,0:T(8,128)(2,1)S(1)}, bf16[2,800,128]{2,1,0:T(8,128)(2,1)S(1)}, u32[]{:S(2)}, u32[]{:S(2)}) collective-permute-start(bf16[2,800,128]{2,1,0:T(8,128)(2,1)S(1)} %get-tuple-element.175), channel_id=1, source_target_pairs={{0,1},{1,2},{2,3},{4,5},{5,6},{6,7},{8,9},{9,10},{10,11},{12,13},{... | collective-permute-start | bytes 1228808 | tf_op jit(solution)/shard_map/ppermute | solution.py:38
  74.6 19.6 %collective-permute-start.17 = (bf16[2,800,128]{2,1,0:T(8,128)(2,1)S(1)}, bf16[2,800,128]{2,1,0:T(8,128)(2,1)S(1)}, u32[]{:S(2)}, u32[]{:S(2)}) collective-permute-start(bf16[2,800,128]{2,1,0:T(8,128)(2,1)S(1)} %add_convert_fusion.1), channel_id=1, source_target_pairs={{0,2},{1,3},{4,6},{5,7},{8,10},{9,11},{12,14},{13,15},{16,18},{17,... | collective-permute-start | bytes 1228808 | tf_op jit(solution)/shard_map/ppermute | solution.py:38
  77.3 22.7 %collective-permute-start.19 = (bf16[512,768]{1,0:T(8,128)(2,1)S(1)}, bf16[512,768]{1,0:T(8,128)(2,1)S(1)}, u32[]{:S(2)}, u32[]{:S(2)}) collective-permute-start(bf16[512,768]{1,0:T(8,128)(2,1)S(1)} %bitcast.35), channel_id=1, source_target_pairs={{0,4},{4,0},{8,12},{12,8},{16,20},{20,16},{24,28},{28,24},{1,5},{5... | collective-permute-start | bytes 2359304 | tf_op jit(solution)/shard_map/ppermute | solution.py:27
  80.5 19.3 %collective-permute-start.20 = (bf16[768,384]{1,0:T(8,128)(2,1)S(1)}, bf16[768,384]{1,0:T(8,128)(2,1)S(1)}, u32[]{:S(2)}, u32[]{:S(2)}) collective-permute-start(bf16[768,384]{1,0:T(8,128)(2,1)S(1)} %slice.51), channel_id=1, source_target_pairs={{0,16},{4,20},{8,24},{12,28},{16,0},{20,4},{24,8},{28,12},{1,17},{... | collective-permute-start | bytes 1769480 | tf_op jit(solution)/shard_map/ppermute | solution.py:27
  81.8 18.0 %collective-permute-start.21 = (bf16[768,384]{1,0:T(8,128)(2,1)S(1)}, bf16[768,384]{1,0:T(8,128)(2,1)S(1)}, u32[]{:S(2)}, u32[]{:S(2)}) collective-permute-start(bf16[768,384]{1,0:T(8,128)(2,1)S(1)} %slice.52), channel_id=1, source_target_pairs={{0,8},{4,12},{8,0},{12,4},{16,24},{20,28},{24,16},{28,20},{1,9},{5... | collective-permute-start | bytes 1769480 | tf_op jit(solution)/shard_map/ppermute | solution.py:27
  132.0 14.6 %collective-permute-start.27 = (bf16[768,384]{1,0:T(8,128)(2,1)S(1)}, bf16[768,384]{1,0:T(8,128)(2,1)S(1)}, u32[]{:S(2)}, u32[]{:S(2)}) collective-permute-start(bf16[768,384]{1,0:T(8,128)(2,1)S(1)} %get-tuple-element.206), channel_id=1, source_target_pairs={{0,16},{4,20},{8,24},{12,28},{16,0},{20,4},{24,8},{28,12},{1,17},{... | collective-permute-start | bytes 1769480 | tf_op jit(solution)/shard_map/ppermute | solution.py:27
  132.3 14.3 %collective-permute-start.28 = (bf16[768,384]{1,0:T(8,128)(2,1)S(1)}, bf16[768,384]{1,0:T(8,128)(2,1)S(1)}, u32[]{:S(2)}, u32[]{:S(2)}) collective-permute-start(bf16[768,384]{1,0:T(8,128)(2,1)S(1)} %get-tuple-element.207), channel_id=1, source_target_pairs={{0,8},{4,12},{8,0},{12,4},{16,24},{20,28},{24,16},{28,20},{1,9},{5... | collective-permute-start | bytes 1769480 | tf_op jit(solution)/shard_map/ppermute | solution.py:27
  135.8 21.2 %collective-permute-start.29 = (bf16[2,800,128]{2,1,0:T(8,128)(2,1)S(1)}, bf16[2,800,128]{2,1,0:T(8,128)(2,1)S(1)}, u32[]{:S(2)}, u32[]{:S(2)}) collective-permute-start(bf16[2,800,128]{2,1,0:T(8,128)(2,1)S(1)} %add_convert_fusion), channel_id=1, source_target_pairs={{2,0},{3,1},{6,4},{7,5},{10,8},{11,9},{14,12},{15,13},{18,16},{19,... | collective-permute-start | bytes 1228808 | tf_op jit(solution)/shard_map/ppermute | solution.py:38
  147.0 26.1 %collective-permute-start.32 = (bf16[1536,384]{1,0:T(8,128)(2,1)S(1)}, bf16[1536,384]{1,0:T(8,128)(2,1)S(1)}, u32[]{:S(2)}, u32[]{:S(2)}) collective-permute-start(bf16[1536,384]{1,0:T(8,128)(2,1)S(1)} %get-tuple-element.235), channel_id=1, source_target_pairs={{0,8},{4,12},{8,0},{12,4},{16,24},{20,28},{24,16},{28,20},{1,9},{5... | collective-permute-start | bytes 3538952 | tf_op jit(solution)/shard_map/ppermute | solution.py:27
  147.8 25.7 %collective-permute-start.33 = (bf16[1536,384]{1,0:T(8,128)(2,1)S(1)}, bf16[1536,384]{1,0:T(8,128)(2,1)S(1)}, u32[]{:S(2)}, u32[]{:S(2)}) collective-permute-start(bf16[1536,384]{1,0:T(8,128)(2,1)S(1)} %get-tuple-element.236), channel_id=1, source_target_pairs={{0,16},{4,20},{8,24},{12,28},{16,0},{20,4},{24,8},{28,12},{1,17},{... | collective-permute-start | bytes 3538952 | tf_op jit(solution)/shard_map/ppermute | solution.py:27
  188.4 16.2 %collective-permute-start.38 = (bf16[832,384]{1,0:T(8,128)(2,1)S(1)}, bf16[832,384]{1,0:T(8,128)(2,1)S(1)}, u32[]{:S(2)}, u32[]{:S(2)}) collective-permute-start(bf16[832,384]{1,0:T(8,128)(2,1)S(1)} %get-tuple-element.256), channel_id=1, source_target_pairs={{0,8},{4,12},{8,0},{12,4},{16,24},{20,28},{24,16},{28,20},{1,9},{5... | collective-permute-start | bytes 1916936 | tf_op jit(solution)/shard_map/ppermute | solution.py:27
  188.7 15.9 %collective-permute-start.39 = (bf16[832,384]{1,0:T(8,128)(2,1)S(1)}, bf16[832,384]{1,0:T(8,128)(2,1)S(1)}, u32[]{:S(2)}, u32[]{:S(2)}) collective-permute-start(bf16[832,384]{1,0:T(8,128)(2,1)S(1)} %get-tuple-element.257), channel_id=1, source_target_pairs={{0,16},{4,20},{8,24},{12,28},{16,0},{20,4},{24,8},{28,12},{1,17},{... | collective-permute-start | bytes 1916936 | tf_op jit(solution)/shard_map/ppermute | solution.py:27
  189.5 15.0 %collective-permute-start.40 = (bf16[384,384]{1,0:T(8,128)(2,1)S(1)}, bf16[384,384]{1,0:T(8,128)(2,1)S(1)}, u32[]{:S(2)}, u32[]{:S(2)}) collective-permute-start(bf16[384,384]{1,0:T(8,128)(2,1)S(1)} %get-tuple-element.259), channel_id=1, source_target_pairs={{0,2},{1,3},{2,0},{3,1},{4,6},{5,7},{6,4},{7,5},{8,10},{9,11},{10,... | collective-permute-start | bytes 884744 | tf_op jit(solution)/shard_map/ppermute | solution.py:32
  205.0 18.5 %collective-permute-start.44 = (bf16[384,384]{1,0:T(8,128)(2,1)S(1)}, bf16[384,384]{1,0:T(8,128)(2,1)S(1)}, u32[]{:S(2)}, u32[]{:S(2)}) collective-permute-start(bf16[384,384]{1,0:T(8,128)(2,1)S(1)} %shard_map.213), channel_id=1, source_target_pairs={{0,8},{4,12},{8,0},{12,4},{16,24},{20,28},{24,16},{28,20},{1,9},{5... | collective-permute-start | bytes 884744 | tf_op jit(solution)/shard_map/ppermute | solution.py:27
  205.1 18.4 %collective-permute-start.48 = (bf16[384,384]{1,0:T(8,128)(2,1)S(1)}, bf16[384,384]{1,0:T(8,128)(2,1)S(1)}, u32[]{:S(2)}, u32[]{:S(2)}) collective-permute-start(bf16[384,384]{1,0:T(8,128)(2,1)S(1)} %shard_map.213), channel_id=1, source_target_pairs={{0,16},{4,20},{8,24},{12,28},{16,0},{20,4},{24,8},{28,12},{1,17},{... | collective-permute-start | bytes 884744 | tf_op jit(solution)/shard_map/ppermute | solution.py:27
  205.4 18.1 %collective-permute-start.49 = (bf16[384,384]{1,0:T(8,128)(2,1)S(1)}, bf16[384,384]{1,0:T(8,128)(2,1)S(1)}, u32[]{:S(2)}, u32[]{:S(2)}) collective-permute-start(bf16[384,384]{1,0:T(8,128)(2,1)S(1)} %shard_map.213), channel_id=1, source_target_pairs={{0,24},{4,28},{8,16},{12,20},{16,8},{20,12},{24,0},{28,4},{1,25},{... | collective-permute-start | bytes 884744 | tf_op jit(solution)/shard_map/ppermute | solution.py:27
  (32 other events, 244.4 us)

commit v4 on v3

--- a/solution.py
+++ b/solution.py
@@ -403,7 +403,7 @@
 
 
 def attend_kernel(tokens, vectors, partial, fq, w_out, *refs):
-    priors, (attended, inverse, resid, second, second_t) = refs[:-5], refs[-5:]
+    priors, (attended, attended_t, inverse, resid, second, second_t) = refs[:-6], refs[-6:]
     seqs = priors[0].shape[0]
     length = tokens.shape[0] // seqs
 
@@ -429,12 +429,13 @@
     normal, _ = normalize(resid[...])
     second[...] = low(normal * vectors[2:3, :] + vectors[3:4, :])
     second_t[...] = second[...].T
-
-
-def mlp_kernel(second, second_other, cotangent, cotangent_other, resid, attended, *refs):
+    attended_t[...] = attended[...].T
+
+
+def mlp_kernel(second, second_other, cotangent, cotangent_other, resid, *refs):
     pieces = refs[:4]
-    out_sum, out_send, back_sum, back_send, hiddens, d_pres, second_other_t, attended_t = refs[4:12]
-    up, down, ready = refs[12:]
+    out_sum, out_send, back_sum, back_send, hiddens, d_pres = refs[4:10]
+    up, down, ready = refs[10:]
     count = second.shape[0]
     parts = grads_layout(second.shape[1], pieces[0].shape[0])
 
@@ -454,8 +455,6 @@
     for k in range(4):
         for copy in copies(k, pieces[k]):
             copy.start()
-    second_other_t[...] = second_other[...].T
-    attended_t[...] = attended[...].T
 
     def piece(k, carry):
         for copy in copies(k, pieces[0]):
@@ -509,8 +508,9 @@
         outs[4][...] = made[half:]
 
 
-def mlp_grads_kernel(second_t, second_other_t, cotangent, cotangent_other, hiddens, d_pres, *refs):
-    outs, made = refs[:5], refs[5]
+def mlp_grads_kernel(second_t, second_other, cotangent, cotangent_other, hiddens, d_pres, *refs):
+    outs, made, second_other_t = refs[:5], refs[5], refs[6]
+    second_other_t[...] = second_other[...].T
     count = cotangent.shape[0]
     own, other = slice(0, count), slice(count, 2 * count)
 
@@ -994,11 +994,12 @@
     priors = scan_rest(prior, running, 1)
     mlp_halves, partial = lax.optimization_barrier((halves_of(mlp_x, mlp_y), partial))
     mlp_pieces = [mlp_full, mlp_x, mlp_y, diagonal_of(mlp_halves)]
-    attended, inverse, resid, second, second_t = call(
+    attended, attended_t, inverse, resid, second, second_t = call(
         attend_kernel,
         5,
         (
             whole((count, D)),
+            whole((D, count)),
             whole((count, D), wide_type),
             whole((count, D), wide_type),
             whole((count, D)),
@@ -1014,8 +1015,6 @@
         back_send,
         hiddens,
         d_pres,
-        second_other_t,
-        attended_t,
     ) = call(
         mlp_kernel,
         20,
@@ -1026,17 +1025,15 @@
             whole((count, D)),
             whole((2 * count, 4 * CHUNK)),
             whole((2 * count, 4 * CHUNK)),
-            whole((D, count)),
-            whole((D, count)),
         ),
-        [pl.BlockSpec(memory_space=pltpu.VMEM)] * 6 + anywhere[:4],
+        [pl.BlockSpec(memory_space=pltpu.VMEM)] * 5 + anywhere[:4],
         [
             pltpu.VMEM((D, 4 * CHUNK), low_type),
             pltpu.VMEM((4 * CHUNK, D), low_type),
             pltpu.SemaphoreType.DMA((4, 3 * shard_count)),
         ],
         limit=18,
-    )(second, second_other, flat_cotangent, cotangent_other, resid, attended, *mlp_pieces)
+    )(second, second_other, flat_cotangent, cotangent_other, resid, *mlp_pieces)
     back_other = flip(back_send, 1)
     out_other = flip(out_send, 1)
     d_resid, d_resid_low, d_vectors_two, d_num, d_den, query_state = call(
@@ -1061,8 +1058,8 @@
         whole((size, CHUNK)) for size in (rows, rows, rows, rows // 2, rows // 2)
     )
     mlp_grads = call(
-        mlp_grads_kernel, 7, piece(2 * D), scratch=[pltpu.VMEM((2 * D, CHUNK), low_type)]
-    )(second_t, second_other_t, flat_cotangent, cotangent_other, hiddens, d_pres)
+        mlp_grads_kernel, 7, piece(2 * D), scratch=[pltpu.VMEM((2 * D, CHUNK), low_type), pltpu.VMEM((D, count), low_type)]
+    )(second_t, second_other, flat_cotangent, cotangent_other, hiddens, d_pres)
     mlp_to_x, mlp_to_y = flip(mlp_grads[3], 4), flip(mlp_grads[4], 2)
     running, fk_t = lax.optimization_barrier((running, fk_t))
     laters = scan_rest(later, running, -1)

time: 241 us -> 241 us (level)
  no operation moved by 1% of the time
where the time goes in v4:
time: 241 us; the launch traced here: 240 us
  waiting for transfers between devices  89.4 us (37%)
  Pallas kernels  85.9 us (36%)
  starting transfers between devices  54.2 us (22%)
  local copies, waits for them, and re-layouts  6.18 us (3%)
  other arithmetic  3.05 us (1%)
    ppermute x12, waiting for transfers between devices, spin(): lax.ppermute(value, 'shard', [(i, (i + step) % count) for i in range(coun...  39.7 us
    ppermute x36, waiting for transfers between devices, flip(): return lax.ppermute(value, 'rep', [(i, i ^ bit) for i in range(count)])  30.6 us
    ppermute x36, starting transfers between devices, flip(): return lax.ppermute(value, 'rep', [(i, i ^ bit) for i in range(count)])  29.9 us
    ppermute x4, waiting for transfers between devices, slide(): return lax.ppermute(value, 'shard', pairs)  19 us
    ppermute x12, starting transfers between devices, spin(): lax.ppermute(value, 'shard', [(i, (i + step) % count) for i in range(coun...  16.3 us
    pallas_call x1, Pallas kernels, shards(): call(mlp_kernel, 20, (whole((count, D), wide_type), whole((count, D)), wh...  14.6 us
    pallas_call x1, Pallas kernels, shards(): call(lambda *refs: local_keys_kernel(*refs, seqs=seqs), 5, (whole((HEADS...  8.59 us
    ppermute x4, starting transfers between devices, slide(): return lax.ppermute(value, 'shard', pairs)  8.04 us
  transfers between devices with their start and end apart: 52, of which 23 were waited for; matrix products, arithmetic and copies ran while one was open for 3% of the time, Pallas kernels for 28%

profile of v4, /device:TPU:9, one launch (start us, length us, event | category | flops | bytes accessed | tf_op | source)
XLA Modules:
  0.0 239.9 jit_solution(14160988046030276783)
XLA Ops:
  12.6 8.7 %collective-permute-done.1.refs_2_ = bf16[264,384]{1,0:T(8,128)(2,1)S(1)} collective-permute-done((bf16[264,384]{1,0:T(8,128)(2,1)S(1)}, bf16[264,384]{1,0:T(8,128)(2,1)S(1)}, u32[]{:S(2)}, u32[]{:S(2)}) %collective-permute-start.1) | collective-permute-done | bytes 202784 | tf_op jit(solution)/shard_map/ppermute | solution.py:32
  29.0 10.3 %collective-permute-done.3.refs_2_ = bf16[768,384]{1,0:T(8,128)(2,1)S(1)} collective-permute-done((bf16[768,384]{1,0:T(8,128)(2,1)S(1)}, bf16[768,384]{1,0:T(8,128)(2,1)S(1)}, u32[]{:S(2)}, u32[]{:S(2)}) %collective-permute-start.3) | collective-permute-done | bytes 589856 | tf_op jit(solution)/shard_map/ppermute | solution.py:27
  44.0 5.4 %collective-permute-done.7 = bf16[384,384]{1,0:T(8,128)(2,1)S(1)} collective-permute-done((bf16[384,384]{1,0:T(8,128)(2,1)S(1)}, bf16[384,384]{1,0:T(8,128)(2,1)S(1)}, u32[]{:S(2)}, u32[]{:S(2)}) %collective-permute-start.7) | collective-permute-done | bytes 294944 | tf_op jit(solution)/shard_map/ppermute | solution.py:27
  54.4 6.5 %shard_map.197 = (bf16[512,768]{1,0:T(8,128)(2,1)S(1)}, bf16[512,1536]{1,0:T(8,128)(2,1)S(1)}, bf16[512,1536]{1,0:T(8,128)(2,1)S(1)}, bf16[1536,512]{1,0:T(8,128...) custom-call(s32[1]{0:T(128)} %bitcast.12.place, bf16[512,768]{1,0:T(8,128)(2,1)S(1)} %bitcast.39, ...), custom_call_target="tpu_custom_call" | custom-call | flops 16000000000 | bytes 48000000 | tf_op jit(solution)/shard_map/pallas_call | solution.py:964
  62.9 6.8 %shard_map.198 = (bf16[768,512]{1,0:T(8,128)(2,1)S(1)}, bf16[512,768]{1,0:T(8,128)(2,1)S(1)}, bf16[512,1536]{1,0:T(8,128)(2,1)S(1)}, bf16[1536,512]{1,0:T(8,128)...) custom-call(s32[1]{0:T(128)} %bitcast.12.place, ...), custom_call_target="tpu_custom_call" | custom-call | flops 17999998976 | bytes 54000000 | tf_op jit(solution)/shard_map/pallas_call | solution.py:979
  69.7 4.8 %collective-permute-done.16.refs_0_ = bf16[2,800,128]{2,1,0:T(8,128)(2,1)S(1)} collective-permute-done((bf16[2,800,128]{2,1,0:T(8,128)(2,1)S(1)}, bf16[2,800,128]{2,1,0:T(8,128)(2,1)S(1)}, u32[]{:S(2)}, u32[]{:S(2)}) %collective-permute-start.16) | collective-permute-done | bytes 409632 | tf_op jit(solution)/shard_map/ppermute | solution.py:38
  82.2 12.0 %collective-permute-done.17.refs_1_ = bf16[2,800,128]{2,1,0:T(8,128)(2,1)S(1)} collective-permute-done((bf16[2,800,128]{2,1,0:T(8,128)(2,1)S(1)}, bf16[2,800,128]{2,1,0:T(8,128)(2,1)S(1)}, u32[]{:S(2)}, u32[]{:S(2)}) %collective-permute-start.17) | collective-permute-done | bytes 409632 | tf_op jit(solution)/shard_map/ppermute | solution.py:38
  94.2 5.1 %shard_map.199 = (bf16[512,768]{1,0:T(8,128)(2,1)S(1)}, bf16[768,512]{1,0:T(8,128)(2,1)S(1)}, f32[512,768]{1,0:T(8,128)S(1)}, f32[512,768]{1,0:T(8,128)S(1)}, bf...) custom-call(bf16[512,768]{1,0:T(8,128)(2,1)S(1)} %bitcast.40, f32[4,768]{1,0:T(4,128)S(1)} %get-tuple-element.165.vectors, ...), custom_call_target="tpu_custom_call" | custom-call | flops 10000000000 | bytes 30000000 | tf_op jit(solution)/shard_map/pallas_call | solution.py:997
  101.8 14.6 %shard_map.200 = (f32[512,768]{1,0:T(8,128)S(1)}, bf16[512,768]{1,0:T(8,128)(2,1)S(1)}, f32[512,768]{1,0:T(8,128)S(1)}, bf16[512,768]{1,0:T(8,128)(2,1)S(1)}, bf...) custom-call(bf16[512,768]{1,0:T(8,128)(2,1)S(1)} %get-tuple-element.181.second, ...), custom_call_target="tpu_custom_call" | custom-call | flops 40000000000 | bytes 120000000 | tf_op jit(solution)/shard_map/pallas_call | solution.py:1018
  118.7 3.9 %shard_map.201 = (f32[512,768]{1,0:T(8,128)S(1)}, bf16[512,768]{1,0:T(8,128)(2,1)S(1)}, f32[2,768]{1,0:T(2,128)S(1)}, bf16[512,768]{1,0:T(8,128)(2,1)S(1)}, bf16...) custom-call(f32[512,768]{1,0:T(8,128)S(1)} %get-tuple-element.185.back_sum, ...), custom_call_target="tpu_custom_call" | custom-call | flops 10000000000 | bytes 30000000 | tf_op jit(solution)/shard_map/pallas_call | solution.py:1039
  124.6 7.2 %shard_map.204 = (bf16[1536,384]{1,0:T(8,128)(2,1)S(1)}, bf16[1536,384]{1,0:T(8,128)(2,1)S(1)}, bf16[1536,384]{1,0:T(8,128)(2,1)S(1)}, bf16[768,384]{1,0:T(8,128)(2,1)S(1)}, bf16[768,384]{1,0:T(8,128)(2,1)S(1)}) custom-call(bf16[768,512]{1,0:T(8,128)(2,1)S(1)} %get-tuple-element.199.second_t, bf16[512,768]{1,0:T(8,128)(2,1)S(1)} %collective-permute-done.18.second_other, ...), custom_call_target="tpu_custom_call" | custom-call | flops 14000000000 | bytes 42000000 | tf_op jit(solution)/shard_map/pallas_call | solution.py:1060
  136.9 7.2 %shard_map.202 = (bf16[512,768]{1,0:T(8,128)(2,1)S(1)}, f32[768,128]{1,0:T(8,128)S(1)}, bf16[768,512]{1,0:T(8,128)(2,1)}) custom-call(bf16[512,768]{1,0:T(8,128)(2,1)S(1)} %get-tuple-element.171.queries, bf16[512,1536]{1,0:T(8,128)(2,1)S(1)} %get-tuple-element.169.keyed.refs_0_, bf16[6,256,256]{2,1,0:T(8,128)(2,1)S(1)} %get-tuple-element.166.maps, ...), custom_call_target="tpu_custom_call" | custom-call | flops 12000000000 | bytes 36000000 | tf_op jit(solution)/shard_map/pallas_call | solution.py:1066
  148.2 8.6 %shard_map.206 = (f32[1536,512]{1,0:T(8,128)S(1)}, f32[512,768]{1,0:T(8,128)S(1)}) custom-call(bf16[512,1536]{1,0:T(8,128)(2,1)S(1)} %get-tuple-element.169.keyed.refs_0_, bf16[1536,512]{1,0:T(8,128)(2,1)S(1)} %get-tuple-element.172.fq_t.refs_1_, bf16[512,1536]{1,0:T(8,128)(2,1)S(1)} %get-tuple-element.215.refs_2_.fk, ...), custom_call_target="tpu_custom_call" | custom-call | flops 10000000000 | bytes 30000000 | tf_op jit(solution)/shard_map/pallas_call | solution.py:1077
  156.8 6.1 %shard_map.207 = (bf16[512,1536]{1,0:T(8,128)(2,1)S(1)}, f32[768,128]{1,0:T(8,128)S(1)}, bf16[4,512,384]{2,1,0:T(8,128)(2,1)S(1)}, bf16[768,512]{1,0:T(8,128)(2,1)}) custom-call(s32[1]{0:T(128)} %bitcast.12.place, bf16[512,1536]{1,0:T(8,128)(2,1)S(1)} %get-tuple-element.169.keyed.refs_0_, bf16[512,1536]{1,0:T(8,128)(2,1)S(1)} %get-tuple-element.215.refs_2_.fk, ...), custom_call_target="tpu_custom_call" | custom-call | flops 14000000000 | bytes 42000000 | tf_op jit(solution)/shard_map/pallas_call | solution.py:1085
  165.0 4.7 %shard_map.208 = (bf16[512,768]{1,0:T(8,128)(2,1)}, bf16[512,768]{1,0:T(8,128)(2,1)}, bf16[4,240,128]{2,1,0:T(8,128)(2,1)S(1)}) custom-call(bf16[512,768]{1,0:T(8,128)(2,1)S(1)} %bitcast.41, f32[4,768]{1,0:T(4,128)S(1)} %get-tuple-element.165.vectors, f32[512,768]{1,0:T(8,128)S(1)} %shard_map.203.early, bf16[512,1536]{1,0:T(8,128)(2,1)S(1)} %get-tuple-element.221.d_keyed, ...), custom_call_target="tpu_custom_call" | custom-call | flops 14000000000 | bytes 42000000 | tf_op jit(solution)/shard_map/pallas_call | solution.py:1097
  169.7 3.2 %collective-permute-done.32.refs_1_ = bf16[1536,384]{1,0:T(8,128)(2,1)S(1)} collective-permute-done((bf16[1536,384]{1,0:T(8,128)(2,1)S(1)}, bf16[1536,384]{1,0:T(8,128)(2,1)S(1)}, u32[]{:S(2)}, u32[]{:S(2)}) %collective-permute-start.32) | collective-permute-done | bytes 1179680 | tf_op jit(solution)/shard_map/ppermute | solution.py:27
  174.6 5.0 %shard_map.210 = (bf16[832,384]{1,0:T(8,128)(2,1)S(1)}, bf16[832,384]{1,0:T(8,128)(2,1)S(1)}, bf16[832,384]{1,0:T(8,128)(2,1)S(1)}, bf16[416,384]{1,0:T(8,128)(2,1)S(1)}, bf16[416,384]{1,0:T(8,128)(2,1)S(1)}) custom-call(s32[1]{0:T(128)} %bitcast.12.place, bf16[512,768]{1,0:T(8,128)(2,1)S(1)} %get-tuple-element.193.d_queries, ...), custom_call_target="tpu_custom_call" | custom-call | flops 14000000000 | bytes 42000000 | tf_op jit(solution)/shard_map/pallas_call | solution.py:1121
  183.9 4.0 %collective-permute-done.37.refs_2_ = bf16[384,384]{1,0:T(8,128)(2,1)S(1)} collective-permute-done((bf16[384,384]{1,0:T(8,128)(2,1)S(1)}, bf16[384,384]{1,0:T(8,128)(2,1)S(1)}, u32[]{:S(2)}, u32[]{:S(2)}) %collective-permute-start.37) | collective-permute-done | bytes 294944 | tf_op jit(solution)/shard_map/ppermute | solution.py:32
  189.3 3.1 %collective-permute-start.40 = (bf16[384,384]{1,0:T(8,128)(2,1)S(1)}, bf16[384,384]{1,0:T(8,128)(2,1)S(1)}, u32[]{:S(2)}, u32[]{:S(2)}) collective-permute-start(bf16[384,384]{1,0:T(8,128)(2,1)S(1)} %get-tuple-element.257), channel_id=1, source_target_pairs={{0,2},{1,3},{2,0},{3,1},{4,6},{5,7},{6,4},{7,5},{8,10},{9,11},{10,... | collective-permute-start | bytes 884744 | tf_op jit(solution)/shard_map/ppermute | solution.py:32
  192.5 11.8 %collective-permute-done.40.refs_1_ = bf16[384,384]{1,0:T(8,128)(2,1)S(1)} collective-permute-done((bf16[384,384]{1,0:T(8,128)(2,1)S(1)}, bf16[384,384]{1,0:T(8,128)(2,1)S(1)}, u32[]{:S(2)}, u32[]{:S(2)}) %collective-permute-start.40) | collective-permute-done | bytes 294944 | tf_op jit(solution)/shard_map/ppermute | solution.py:32
  207.5 3.1 %collective-permute-start.42 = (bf16[208,384]{1,0:T(8,128)(2,1)S(1)}, bf16[208,384]{1,0:T(8,128)(2,1)S(1)}, u32[]{:S(2)}, u32[]{:S(2)}) collective-permute-start(bf16[208,384]{1,0:T(8,128)(2,1)S(1)} %get-tuple-element.263), channel_id=1, source_target_pairs={{0,2},{1,3},{2,0},{3,1},{4,6},{5,7},{6,4},{7,5},{8,10},{9,11},{10,... | collective-permute-start | bytes 479240 | tf_op jit(solution)/shard_map/ppermute | solution.py:32
  212.1 4.5 %collective-permute-done.42.refs_1_ = bf16[208,384]{1,0:T(8,128)(2,1)S(1)} collective-permute-done((bf16[208,384]{1,0:T(8,128)(2,1)S(1)}, bf16[208,384]{1,0:T(8,128)(2,1)S(1)}, u32[]{:S(2)}, u32[]{:S(2)}) %collective-permute-start.42) | collective-permute-done | bytes 159776 | tf_op jit(solution)/shard_map/ppermute | solution.py:32
  216.6 6.7 %collective-permute-done.43.refs_2_ = bf16[208,384]{1,0:T(8,128)(2,1)S(1)} collective-permute-done((bf16[208,384]{1,0:T(8,128)(2,1)S(1)}, bf16[208,384]{1,0:T(8,128)(2,1)S(1)}, u32[]{:S(2)}, u32[]{:S(2)}) %collective-permute-start.43) | collective-permute-done | bytes 159776 | tf_op jit(solution)/shard_map/ppermute | solution.py:32
  230.9 3.2 %collective-permute-done.47 = bf16[208,384]{1,0:T(8,128)(2,1)S(1)} collective-permute-done((bf16[208,384]{1,0:T(8,128)(2,1)S(1)}, bf16[208,384]{1,0:T(8,128)(2,1)S(1)}, u32[]{:S(2)}, u32[]{:S(2)}) %collective-permute-start.47) | collective-permute-done | bytes 159776 | tf_op jit(solution)/shard_map/ppermute | solution.py:27
  (131 shorter events, 82.3 us)
Async XLA Ops:
  4.6 16.7 %collective-permute-start.1 = (bf16[264,384]{1,0:T(8,128)(2,1)S(1)}, bf16[264,384]{1,0:T(8,128)(2,1)S(1)}, u32[]{:S(2)}, u32[]{:S(2)}) collective-permute-start(bf16[264,384]{1,0:T(8,128)(2,1)S(1)} %maximum_maximum_fusion.refs_0_), channel_id=1, source_target_pairs={{0,2},{1,3},{2,0},{3,1},{4,6},{5,7},{6,4},{7,5},{8,10},{9,11},{10,... | collective-permute-start | bytes 608264 | tf_op jit(solution)/shard_map/ppermute | solution.py:32
  5.7 18.5 %collective-permute-start.2 = (bf16[264,384]{1,0:T(8,128)(2,1)S(1)}, bf16[264,384]{1,0:T(8,128)(2,1)S(1)}, u32[]{:S(2)}, u32[]{:S(2)}) collective-permute-start(bf16[264,384]{1,0:T(8,128)(2,1)S(1)} %maximum_maximum_fusion.refs_0_), channel_id=1, source_target_pairs={{0,3},{1,0},{2,1},{3,2},{4,7},{5,4},{6,5},{7,6},{8,11},{9,8},{10,9... | collective-permute-start | bytes 608264 | tf_op jit(solution)/shard_map/ppermute | solution.py:32
  24.8 14.5 %collective-permute-start.3 = (bf16[768,384]{1,0:T(8,128)(2,1)S(1)}, bf16[768,384]{1,0:T(8,128)(2,1)S(1)}, u32[]{:S(2)}, u32[]{:S(2)}) collective-permute-start(bf16[768,384]{1,0:T(8,128)(2,1)S(1)} %bitcast.42), channel_id=1, source_target_pairs={{0,8},{4,12},{8,0},{12,4},{16,24},{20,28},{24,16},{28,20},{1,9},{5... | collective-permute-start | bytes 1769480 | tf_op jit(solution)/shard_map/ppermute | solution.py:27
  26.0 14.1 %collective-permute-start.4 = (bf16[768,384]{1,0:T(8,128)(2,1)S(1)}, bf16[768,384]{1,0:T(8,128)(2,1)S(1)}, u32[]{:S(2)}, u32[]{:S(2)}) collective-permute-start(bf16[768,384]{1,0:T(8,128)(2,1)S(1)} %bitcast.43), channel_id=1, source_target_pairs={{0,16},{4,20},{8,24},{12,28},{16,0},{20,4},{24,8},{28,12},{1,17},{... | collective-permute-start | bytes 1769480 | tf_op jit(solution)/shard_map/ppermute | solution.py:27
  27.3 12.9 %collective-permute-start.5 = (bf16[384,384]{1,0:T(8,128)(2,1)S(1)}, bf16[384,384]{1,0:T(8,128)(2,1)S(1)}, u32[]{:S(2)}, u32[]{:S(2)}) collective-permute-start(bf16[384,384]{1,0:T(8,128)(2,1)S(1)} %pad_maximum_fusion.2), channel_id=1, source_target_pairs={{0,1},{1,2},{2,3},{3,0},{4,5},{5,6},{6,7},{7,4},{8,9},{9,10},{10,1... | collective-permute-start | bytes 884744 | tf_op jit(solution)/shard_map/ppermute | solution.py:32
  27.3 14.1 %collective-permute-start.6 = (bf16[384,384]{1,0:T(8,128)(2,1)S(1)}, bf16[384,384]{1,0:T(8,128)(2,1)S(1)}, u32[]{:S(2)}, u32[]{:S(2)}) collective-permute-start(bf16[384,384]{1,0:T(8,128)(2,1)S(1)} %pad_maximum_fusion.2), channel_id=1, source_target_pairs={{0,3},{1,0},{2,1},{3,2},{4,7},{5,4},{6,5},{7,6},{8,11},{9,8},{10,9... | collective-permute-start | bytes 884744 | tf_op jit(solution)/shard_map/ppermute | solution.py:32
  51.9 27.5 %collective-permute-start.14 = (bf16[1536,384]{1,0:T(8,128)(2,1)S(1)}, bf16[1536,384]{1,0:T(8,128)(2,1)S(1)}, u32[]{:S(2)}, u32[]{:S(2)}) collective-permute-start(bf16[1536,384]{1,0:T(8,128)(2,1)S(1)} %bitcast.32), channel_id=1, source_target_pairs={{0,8},{4,12},{8,0},{12,4},{16,24},{20,28},{24,16},{28,20},{1,9},{5... | collective-permute-start | bytes 3538952 | tf_op jit(solution)/shard_map/ppermute | solution.py:27
  53.2 27.3 %collective-permute-start.15 = (bf16[1536,384]{1,0:T(8,128)(2,1)S(1)}, bf16[1536,384]{1,0:T(8,128)(2,1)S(1)}, u32[]{:S(2)}, u32[]{:S(2)}) collective-permute-start(bf16[1536,384]{1,0:T(8,128)(2,1)S(1)} %bitcast.33), channel_id=1, source_target_pairs={{0,16},{4,20},{8,24},{12,28},{16,0},{20,4},{24,8},{28,12},{1,17},{... | collective-permute-start | bytes 3538952 | tf_op jit(solution)/shard_map/ppermute | solution.py:27
  60.9 13.6 %collective-permute-start.16 = (bf16[2,800,128]{2,1,0:T(8,128)(2,1)S(1)}, bf16[2,800,128]{2,1,0:T(8,128)(2,1)S(1)}, u32[]{:S(2)}, u32[]{:S(2)}) collective-permute-start(bf16[2,800,128]{2,1,0:T(8,128)(2,1)S(1)} %get-tuple-element.174), channel_id=1, source_target_pairs={{0,1},{1,2},{2,3},{4,5},{5,6},{6,7},{8,9},{9,10},{10,11},{12,13},{... | collective-permute-start | bytes 1228808 | tf_op jit(solution)/shard_map/ppermute | solution.py:38
  74.6 19.6 %collective-permute-start.17 = (bf16[2,800,128]{2,1,0:T(8,128)(2,1)S(1)}, bf16[2,800,128]{2,1,0:T(8,128)(2,1)S(1)}, u32[]{:S(2)}, u32[]{:S(2)}) collective-permute-start(bf16[2,800,128]{2,1,0:T(8,128)(2,1)S(1)} %add_convert_fusion.1), channel_id=1, source_target_pairs={{0,2},{1,3},{4,6},{5,7},{8,10},{9,11},{12,14},{13,15},{16,18},{17,... | collective-permute-start | bytes 1228808 | tf_op jit(solution)/shard_map/ppermute | solution.py:38
  77.3 22.7 %collective-permute-start.19 = (bf16[512,768]{1,0:T(8,128)(2,1)S(1)}, bf16[512,768]{1,0:T(8,128)(2,1)S(1)}, u32[]{:S(2)}, u32[]{:S(2)}) collective-permute-start(bf16[512,768]{1,0:T(8,128)(2,1)S(1)} %bitcast.35), channel_id=1, source_target_pairs={{0,4},{4,0},{8,12},{12,8},{16,20},{20,16},{24,28},{28,24},{1,5},{5... | collective-permute-start | bytes 2359304 | tf_op jit(solution)/shard_map/ppermute | solution.py:27
  80.5 19.3 %collective-permute-start.20 = (bf16[768,384]{1,0:T(8,128)(2,1)S(1)}, bf16[768,384]{1,0:T(8,128)(2,1)S(1)}, u32[]{:S(2)}, u32[]{:S(2)}) collective-permute-start(bf16[768,384]{1,0:T(8,128)(2,1)S(1)} %slice.51), channel_id=1, source_target_pairs={{0,16},{4,20},{8,24},{12,28},{16,0},{20,4},{24,8},{28,12},{1,17},{... | collective-permute-start | bytes 1769480 | tf_op jit(solution)/shard_map/ppermute | solution.py:27
  81.8 18.0 %collective-permute-start.21 = (bf16[768,384]{1,0:T(8,128)(2,1)S(1)}, bf16[768,384]{1,0:T(8,128)(2,1)S(1)}, u32[]{:S(2)}, u32[]{:S(2)}) collective-permute-start(bf16[768,384]{1,0:T(8,128)(2,1)S(1)} %slice.52), channel_id=1, source_target_pairs={{0,8},{4,12},{8,0},{12,4},{16,24},{20,28},{24,16},{28,20},{1,9},{5... | collective-permute-start | bytes 1769480 | tf_op jit(solution)/shard_map/ppermute | solution.py:27
  131.8 14.6 %collective-permute-start.27 = (bf16[768,384]{1,0:T(8,128)(2,1)S(1)}, bf16[768,384]{1,0:T(8,128)(2,1)S(1)}, u32[]{:S(2)}, u32[]{:S(2)}) collective-permute-start(bf16[768,384]{1,0:T(8,128)(2,1)S(1)} %get-tuple-element.204), channel_id=1, source_target_pairs={{0,16},{4,20},{8,24},{12,28},{16,0},{20,4},{24,8},{28,12},{1,17},{... | collective-permute-start | bytes 1769480 | tf_op jit(solution)/shard_map/ppermute | solution.py:27
  132.1 14.3 %collective-permute-start.28 = (bf16[768,384]{1,0:T(8,128)(2,1)S(1)}, bf16[768,384]{1,0:T(8,128)(2,1)S(1)}, u32[]{:S(2)}, u32[]{:S(2)}) collective-permute-start(bf16[768,384]{1,0:T(8,128)(2,1)S(1)} %get-tuple-element.205), channel_id=1, source_target_pairs={{0,8},{4,12},{8,0},{12,4},{16,24},{20,28},{24,16},{28,20},{1,9},{5... | collective-permute-start | bytes 1769480 | tf_op jit(solution)/shard_map/ppermute | solution.py:27
  135.4 21.4 %collective-permute-start.29 = (bf16[2,800,128]{2,1,0:T(8,128)(2,1)S(1)}, bf16[2,800,128]{2,1,0:T(8,128)(2,1)S(1)}, u32[]{:S(2)}, u32[]{:S(2)}) collective-permute-start(bf16[2,800,128]{2,1,0:T(8,128)(2,1)S(1)} %add_convert_fusion), channel_id=1, source_target_pairs={{2,0},{3,1},{6,4},{7,5},{10,8},{11,9},{14,12},{15,13},{18,16},{19,... | collective-permute-start | bytes 1228808 | tf_op jit(solution)/shard_map/ppermute | solution.py:38
  146.8 26.1 %collective-permute-start.32 = (bf16[1536,384]{1,0:T(8,128)(2,1)S(1)}, bf16[1536,384]{1,0:T(8,128)(2,1)S(1)}, u32[]{:S(2)}, u32[]{:S(2)}) collective-permute-start(bf16[1536,384]{1,0:T(8,128)(2,1)S(1)} %get-tuple-element.233), channel_id=1, source_target_pairs={{0,8},{4,12},{8,0},{12,4},{16,24},{20,28},{24,16},{28,20},{1,9},{5... | collective-permute-start | bytes 3538952 | tf_op jit(solution)/shard_map/ppermute | solution.py:27
  147.6 25.7 %collective-permute-start.33 = (bf16[1536,384]{1,0:T(8,128)(2,1)S(1)}, bf16[1536,384]{1,0:T(8,128)(2,1)S(1)}, u32[]{:S(2)}, u32[]{:S(2)}) collective-permute-start(bf16[1536,384]{1,0:T(8,128)(2,1)S(1)} %get-tuple-element.234), channel_id=1, source_target_pairs={{0,16},{4,20},{8,24},{12,28},{16,0},{20,4},{24,8},{28,12},{1,17},{... | collective-permute-start | bytes 3538952 | tf_op jit(solution)/shard_map/ppermute | solution.py:27
  188.1 16.2 %collective-permute-start.38 = (bf16[832,384]{1,0:T(8,128)(2,1)S(1)}, bf16[832,384]{1,0:T(8,128)(2,1)S(1)}, u32[]{:S(2)}, u32[]{:S(2)}) collective-permute-start(bf16[832,384]{1,0:T(8,128)(2,1)S(1)} %get-tuple-element.254), channel_id=1, source_target_pairs={{0,8},{4,12},{8,0},{12,4},{16,24},{20,28},{24,16},{28,20},{1,9},{5... | collective-permute-start | bytes 1916936 | tf_op jit(solution)/shard_map/ppermute | solution.py:27
  188.5 15.8 %collective-permute-start.39 = (bf16[832,384]{1,0:T(8,128)(2,1)S(1)}, bf16[832,384]{1,0:T(8,128)(2,1)S(1)}, u32[]{:S(2)}, u32[]{:S(2)}) collective-permute-start(bf16[832,384]{1,0:T(8,128)(2,1)S(1)} %get-tuple-element.255), channel_id=1, source_target_pairs={{0,16},{4,20},{8,24},{12,28},{16,0},{20,4},{24,8},{28,12},{1,17},{... | collective-permute-start | bytes 1916936 | tf_op jit(solution)/shard_map/ppermute | solution.py:27
  189.3 15.0 %collective-permute-start.40 = (bf16[384,384]{1,0:T(8,128)(2,1)S(1)}, bf16[384,384]{1,0:T(8,128)(2,1)S(1)}, u32[]{:S(2)}, u32[]{:S(2)}) collective-permute-start(bf16[384,384]{1,0:T(8,128)(2,1)S(1)} %get-tuple-element.257), channel_id=1, source_target_pairs={{0,2},{1,3},{2,0},{3,1},{4,6},{5,7},{6,4},{7,5},{8,10},{9,11},{10,... | collective-permute-start | bytes 884744 | tf_op jit(solution)/shard_map/ppermute | solution.py:32
  204.8 18.5 %collective-permute-start.44 = (bf16[384,384]{1,0:T(8,128)(2,1)S(1)}, bf16[384,384]{1,0:T(8,128)(2,1)S(1)}, u32[]{:S(2)}, u32[]{:S(2)}) collective-permute-start(bf16[384,384]{1,0:T(8,128)(2,1)S(1)} %shard_map.213), channel_id=1, source_target_pairs={{0,8},{4,12},{8,0},{12,4},{16,24},{20,28},{24,16},{28,20},{1,9},{5... | collective-permute-start | bytes 884744 | tf_op jit(solution)/shard_map/ppermute | solution.py:27
  204.9 18.4 %collective-permute-start.48 = (bf16[384,384]{1,0:T(8,128)(2,1)S(1)}, bf16[384,384]{1,0:T(8,128)(2,1)S(1)}, u32[]{:S(2)}, u32[]{:S(2)}) collective-permute-start(bf16[384,384]{1,0:T(8,128)(2,1)S(1)} %shard_map.213), channel_id=1, source_target_pairs={{0,16},{4,20},{8,24},{12,28},{16,0},{20,4},{24,8},{28,12},{1,17},{... | collective-permute-start | bytes 884744 | tf_op jit(solution)/shard_map/ppermute | solution.py:27
  205.2 18.1 %collective-permute-start.49 = (bf16[384,384]{1,0:T(8,128)(2,1)S(1)}, bf16[384,384]{1,0:T(8,128)(2,1)S(1)}, u32[]{:S(2)}, u32[]{:S(2)}) collective-permute-start(bf16[384,384]{1,0:T(8,128)(2,1)S(1)} %shard_map.213), channel_id=1, source_target_pairs={{0,24},{4,28},{8,16},{12,20},{16,8},{20,12},{24,0},{28,4},{1,25},{... | collective-permute-start | bytes 884744 | tf_op jit(solution)/shard_map/ppermute | solution.py:27
  (30 other events, 221.3 us)

commit v5 on v3

--- a/solution.py
+++ b/solution.py
@@ -859,7 +859,7 @@
     ]
 
 
-def call(kernel, weight, out_shape, in_specs=None, scratch=(), limit=8, **rest):
+def call(kernel, weight, out_shape, in_specs=None, scratch=(), limit=12, **rest):
     if in_specs is not None:
         rest["in_specs"] = in_specs
     return pl.pallas_call(

time: 241 us -> 241 us (level)
  no operation moved by 1% of the time
where the time goes in v5:
time: 241 us; the launch traced here: 240 us
  waiting for transfers between devices  89.3 us (37%)
  Pallas kernels  86 us (36%)
  starting transfers between devices  54.2 us (22%)
  local copies, waits for them, and re-layouts  6.22 us (3%)
  other arithmetic  3.05 us (1%)
    ppermute x12, waiting for transfers between devices, spin(): lax.ppermute(value, 'shard', [(i, (i + step) % count) for i in range(coun...  39.8 us
    ppermute x36, waiting for transfers between devices, flip(): return lax.ppermute(value, 'rep', [(i, i ^ bit) for i in range(count)])  30.3 us
    ppermute x36, starting transfers between devices, flip(): return lax.ppermute(value, 'rep', [(i, i ^ bit) for i in range(count)])  29.7 us
    ppermute x4, waiting for transfers between devices, slide(): return lax.ppermute(value, 'shard', pairs)  19.2 us
    ppermute x12, starting transfers between devices, spin(): lax.ppermute(value, 'shard', [(i, (i + step) % count) for i in range(coun...  16.5 us
    pallas_call x1, Pallas kernels, shards(): call(mlp_kernel, 20, (whole((count, D), wide_type), whole((count, D)), wh...  15.1 us
    pallas_call x1, Pallas kernels, shards(): call(lambda *refs: local_keys_kernel(*refs, seqs=seqs), 5, (whole((HEADS...  8.59 us
    ppermute x4, starting transfers between devices, slide(): return lax.ppermute(value, 'shard', pairs)  8.02 us
  transfers between devices with their start and end apart: 52, of which 23 were waited for; matrix products, arithmetic and copies ran while one was open for 3% of the time, Pallas kernels for 28%

profile of v5, /device:TPU:9, one launch (start us, length us, event | category | flops | bytes accessed | tf_op | source)
XLA Modules:
  0.0 240.1 jit_solution(1613739924154010666)
XLA Ops:
  12.6 8.7 %collective-permute-done.1.refs_2_ = bf16[264,384]{1,0:T(8,128)(2,1)S(1)} collective-permute-done((bf16[264,384]{1,0:T(8,128)(2,1)S(1)}, bf16[264,384]{1,0:T(8,128)(2,1)S(1)}, u32[]{:S(2)}, u32[]{:S(2)}) %collective-permute-start.1) | collective-permute-done | bytes 202784 | tf_op jit(solution)/shard_map/ppermute | solution.py:32
  29.0 10.3 %collective-permute-done.3.refs_2_ = bf16[768,384]{1,0:T(8,128)(2,1)S(1)} collective-permute-done((bf16[768,384]{1,0:T(8,128)(2,1)S(1)}, bf16[768,384]{1,0:T(8,128)(2,1)S(1)}, u32[]{:S(2)}, u32[]{:S(2)}) %collective-permute-start.3) | collective-permute-done | bytes 589856 | tf_op jit(solution)/shard_map/ppermute | solution.py:27
  44.0 5.4 %collective-permute-done.7 = bf16[384,384]{1,0:T(8,128)(2,1)S(1)} collective-permute-done((bf16[384,384]{1,0:T(8,128)(2,1)S(1)}, bf16[384,384]{1,0:T(8,128)(2,1)S(1)}, u32[]{:S(2)}, u32[]{:S(2)}) %collective-permute-start.7) | collective-permute-done | bytes 294944 | tf_op jit(solution)/shard_map/ppermute | solution.py:27
  54.4 6.5 %shard_map.197 = (bf16[512,768]{1,0:T(8,128)(2,1)S(1)}, bf16[512,1536]{1,0:T(8,128)(2,1)S(1)}, bf16[512,1536]{1,0:T(8,128)(2,1)S(1)}, bf16[1536,512]{1,0:T(8,128...) custom-call(s32[1]{0:T(128)} %bitcast.12.place, bf16[512,768]{1,0:T(8,128)(2,1)S(1)} %bitcast.39, ...), custom_call_target="tpu_custom_call" | custom-call | flops 16000000000 | bytes 48000000 | tf_op jit(solution)/shard_map/pallas_call | solution.py:964
  62.9 6.8 %shard_map.198 = (bf16[768,512]{1,0:T(8,128)(2,1)S(1)}, bf16[512,768]{1,0:T(8,128)(2,1)S(1)}, bf16[512,1536]{1,0:T(8,128)(2,1)S(1)}, bf16[1536,512]{1,0:T(8,128)...) custom-call(s32[1]{0:T(128)} %bitcast.12.place, ...), custom_call_target="tpu_custom_call" | custom-call | flops 17999998976 | bytes 54000000 | tf_op jit(solution)/shard_map/pallas_call | solution.py:979
  69.7 4.8 %collective-permute-done.16.refs_0_ = bf16[2,800,128]{2,1,0:T(8,128)(2,1)S(1)} collective-permute-done((bf16[2,800,128]{2,1,0:T(8,128)(2,1)S(1)}, bf16[2,800,128]{2,1,0:T(8,128)(2,1)S(1)}, u32[]{:S(2)}, u32[]{:S(2)}) %collective-permute-start.16) | collective-permute-done | bytes 409632 | tf_op jit(solution)/shard_map/ppermute | solution.py:38
  82.2 12.0 %collective-permute-done.17.refs_1_ = bf16[2,800,128]{2,1,0:T(8,128)(2,1)S(1)} collective-permute-done((bf16[2,800,128]{2,1,0:T(8,128)(2,1)S(1)}, bf16[2,800,128]{2,1,0:T(8,128)(2,1)S(1)}, u32[]{:S(2)}, u32[]{:S(2)}) %collective-permute-start.17) | collective-permute-done | bytes 409632 | tf_op jit(solution)/shard_map/ppermute | solution.py:38
  94.2 5.1 %shard_map.199 = (bf16[512,768]{1,0:T(8,128)(2,1)S(1)}, f32[512,768]{1,0:T(8,128)S(1)}, f32[512,768]{1,0:T(8,128)S(1)}, bf16[512,768]{1,0:T(8,128)(2,1)S(1)}, bf16[768,512]{1,0:T(8,128)(2,1)S(1)}) custom-call(bf16[512,768]{1,0:T(8,128)(2,1)S(1)} %bitcast.40, f32[4,768]{1,0:T(4,128)S(1)} %get-tuple-element.166.vectors, ...), custom_call_target="tpu_custom_call" | custom-call | flops 10000000000 | bytes 30000000 | tf_op jit(solution)/shard_map/pallas_call | solution.py:997
  101.7 15.1 %shard_map.200 = (f32[512,768]{1,0:T(8,128)S(1)}, bf16[512,768]{1,0:T(8,128)(2,1)S(1)}, f32[512,768]{1,0:T(8,128)S(1)}, bf16[512,768]{1,0:T(8,128)(2,1)S(1)}, bf...) custom-call(bf16[512,768]{1,0:T(8,128)(2,1)S(1)} %get-tuple-element., ...), custom_call_target="tpu_custom_call" | custom-call | flops 40000000000 | bytes 120000000 | tf_op jit(solution)/shard_map/pallas_call | solution.py:1019
  119.2 3.9 %shard_map.201 = (f32[512,768]{1,0:T(8,128)S(1)}, bf16[512,768]{1,0:T(8,128)(2,1)S(1)}, f32[2,768]{1,0:T(2,128)S(1)}, bf16[512,768]{1,0:T(8,128)(2,1)S(1)}, bf16...) custom-call(f32[512,768]{1,0:T(8,128)S(1)} %get-tuple-element.187.back_sum, ...), custom_call_target="tpu_custom_call" | custom-call | flops 10000000000 | bytes 30000000 | tf_op jit(solution)/shard_map/pallas_call | solution.py:1042
  125.1 6.9 %shard_map.204 = (bf16[1536,384]{1,0:T(8,128)(2,1)S(1)}, bf16[1536,384]{1,0:T(8,128)(2,1)S(1)}, bf16[1536,384]{1,0:T(8,128)(2,1)S(1)}, bf16[768,384]{1,0:T(8,128)(2,1)S(1)}, bf16[768,384]{1,0:T(8,128)(2,1)S(1)}) custom-call(bf16[768,512]{1,0:T(8,128)(2,1)S(1)} %get-tuple-element.200.second_t, bf16[768,512]{1,0:T(8,128)(2,1)S(1)} %get-tuple-element.201.second_other_t, ...), custom_call_target="tpu_custom_call" | custom-call | flops 14000000000 | bytes 42000000 | tf_op jit(solution)/shard_map/pallas_call | solution.py:1063
  137.4 7.2 %shard_map.202 = (bf16[512,768]{1,0:T(8,128)(2,1)S(1)}, f32[768,128]{1,0:T(8,128)S(1)}, bf16[768,512]{1,0:T(8,128)(2,1)}) custom-call(bf16[512,768]{1,0:T(8,128)(2,1)S(1)} %copy-done.7, bf16[512,1536]{1,0:T(8,128)(2,1)S(1)} %get-tuple-element.170.keyed.refs_0_, bf16[6,256,256]{2,1,0:T(8,128)(2,1)S(1)} %get-tuple-element.167.maps, ...), custom_call_target="tpu_custom_call" | custom-call | flops 12000000000 | bytes 36000000 | tf_op jit(solution)/shard_map/pallas_call | solution.py:1069
  148.5 8.6 %shard_map.206 = (f32[1536,512]{1,0:T(8,128)S(1)}, f32[512,768]{1,0:T(8,128)S(1)}) custom-call(bf16[512,1536]{1,0:T(8,128)(2,1)S(1)} %get-tuple-element.170.keyed.refs_0_, bf16[1536,512]{1,0:T(8,128)(2,1)S(1)} %get-tuple-element.173.fq_t.refs_1_, bf16[512,1536]{1,0:T(8,128)(2,1)S(1)} %get-tuple-element.217.refs_2_.fk, ...), custom_call_target="tpu_custom_call" | custom-call | flops 10000000000 | bytes 30000000 | tf_op jit(solution)/shard_map/pallas_call | solution.py:1080
  157.1 6.1 %shard_map.207 = (bf16[512,1536]{1,0:T(8,128)(2,1)S(1)}, f32[768,128]{1,0:T(8,128)S(1)}, bf16[4,512,384]{2,1,0:T(8,128)(2,1)S(1)}, bf16[768,512]{1,0:T(8,128)(2,1)}) custom-call(s32[1]{0:T(128)} %bitcast.12.place, bf16[512,1536]{1,0:T(8,128)(2,1)S(1)} %get-tuple-element.170.keyed.refs_0_, bf16[512,1536]{1,0:T(8,128)(2,1)S(1)} %get-tuple-element.217.refs_2_.fk, ...), custom_call_target="tpu_custom_call" | custom-call | flops 14000000000 | bytes 42000000 | tf_op jit(solution)/shard_map/pallas_call | solution.py:1088
  165.3 4.7 %shard_map.208 = (bf16[512,768]{1,0:T(8,128)(2,1)}, bf16[512,768]{1,0:T(8,128)(2,1)}, bf16[4,240,128]{2,1,0:T(8,128)(2,1)S(1)}) custom-call(bf16[512,768]{1,0:T(8,128)(2,1)S(1)} %bitcast.41, f32[4,768]{1,0:T(4,128)S(1)} %get-tuple-element.166.vectors, f32[512,768]{1,0:T(8,128)S(1)} %shard_map.203.early, bf16[512,1536]{1,0:T(8,128)(2,1)S(1)} %get-tuple-element.223.d_keyed, ...), custom_call_target="tpu_custom_call" | custom-call | flops 14000000000 | bytes 42000000 | tf_op jit(solution)/shard_map/pallas_call | solution.py:1100
  170.0 3.1 %collective-permute-done.32.refs_1_ = bf16[1536,384]{1,0:T(8,128)(2,1)S(1)} collective-permute-done((bf16[1536,384]{1,0:T(8,128)(2,1)S(1)}, bf16[1536,384]{1,0:T(8,128)(2,1)S(1)}, u32[]{:S(2)}, u32[]{:S(2)}) %collective-permute-start.32) | collective-permute-done | bytes 1179680 | tf_op jit(solution)/shard_map/ppermute | solution.py:27
  175.0 5.0 %shard_map.210 = (bf16[832,384]{1,0:T(8,128)(2,1)S(1)}, bf16[832,384]{1,0:T(8,128)(2,1)S(1)}, bf16[832,384]{1,0:T(8,128)(2,1)S(1)}, bf16[416,384]{1,0:T(8,128)(2,1)S(1)}, bf16[416,384]{1,0:T(8,128)(2,1)S(1)}) custom-call(s32[1]{0:T(128)} %bitcast.12.place, bf16[512,768]{1,0:T(8,128)(2,1)S(1)} %get-tuple-element.194.d_queries, ...), custom_call_target="tpu_custom_call" | custom-call | flops 14000000000 | bytes 42000000 | tf_op jit(solution)/shard_map/pallas_call | solution.py:1124
  184.1 4.0 %collective-permute-done.37.refs_2_ = bf16[384,384]{1,0:T(8,128)(2,1)S(1)} collective-permute-done((bf16[384,384]{1,0:T(8,128)(2,1)S(1)}, bf16[384,384]{1,0:T(8,128)(2,1)S(1)}, u32[]{:S(2)}, u32[]{:S(2)}) %collective-permute-start.37) | collective-permute-done | bytes 294944 | tf_op jit(solution)/shard_map/ppermute | solution.py:32
  189.5 3.1 %collective-permute-start.40 = (bf16[384,384]{1,0:T(8,128)(2,1)S(1)}, bf16[384,384]{1,0:T(8,128)(2,1)S(1)}, u32[]{:S(2)}, u32[]{:S(2)}) collective-permute-start(bf16[384,384]{1,0:T(8,128)(2,1)S(1)} %get-tuple-element.259), channel_id=1, source_target_pairs={{0,2},{1,3},{2,0},{3,1},{4,6},{5,7},{6,4},{7,5},{8,10},{9,11},{10,... | collective-permute-start | bytes 884744 | tf_op jit(solution)/shard_map/ppermute | solution.py:32
  192.6 11.9 %collective-permute-done.40.refs_1_ = bf16[384,384]{1,0:T(8,128)(2,1)S(1)} collective-permute-done((bf16[384,384]{1,0:T(8,128)(2,1)S(1)}, bf16[384,384]{1,0:T(8,128)(2,1)S(1)}, u32[]{:S(2)}, u32[]{:S(2)}) %collective-permute-start.40) | collective-permute-done | bytes 294944 | tf_op jit(solution)/shard_map/ppermute | solution.py:32
  207.7 3.1 %collective-permute-start.42 = (bf16[208,384]{1,0:T(8,128)(2,1)S(1)}, bf16[208,384]{1,0:T(8,128)(2,1)S(1)}, u32[]{:S(2)}, u32[]{:S(2)}) collective-permute-start(bf16[208,384]{1,0:T(8,128)(2,1)S(1)} %get-tuple-element.265), channel_id=1, source_target_pairs={{0,2},{1,3},{2,0},{3,1},{4,6},{5,7},{6,4},{7,5},{8,10},{9,11},{10,... | collective-permute-start | bytes 479240 | tf_op jit(solution)/shard_map/ppermute | solution.py:32
  212.3 4.5 %collective-permute-done.42.refs_1_ = bf16[208,384]{1,0:T(8,128)(2,1)S(1)} collective-permute-done((bf16[208,384]{1,0:T(8,128)(2,1)S(1)}, bf16[208,384]{1,0:T(8,128)(2,1)S(1)}, u32[]{:S(2)}, u32[]{:S(2)}) %collective-permute-start.42) | collective-permute-done | bytes 159776 | tf_op jit(solution)/shard_map/ppermute | solution.py:32
  216.8 6.7 %collective-permute-done.43.refs_2_ = bf16[208,384]{1,0:T(8,128)(2,1)S(1)} collective-permute-done((bf16[208,384]{1,0:T(8,128)(2,1)S(1)}, bf16[208,384]{1,0:T(8,128)(2,1)S(1)}, u32[]{:S(2)}, u32[]{:S(2)}) %collective-permute-start.43) | collective-permute-done | bytes 159776 | tf_op jit(solution)/shard_map/ppermute | solution.py:32
  231.1 3.2 %collective-permute-done.47 = bf16[208,384]{1,0:T(8,128)(2,1)S(1)} collective-permute-done((bf16[208,384]{1,0:T(8,128)(2,1)S(1)}, bf16[208,384]{1,0:T(8,128)(2,1)S(1)}, u32[]{:S(2)}, u32[]{:S(2)}) %collective-permute-start.47) | collective-permute-done | bytes 159776 | tf_op jit(solution)/shard_map/ppermute | solution.py:27
  (143 shorter events, 82.2 us)
Async XLA Ops:
  4.6 16.7 %collective-permute-start.1 = (bf16[264,384]{1,0:T(8,128)(2,1)S(1)}, bf16[264,384]{1,0:T(8,128)(2,1)S(1)}, u32[]{:S(2)}, u32[]{:S(2)}) collective-permute-start(bf16[264,384]{1,0:T(8,128)(2,1)S(1)} %maximum_maximum_fusion.refs_0_), channel_id=1, source_target_pairs={{0,2},{1,3},{2,0},{3,1},{4,6},{5,7},{6,4},{7,5},{8,10},{9,11},{10,... | collective-permute-start | bytes 608264 | tf_op jit(solution)/shard_map/ppermute | solution.py:32
  5.7 18.5 %collective-permute-start.2 = (bf16[264,384]{1,0:T(8,128)(2,1)S(1)}, bf16[264,384]{1,0:T(8,128)(2,1)S(1)}, u32[]{:S(2)}, u32[]{:S(2)}) collective-permute-start(bf16[264,384]{1,0:T(8,128)(2,1)S(1)} %maximum_maximum_fusion.refs_0_), channel_id=1, source_target_pairs={{0,3},{1,0},{2,1},{3,2},{4,7},{5,4},{6,5},{7,6},{8,11},{9,8},{10,9... | collective-permute-start | bytes 608264 | tf_op jit(solution)/shard_map/ppermute | solution.py:32
  24.8 14.5 %collective-permute-start.3 = (bf16[768,384]{1,0:T(8,128)(2,1)S(1)}, bf16[768,384]{1,0:T(8,128)(2,1)S(1)}, u32[]{:S(2)}, u32[]{:S(2)}) collective-permute-start(bf16[768,384]{1,0:T(8,128)(2,1)S(1)} %bitcast.42), channel_id=1, source_target_pairs={{0,8},{4,12},{8,0},{12,4},{16,24},{20,28},{24,16},{28,20},{1,9},{5... | collective-permute-start | bytes 1769480 | tf_op jit(solution)/shard_map/ppermute | solution.py:27
  26.0 14.1 %collective-permute-start.4 = (bf16[768,384]{1,0:T(8,128)(2,1)S(1)}, bf16[768,384]{1,0:T(8,128)(2,1)S(1)}, u32[]{:S(2)}, u32[]{:S(2)}) collective-permute-start(bf16[768,384]{1,0:T(8,128)(2,1)S(1)} %bitcast.43), channel_id=1, source_target_pairs={{0,16},{4,20},{8,24},{12,28},{16,0},{20,4},{24,8},{28,12},{1,17},{... | collective-permute-start | bytes 1769480 | tf_op jit(solution)/shard_map/ppermute | solution.py:27
  27.3 12.9 %collective-permute-start.5 = (bf16[384,384]{1,0:T(8,128)(2,1)S(1)}, bf16[384,384]{1,0:T(8,128)(2,1)S(1)}, u32[]{:S(2)}, u32[]{:S(2)}) collective-permute-start(bf16[384,384]{1,0:T(8,128)(2,1)S(1)} %pad_maximum_fusion.2), channel_id=1, source_target_pairs={{0,1},{1,2},{2,3},{3,0},{4,5},{5,6},{6,7},{7,4},{8,9},{9,10},{10,1... | collective-permute-start | bytes 884744 | tf_op jit(solution)/shard_map/ppermute | solution.py:32
  27.3 14.1 %collective-permute-start.6 = (bf16[384,384]{1,0:T(8,128)(2,1)S(1)}, bf16[384,384]{1,0:T(8,128)(2,1)S(1)}, u32[]{:S(2)}, u32[]{:S(2)}) collective-permute-start(bf16[384,384]{1,0:T(8,128)(2,1)S(1)} %pad_maximum_fusion.2), channel_id=1, source_target_pairs={{0,3},{1,0},{2,1},{3,2},{4,7},{5,4},{6,5},{7,6},{8,11},{9,8},{10,9... | collective-permute-start | bytes 884744 | tf_op jit(solution)/shard_map/ppermute | solution.py:32
  51.9 27.5 %collective-permute-start.14 = (bf16[1536,384]{1,0:T(8,128)(2,1)S(1)}, bf16[1536,384]{1,0:T(8,128)(2,1)S(1)}, u32[]{:S(2)}, u32[]{:S(2)}) collective-permute-start(bf16[1536,384]{1,0:T(8,128)(2,1)S(1)} %bitcast.32), channel_id=1, source_target_pairs={{0,8},{4,12},{8,0},{12,4},{16,24},{20,28},{24,16},{28,20},{1,9},{5... | collective-permute-start | bytes 3538952 | tf_op jit(solution)/shard_map/ppermute | solution.py:27
  53.2 27.3 %collective-permute-start.15 = (bf16[1536,384]{1,0:T(8,128)(2,1)S(1)}, bf16[1536,384]{1,0:T(8,128)(2,1)S(1)}, u32[]{:S(2)}, u32[]{:S(2)}) collective-permute-start(bf16[1536,384]{1,0:T(8,128)(2,1)S(1)} %bitcast.33), channel_id=1, source_target_pairs={{0,16},{4,20},{8,24},{12,28},{16,0},{20,4},{24,8},{28,12},{1,17},{... | collective-permute-start | bytes 3538952 | tf_op jit(solution)/shard_map/ppermute | solution.py:27
  60.9 13.6 %collective-permute-start.16 = (bf16[2,800,128]{2,1,0:T(8,128)(2,1)S(1)}, bf16[2,800,128]{2,1,0:T(8,128)(2,1)S(1)}, u32[]{:S(2)}, u32[]{:S(2)}) collective-permute-start(bf16[2,800,128]{2,1,0:T(8,128)(2,1)S(1)} %get-tuple-element.175), channel_id=1, source_target_pairs={{0,1},{1,2},{2,3},{4,5},{5,6},{6,7},{8,9},{9,10},{10,11},{12,13},{... | collective-permute-start | bytes 1228808 | tf_op jit(solution)/shard_map/ppermute | solution.py:38
  74.6 19.6 %collective-permute-start.17 = (bf16[2,800,128]{2,1,0:T(8,128)(2,1)S(1)}, bf16[2,800,128]{2,1,0:T(8,128)(2,1)S(1)}, u32[]{:S(2)}, u32[]{:S(2)}) collective-permute-start(bf16[2,800,128]{2,1,0:T(8,128)(2,1)S(1)} %add_convert_fusion.1), channel_id=1, source_target_pairs={{0,2},{1,3},{4,6},{5,7},{8,10},{9,11},{12,14},{13,15},{16,18},{17,... | collective-permute-start | bytes 1228808 | tf_op jit(solution)/shard_map/ppermute | solution.py:38
  77.3 22.7 %collective-permute-start.19 = (bf16[512,768]{1,0:T(8,128)(2,1)S(1)}, bf16[512,768]{1,0:T(8,128)(2,1)S(1)}, u32[]{:S(2)}, u32[]{:S(2)}) collective-permute-start(bf16[512,768]{1,0:T(8,128)(2,1)S(1)} %bitcast.35), channel_id=1, source_target_pairs={{0,4},{4,0},{8,12},{12,8},{16,20},{20,16},{24,28},{28,24},{1,5},{5... | collective-permute-start | bytes 2359304 | tf_op jit(solution)/shard_map/ppermute | solution.py:27
  80.5 19.3 %collective-permute-start.20 = (bf16[768,384]{1,0:T(8,128)(2,1)S(1)}, bf16[768,384]{1,0:T(8,128)(2,1)S(1)}, u32[]{:S(2)}, u32[]{:S(2)}) collective-permute-start(bf16[768,384]{1,0:T(8,128)(2,1)S(1)} %slice.51), channel_id=1, source_target_pairs={{0,16},{4,20},{8,24},{12,28},{16,0},{20,4},{24,8},{28,12},{1,17},{... | collective-permute-start | bytes 1769480 | tf_op jit(solution)/shard_map/ppermute | solution.py:27
  81.8 18.0 %collective-permute-start.21 = (bf16[768,384]{1,0:T(8,128)(2,1)S(1)}, bf16[768,384]{1,0:T(8,128)(2,1)S(1)}, u32[]{:S(2)}, u32[]{:S(2)}) collective-permute-start(bf16[768,384]{1,0:T(8,128)(2,1)S(1)} %slice.52), channel_id=1, source_target_pairs={{0,8},{4,12},{8,0},{12,4},{16,24},{20,28},{24,16},{28,20},{1,9},{5... | collective-permute-start | bytes 1769480 | tf_op jit(solution)/shard_map/ppermute | solution.py:27
  132.0 14.6 %collective-permute-start.27 = (bf16[768,384]{1,0:T(8,128)(2,1)S(1)}, bf16[768,384]{1,0:T(8,128)(2,1)S(1)}, u32[]{:S(2)}, u32[]{:S(2)}) collective-permute-start(bf16[768,384]{1,0:T(8,128)(2,1)S(1)} %get-tuple-element.206), channel_id=1, source_target_pairs={{0,16},{4,20},{8,24},{12,28},{16,0},{20,4},{24,8},{28,12},{1,17},{... | collective-permute-start | bytes 1769480 | tf_op jit(solution)/shard_map/ppermute | solution.py:27
  132.3 14.3 %collective-permute-start.28 = (bf16[768,384]{1,0:T(8,128)(2,1)S(1)}, bf16[768,384]{1,0:T(8,128)(2,1)S(1)}, u32[]{:S(2)}, u32[]{:S(2)}) collective-permute-start(bf16[768,384]{1,0:T(8,128)(2,1)S(1)} %get-tuple-element.207), channel_id=1, source_target_pairs={{0,8},{4,12},{8,0},{12,4},{16,24},{20,28},{24,16},{28,20},{1,9},{5... | collective-permute-start | bytes 1769480 | tf_op jit(solution)/shard_map/ppermute | solution.py:27
  135.8 21.2 %collective-permute-start.29 = (bf16[2,800,128]{2,1,0:T(8,128)(2,1)S(1)}, bf16[2,800,128]{2,1,0:T(8,128)(2,1)S(1)}, u32[]{:S(2)}, u32[]{:S(2)}) collective-permute-start(bf16[2,800,128]{2,1,0:T(8,128)(2,1)S(1)} %add_convert_fusion), channel_id=1, source_target_pairs={{2,0},{3,1},{6,4},{7,5},{10,8},{11,9},{14,12},{15,13},{18,16},{19,... | collective-permute-start | bytes 1228808 | tf_op jit(solution)/shard_map/ppermute | solution.py:38
  147.0 26.1 %collective-permute-start.32 = (bf16[1536,384]{1,0:T(8,128)(2,1)S(1)}, bf16[1536,384]{1,0:T(8,128)(2,1)S(1)}, u32[]{:S(2)}, u32[]{:S(2)}) collective-permute-start(bf16[1536,384]{1,0:T(8,128)(2,1)S(1)} %get-tuple-element.235), channel_id=1, source_target_pairs={{0,8},{4,12},{8,0},{12,4},{16,24},{20,28},{24,16},{28,20},{1,9},{5... | collective-permute-start | bytes 3538952 | tf_op jit(solution)/shard_map/ppermute | solution.py:27
  147.8 25.7 %collective-permute-start.33 = (bf16[1536,384]{1,0:T(8,128)(2,1)S(1)}, bf16[1536,384]{1,0:T(8,128)(2,1)S(1)}, u32[]{:S(2)}, u32[]{:S(2)}) collective-permute-start(bf16[1536,384]{1,0:T(8,128)(2,1)S(1)} %get-tuple-element.236), channel_id=1, source_target_pairs={{0,16},{4,20},{8,24},{12,28},{16,0},{20,4},{24,8},{28,12},{1,17},{... | collective-permute-start | bytes 3538952 | tf_op jit(solution)/shard_map/ppermute | solution.py:27
  188.3 16.2 %collective-permute-start.38 = (bf16[832,384]{1,0:T(8,128)(2,1)S(1)}, bf16[832,384]{1,0:T(8,128)(2,1)S(1)}, u32[]{:S(2)}, u32[]{:S(2)}) collective-permute-start(bf16[832,384]{1,0:T(8,128)(2,1)S(1)} %get-tuple-element.256), channel_id=1, source_target_pairs={{0,8},{4,12},{8,0},{12,4},{16,24},{20,28},{24,16},{28,20},{1,9},{5... | collective-permute-start | bytes 1916936 | tf_op jit(solution)/shard_map/ppermute | solution.py:27
  188.7 15.8 %collective-permute-start.39 = (bf16[832,384]{1,0:T(8,128)(2,1)S(1)}, bf16[832,384]{1,0:T(8,128)(2,1)S(1)}, u32[]{:S(2)}, u32[]{:S(2)}) collective-permute-start(bf16[832,384]{1,0:T(8,128)(2,1)S(1)} %get-tuple-element.257), channel_id=1, source_target_pairs={{0,16},{4,20},{8,24},{12,28},{16,0},{20,4},{24,8},{28,12},{1,17},{... | collective-permute-start | bytes 1916936 | tf_op jit(solution)/shard_map/ppermute | solution.py:27
  189.5 15.0 %collective-permute-start.40 = (bf16[384,384]{1,0:T(8,128)(2,1)S(1)}, bf16[384,384]{1,0:T(8,128)(2,1)S(1)}, u32[]{:S(2)}, u32[]{:S(2)}) collective-permute-start(bf16[384,384]{1,0:T(8,128)(2,1)S(1)} %get-tuple-element.259), channel_id=1, source_target_pairs={{0,2},{1,3},{2,0},{3,1},{4,6},{5,7},{6,4},{7,5},{8,10},{9,11},{10,... | collective-permute-start | bytes 884744 | tf_op jit(solution)/shard_map/ppermute | solution.py:32
  205.0 18.5 %collective-permute-start.44 = (bf16[384,384]{1,0:T(8,128)(2,1)S(1)}, bf16[384,384]{1,0:T(8,128)(2,1)S(1)}, u32[]{:S(2)}, u32[]{:S(2)}) collective-permute-start(bf16[384,384]{1,0:T(8,128)(2,1)S(1)} %shard_map.213), channel_id=1, source_target_pairs={{0,8},{4,12},{8,0},{12,4},{16,24},{20,28},{24,16},{28,20},{1,9},{5... | collective-permute-start | bytes 884744 | tf_op jit(solution)/shard_map/ppermute | solution.py:27
  205.1 18.4 %collective-permute-start.48 = (bf16[384,384]{1,0:T(8,128)(2,1)S(1)}, bf16[384,384]{1,0:T(8,128)(2,1)S(1)}, u32[]{:S(2)}, u32[]{:S(2)}) collective-permute-start(bf16[384,384]{1,0:T(8,128)(2,1)S(1)} %shard_map.213), channel_id=1, source_target_pairs={{0,16},{4,20},{8,24},{12,28},{16,0},{20,4},{24,8},{28,12},{1,17},{... | collective-permute-start | bytes 884744 | tf_op jit(solution)/shard_map/ppermute | solution.py:27
  205.4 18.1 %collective-permute-start.49 = (bf16[384,384]{1,0:T(8,128)(2,1)S(1)}, bf16[384,384]{1,0:T(8,128)(2,1)S(1)}, u32[]{:S(2)}, u32[]{:S(2)}) collective-permute-start(bf16[384,384]{1,0:T(8,128)(2,1)S(1)} %shard_map.213), channel_id=1, source_target_pairs={{0,24},{4,28},{8,16},{12,20},{16,8},{20,12},{24,0},{28,4},{1,25},{... | collective-permute-start | bytes 884744 | tf_op jit(solution)/shard_map/ppermute | solution.py:27
  (36 other events, 276.6 us)
